TPU v7x, 32 devices: a whole 2x2x4 slice. The times are simulated.
32 devices in a mesh: dp: 4 (over z), seq: 8 (over y, x, core).
Axes of the slice: x: 2, y: 2, z: 4, core: 2. Of those that a mesh axis runs over, the one named last changes fastest.
Arguments:
- hidden: bfloat16 [4096, 2048], P(('dp', 'seq')), may hold values from -6 to 6
- cotangent: bfloat16 [4096, 2048], P(('dp', 'seq')), may hold values from -6 to 6
- attn_gain: bfloat16 [2048], P(('dp', 'seq')), may hold values from 0.25 to 1.75
- q_weight: bfloat16 [2048, 3072], P(('dp', 'seq')), may hold values from -0.125 to 0.125
- kv_down: bfloat16 [2048, 576], P(('dp', 'seq')), may hold values from -0.125 to 0.125
- kv_gain: bfloat16 [512], P(('dp', 'seq')), may hold values from 0.25 to 1.75
- kv_up: bfloat16 [512, 4096], P(('dp', 'seq')), may hold values from -0.25 to 0.25
- out_weight: bfloat16 [2048, 2048], P(('dp', 'seq')), may hold values from -2 to 2
- ffn_gain: bfloat16 [2048], P(('dp', 'seq')), may hold values from 0.25 to 1.75
- shared_gate_up: bfloat16 [2048, 5632], P(('dp', 'seq')), may hold values from -0.125 to 0.125
- shared_down: bfloat16 [2816, 2048], P(('dp', 'seq')), may hold values from -0.109375 to 0.109375
- expert_gate_up: bfloat16 [2048, 16, 2816], P('dp', 'seq'), may hold values from -0.125 to 0.125
- expert_down: bfloat16 [1408, 16, 2048], P('dp', 'seq'), may hold values from -0.15625 to 0.15625
- expert_ids: int32 [4096, 6], P('dp'), may hold values from 0 to 15, all different within a row; in each aligned block of 128 rows (0 to 127, 128 to 255, ...) at most 96 rows name the same one
- gate_fix: int32 [4096, 6], P(('dp', 'seq')), may hold values from 1024 to 8191
- block_ids: int32 [4, 1024], P('dp'), may hold values from 0 to 7, never falling along the last dimension, each value on 1 to 256 neighbouring positions
Outputs:
- output: bfloat16 [4096, 2048], P(('dp', 'seq'))
- d_hidden: float32 [4096, 2048], P(('dp', 'seq'))
- d_attn_gain: float32 [2048], P(('dp', 'seq'))
- d_q_weight: float32 [2048, 3072], P(('dp', 'seq'))
- d_kv_down: float32 [2048, 576], P(('dp', 'seq'))
- d_kv_gain: float32 [512], P(('dp', 'seq'))
- d_kv_up: float32 [512, 4096], P(('dp', 'seq'))
- d_out_weight: float32 [2048, 2048], P(('dp', 'seq'))
- d_ffn_gain: float32 [2048], P(('dp', 'seq'))
- d_shared_gate_up: float32 [2048, 5632], P(('dp', 'seq'))
- d_shared_down: float32 [2816, 2048], P(('dp', 'seq'))
- d_expert_gate_up: float32 [2048, 16, 2816], P('dp', 'seq')
- d_expert_down: float32 [1408, 16, 2048], P('dp', 'seq')
Inputs may be any that keep to these rules, and one draw needn't show every extreme that they name: `expert_ids`: each row names 6 different experts; within each aligned block of 128 rows (the rows of one device) no expert is named by more than 96 rows. `block_ids`: along each sequence the block number never falls, and each block spans 1 to 256 positions.
All inputs are finite; a program needn't handle non-finite values.
Results may differ from a plain program's by a relative error of at most 0.018.
Values may be sent and summed in bfloat16 or wider, within the bound.
No kernel may reach another device: no remote copies, remote signals or barrier semaphores. Data moves between devices by JAX's collectives and lax.ppermute only.
A program may use at most 448 MiB of HBM per device.

v0:
```python
import jax
import jax.numpy as jnp
from jax import lax
from jax.sharding import PartitionSpec as P

H = 16
NOPE = 128
ROPE = 64
VD = 128
KV_RANK = 512
TOP = 6


EPS = 1e-06
THETA = 10000.0
GATE_UNIT = 16384.0


def matmul(left_side, right_side):
    return jnp.dot(left_side, right_side, preferred_element_type=jnp.float32)


def lead_dot(left_side, right_side):
    return lax.dot_general(
        left_side, right_side, (((0,), (0,)), ((), ())), preferred_element_type=jnp.float32
    )


def tail_dot(left_side, right_side):
    return lax.dot_general(
        left_side, right_side, (((1,), (1,)), ((), ())), preferred_element_type=jnp.float32
    )


def rms_norm(values, scale_vec):
    return values * lax.rsqrt(jnp.mean(values * values, axis=-1, keepdims=True) + EPS) * scale_vec


def swiglu(joined):
    half_width = joined.shape[-1] // 2
    return jax.nn.silu(joined[..., :half_width]) * joined[..., half_width:]


def rotary_tables(positions):
    half_width = ROPE // 2
    frequency = THETA ** (-jnp.arange(half_width, dtype=jnp.float32) * 2.0 / ROPE)
    angles = positions.astype(jnp.float32)[:, None] * frequency[None, :]
    return (jnp.cos(angles), jnp.sin(angles))


def rotate(values, cosine, sine_table):
    half_width = values.shape[-1] // 2
    leading = values[..., :half_width]
    trailing = values[..., half_width:]
    return jnp.concatenate(
        [leading * cosine - trailing * sine_table, trailing * cosine + leading * sine_table],
        axis=-1,
    )


def assemble(query_in, rope_in, expand_in, cosine, sine_table):
    tokens = query_in.shape[0]
    query_heads = query_in.reshape(tokens, H, NOPE + ROPE)
    expand_heads = expand_in.reshape(tokens, H, NOPE + VD)
    query_rot = rotate(query_heads[..., NOPE:], cosine[:, None, :], sine_table[:, None, :])
    key_rot = jnp.broadcast_to(rotate(rope_in, cosine, sine_table)[:, None, :], (tokens, H, ROPE))
    return jnp.concatenate(
        [
            query_heads[..., :NOPE],
            query_rot,
            expand_heads[..., :NOPE],
            key_rot,
            expand_heads[..., NOPE:],
        ],
        axis=-1,
    )


def split_packed(packed):
    head_width = NOPE + ROPE
    return (
        packed[..., :head_width],
        packed[..., head_width : 2 * head_width],
        packed[..., 2 * head_width :],
    )


def block_rows():
    return 512


def scores_for(query_part, key_rows, block_part, blocks):
    head_width = query_part.shape[-1]
    scores = jnp.einsum(
        "sqhd,skhd->shqk", query_part, key_rows, preferred_element_type=jnp.float32
    ) * head_width ** (-0.5)
    allowed = blocks[:, None, None, :] <= block_part[:, None, :, None]
    return jnp.where(allowed, scores, -1e30)


def attend_forward(packed, blocks):
    queries, key_rows, values = split_packed(packed)
    sequences, length, head_count = (packed.shape[0], packed.shape[1], packed.shape[2])
    rows_per = block_rows()

    def one_block(number):
        offset = number * rows_per
        query_part = lax.dynamic_slice_in_dim(queries, offset, rows_per, 1)
        block_part = lax.dynamic_slice_in_dim(blocks, offset, rows_per, 1)
        scores = scores_for(query_part, key_rows, block_part, blocks)
        row_max = jnp.max(scores, axis=-1, keepdims=True)
        weights = jnp.exp(scores - row_max)
        row_total = jnp.sum(weights, axis=-1, keepdims=True)
        shares = (weights / row_total).astype(jnp.bfloat16)
        attended = jnp.einsum("shqk,skhd->sqhd", shares, values, preferred_element_type=jnp.float32)
        return (attended.astype(jnp.bfloat16), (row_max + jnp.log(row_total))[..., 0])

    outputs, log_sums = lax.map(one_block, jnp.arange(length // rows_per))
    outputs = jnp.moveaxis(outputs, 0, 1).reshape(sequences, length, head_count, -1)
    log_sums = jnp.transpose(log_sums, (1, 2, 0, 3)).reshape(sequences, head_count, length)
    return (outputs, log_sums)


def attend_backward(packed, blocks, log_sums, grad_out):
    queries, key_rows, values = split_packed(packed)
    sequences, length, head_count = (packed.shape[0], packed.shape[1], packed.shape[2])
    rows_per = block_rows()
    score_scale = queries.shape[-1] ** (-0.5)

    def one_block(carried, number):
        key_grad, value_grad = carried
        offset = number * rows_per
        query_part = lax.dynamic_slice_in_dim(queries, offset, rows_per, 1)
        block_part = lax.dynamic_slice_in_dim(blocks, offset, rows_per, 1)
        sums_part = lax.dynamic_slice_in_dim(log_sums, offset, rows_per, 2)
        grad_part = lax.dynamic_slice_in_dim(grad_out, offset, rows_per, 1)
        scores = scores_for(query_part, key_rows, block_part, blocks)
        probs_full = jnp.exp(scores - sums_part[..., None])
        shares = probs_full.astype(jnp.bfloat16)
        prob_grad = jnp.einsum(
            "sqhd,skhd->shqk", grad_part, values, preferred_element_type=jnp.float32
        )
        centre = jnp.sum(probs_full * prob_grad, axis=-1, keepdims=True)
        score_grad = (probs_full * (prob_grad - centre)).astype(jnp.bfloat16)
        query_grad = (
            jnp.einsum("shqk,skhd->sqhd", score_grad, key_rows, preferred_element_type=jnp.float32)
            * score_scale
        )
        key_grad = (
            key_grad
            + jnp.einsum(
                "shqk,sqhd->skhd", score_grad, query_part, preferred_element_type=jnp.float32
            )
            * score_scale
        )
        value_grad = value_grad + jnp.einsum(
            "shqk,sqhd->skhd", shares, grad_part, preferred_element_type=jnp.float32
        )
        return ((key_grad, value_grad), query_grad)

    start_carry = (jnp.zeros(key_rows.shape, jnp.float32), jnp.zeros(values.shape, jnp.float32))
    (key_grad, value_grad), query_grads = lax.scan(
        one_block, start_carry, jnp.arange(length // rows_per)
    )
    query_grads = jnp.moveaxis(query_grads, 0, 1).reshape(sequences, length, head_count, -1)
    return jnp.concatenate([query_grads, key_grad, value_grad], axis=-1)


def pick_rows(source_rows, row_index, row_live):
    flat = source_rows.reshape(-1, source_rows.shape[-1])
    chosen = jnp.take(flat, row_index.reshape(-1), axis=0).reshape(
        row_index.shape + (source_rows.shape[-1],)
    )
    return jnp.where(row_live[..., None], chosen, jnp.zeros((), source_rows.dtype))


def body(
    hidden,
    cotangent,
    attn_gain,
    q_weight,
    kv_down,
    kv_gain,
    kv_up,
    out_weight,
    ffn_gain,
    shared_gate_up,
    shared_down,
    expert_gate_up,
    expert_down,
    expert_ids,
    gate_fix,
    block_ids,
):
    seq_count = lax.axis_size("seq")
    seq_index = lax.axis_index("seq")
    tokens = hidden.shape[0]
    sequences, length = block_ids.shape
    part_length = length // seq_count
    gathered = (
        lax.all_gather(attn_gain, ("dp", "seq"), axis=0, tiled=True),
        lax.all_gather(q_weight, ("dp", "seq"), axis=0, tiled=True),
        lax.all_gather(kv_down, ("dp", "seq"), axis=0, tiled=True),
        lax.all_gather(kv_gain, ("dp", "seq"), axis=0, tiled=True),
        lax.all_gather(kv_up, ("dp", "seq"), axis=0, tiled=True),
        lax.all_gather(out_weight, ("dp", "seq"), axis=0, tiled=True),
        lax.all_gather(ffn_gain, ("dp", "seq"), axis=0, tiled=True),
        lax.all_gather(shared_gate_up, ("dp", "seq"), axis=0, tiled=True),
        lax.all_gather(shared_down, ("dp", "seq"), axis=0, tiled=True),
    )
    (
        gain_attn,
        weight_q,
        weight_down,
        gain_kv,
        weight_up,
        weight_out,
        gain_ffn,
        weight_gate_up,
        weight_shared,
    ) = gathered
    row_values = hidden.astype(jnp.float32)
    positions = seq_index * part_length + jnp.arange(tokens, dtype=jnp.int32) % part_length
    cosine, sine_table = rotary_tables(positions)
    normed, norm_pull = jax.vjp(rms_norm, row_values, gain_attn.astype(jnp.float32))
    normed_low = normed.astype(jnp.bfloat16)
    query_raw = matmul(normed_low, weight_q)
    latent_in = matmul(normed_low, weight_down)
    latent, latent_pull = jax.vjp(rms_norm, latent_in[:, :KV_RANK], gain_kv.astype(jnp.float32))
    latent_low = latent.astype(jnp.bfloat16)
    expanded = matmul(latent_low, weight_up)

    def pack_local(query_in, rope_in, expand_in):
        return assemble(query_in, rope_in, expand_in, cosine, sine_table)

    packed, pack_pull = jax.vjp(pack_local, query_raw, latent_in[:, KV_RANK:], expanded)
    packed_low = packed.astype(jnp.bfloat16).reshape(sequences, part_length, H, -1)
    by_head = lax.all_to_all(packed_low, "seq", split_axis=2, concat_axis=1, tiled=True)
    attended, log_sums = attend_forward(by_head, block_ids)
    by_token = lax.all_to_all(attended, "seq", split_axis=1, concat_axis=2, tiled=True)
    heads_out = by_token.reshape(tokens, -1)
    residual = row_values + matmul(heads_out, weight_out)
    normed_ffn, ffn_pull = jax.vjp(rms_norm, residual, gain_ffn.astype(jnp.float32))
    ffn_low = normed_ffn.astype(jnp.bfloat16)
    shared_in = matmul(ffn_low, weight_gate_up)
    shared_act, shared_pull = jax.vjp(swiglu, shared_in)
    shared_low = shared_act.astype(jnp.bfloat16)
    shared_out = matmul(shared_low, weight_shared)
    per_device = expert_gate_up.shape[1]
    experts = per_device * seq_count
    capacity = TOP * tokens // per_device
    slot_bound = 2 * TOP * tokens // experts
    labels = jnp.arange(experts, dtype=jnp.int32)
    group_hits = jnp.sum((expert_ids[:, :, None] == labels).astype(jnp.int32), axis=1)
    source_counts = jnp.sum(group_hits.reshape(seq_count, tokens, experts), axis=1)
    own_picks = lax.dynamic_slice_in_dim(expert_ids, seq_index * tokens, tokens, 0)
    own_hits = lax.dynamic_slice_in_dim(group_hits, seq_index * tokens, tokens, 0)
    own_before = jnp.cumsum(own_hits, axis=0) - own_hits
    pair_rank = jnp.take_along_axis(own_before, own_picks, axis=1)
    rank_index = jnp.arange(slot_bound, dtype=jnp.int32)
    placed = own_hits[:, :, None] * (own_before[:, :, None] == rank_index).astype(jnp.int32)
    token_number = jnp.arange(tokens, dtype=jnp.int32)
    sender_row = jnp.sum(placed * token_number[:, None, None], axis=0)
    sender_live = jnp.sum(placed, axis=0) > 0
    gate_values = gate_fix.astype(jnp.float32) / GATE_UNIT
    gate_by_expert = jnp.sum(
        gate_values[:, :, None] * (own_picks[:, :, None] == labels).astype(jnp.float32), axis=1
    )
    gate_slots = jnp.sum(placed.astype(jnp.float32) * gate_by_expert[:, :, None], axis=0)
    own_counts = lax.dynamic_slice_in_dim(source_counts, seq_index * per_device, per_device, 1)
    source_ends = jnp.cumsum(own_counts, axis=0)
    starts = source_ends - own_counts
    slot_index = jnp.arange(capacity, dtype=jnp.int32)
    source_of = jnp.sum(
        (source_ends.T[:, :, None] <= slot_index[None, None, :]).astype(jnp.int32), axis=1
    )
    slot_live = slot_index[None, :] < source_ends[-1][:, None]
    source_safe = jnp.minimum(source_of, seq_count - 1)
    offset_in = slot_index[None, :] - jnp.take_along_axis(starts.T, source_safe, axis=1)
    local_expert = jnp.arange(per_device, dtype=jnp.int32)[:, None]
    gather_index = jnp.where(
        slot_live, (source_safe * per_device + local_expert) * slot_bound + offset_in, 0
    )
    back_slot = starts[:, :, None] + rank_index[None, None, :]
    back_live = (rank_index[None, None, :] < own_counts[:, :, None]) & (back_slot < capacity)
    back_index = jnp.where(back_live, local_expert[None, :, :] * capacity + back_slot, 0)
    pair_index = own_picks * slot_bound + pair_rank
    send_rows = pick_rows(ffn_low, sender_row, sender_live).reshape(
        seq_count, per_device, slot_bound, -1
    )
    arrived = lax.all_to_all(send_rows, "seq", split_axis=0, concat_axis=0, tiled=True)
    slot_rows = pick_rows(arrived, gather_index, slot_live)
    expert_pair = (
        lax.all_gather(expert_gate_up, "dp", axis=0, tiled=True),
        lax.all_gather(expert_down, "dp", axis=0, tiled=True),
    )
    weight_experts_in, weight_experts_out = expert_pair
    expert_in = jnp.einsum(
        "ecd,def->ecf", slot_rows, weight_experts_in, preferred_element_type=jnp.float32
    )
    expert_act, expert_pull = jax.vjp(swiglu, expert_in)
    expert_low = expert_act.astype(jnp.bfloat16)
    expert_out = jnp.einsum(
        "ecf,fed->ecd", expert_low, weight_experts_out, preferred_element_type=jnp.float32
    ).astype(jnp.bfloat16)
    returned = lax.all_to_all(
        pick_rows(expert_out, back_index, back_live), "seq", split_axis=0, concat_axis=0, tiled=True
    )
    pair_rows = jnp.take(
        returned.reshape(-1, returned.shape[-1]), pair_index.reshape(-1), axis=0
    ).reshape(tokens, TOP, -1)
    routed = jnp.sum(gate_values[:, :, None] * pair_rows.astype(jnp.float32), axis=1)
    output = (residual + shared_out + routed).astype(jnp.bfloat16)
    regathered = (weight_q, weight_down, weight_up, weight_out, weight_gate_up, weight_shared)
    weight_q, weight_down, weight_up, weight_out, weight_gate_up, weight_shared = regathered
    grad_rows = cotangent.astype(jnp.float32)
    grad_pairs = (pick_rows(grad_rows, sender_row, sender_live) * gate_slots[..., None]).astype(
        jnp.bfloat16
    )
    grad_arrived = lax.all_to_all(
        grad_pairs.reshape(seq_count, per_device, slot_bound, -1),
        "seq",
        split_axis=0,
        concat_axis=0,
        tiled=True,
    )
    grad_slots = pick_rows(grad_arrived, gather_index, slot_live)
    hidden_grad = jnp.einsum(
        "ecd,fed->ecf", grad_slots, weight_experts_out, preferred_element_type=jnp.float32
    )
    (expert_in_grad,) = expert_pull(hidden_grad)
    expert_in_low = expert_in_grad.astype(jnp.bfloat16)
    grad_expert_out = jnp.einsum(
        "ecf,ecd->fed", expert_low, grad_slots, preferred_element_type=jnp.float32
    )
    grad_expert_in = jnp.einsum(
        "ecd,ecf->def", slot_rows, expert_in_low, preferred_element_type=jnp.float32
    )
    slot_grad = jnp.einsum(
        "ecf,def->ecd", expert_in_low, weight_experts_in, preferred_element_type=jnp.float32
    ).astype(jnp.bfloat16)
    expert_grads = (
        lax.psum_scatter(
            grad_expert_in.astype(jnp.bfloat16), "dp", scatter_dimension=0, tiled=True
        ).astype(jnp.float32),
        lax.psum_scatter(
            grad_expert_out.astype(jnp.bfloat16), "dp", scatter_dimension=0, tiled=True
        ).astype(jnp.float32),
    )
    grad_returned = lax.all_to_all(
        pick_rows(slot_grad, back_index, back_live), "seq", split_axis=0, concat_axis=0, tiled=True
    )
    routed_rows = jnp.take(
        grad_returned.reshape(-1, grad_returned.shape[-1]), pair_index.reshape(-1), axis=0
    )
    routed_grad = jnp.sum(routed_rows.reshape(tokens, TOP, -1).astype(jnp.float32), axis=1)
    grad_shared = lead_dot(shared_low, cotangent)
    shared_grad_act = tail_dot(cotangent, weight_shared)
    (shared_in_grad,) = shared_pull(shared_grad_act)
    shared_in_low = shared_in_grad.astype(jnp.bfloat16)
    grad_gate_up = lead_dot(ffn_low, shared_in_low)
    ffn_grad = tail_dot(shared_in_low, weight_gate_up) + routed_grad
    residual_from_norm, gain_ffn_grad = ffn_pull(ffn_grad)
    ffn_grads = (
        lax.psum_scatter(gain_ffn_grad, ("dp", "seq"), scatter_dimension=0, tiled=True),
        lax.psum_scatter(grad_gate_up, ("dp", "seq"), scatter_dimension=0, tiled=True),
        lax.psum_scatter(grad_shared, ("dp", "seq"), scatter_dimension=0, tiled=True),
    )
    residual_grad = grad_rows + residual_from_norm
    residual_low = residual_grad.astype(jnp.bfloat16)
    grad_out_weight = lead_dot(heads_out, residual_low)
    heads_grad = (
        tail_dot(residual_low, weight_out)
        .astype(jnp.bfloat16)
        .reshape(sequences, part_length, H, -1)
    )
    heads_grad_by_head = lax.all_to_all(heads_grad, "seq", split_axis=2, concat_axis=1, tiled=True)
    packed_grad = attend_backward(by_head, block_ids, log_sums, heads_grad_by_head).astype(
        jnp.bfloat16
    )
    packed_back = (
        lax.all_to_all(packed_grad, "seq", split_axis=1, concat_axis=2, tiled=True)
        .reshape(tokens, H, -1)
        .astype(jnp.float32)
    )
    query_grad, rope_grad, expand_grad = pack_pull(packed_back)
    expand_low = expand_grad.astype(jnp.bfloat16)
    grad_kv_up = lead_dot(latent_low, expand_low)
    latent_grad, gain_kv_grad = latent_pull(tail_dot(expand_low, weight_up))
    down_low = jnp.concatenate([latent_grad, rope_grad], axis=1).astype(jnp.bfloat16)
    query_low = query_grad.astype(jnp.bfloat16)
    grad_q = lead_dot(normed_low, query_low)
    grad_down = lead_dot(normed_low, down_low)
    normed_grad = tail_dot(query_low, weight_q) + tail_dot(down_low, weight_down)
    rows_from_norm, gain_attn_grad = norm_pull(normed_grad)
    input_grad = residual_grad + rows_from_norm
    attention_grads = (
        lax.psum_scatter(gain_attn_grad, ("dp", "seq"), scatter_dimension=0, tiled=True),
        lax.psum_scatter(grad_q, ("dp", "seq"), scatter_dimension=0, tiled=True),
        lax.psum_scatter(grad_down, ("dp", "seq"), scatter_dimension=0, tiled=True),
        lax.psum_scatter(gain_kv_grad, ("dp", "seq"), scatter_dimension=0, tiled=True),
        lax.psum_scatter(grad_kv_up, ("dp", "seq"), scatter_dimension=0, tiled=True),
        lax.psum_scatter(grad_out_weight, ("dp", "seq"), scatter_dimension=0, tiled=True),
    )
    return (
        output,
        input_grad,
        attention_grads[0],
        attention_grads[1],
        attention_grads[2],
        attention_grads[3],
        attention_grads[4],
        attention_grads[5],
        ffn_grads[0],
        ffn_grads[1],
        ffn_grads[2],
        expert_grads[0],
        expert_grads[1],
    )


def solution(mesh):
    return jax.shard_map(
        body,
        mesh=mesh,
        in_specs=(
            P(("dp", "seq"), None),
            P(("dp", "seq"), None),
            P(("dp", "seq")),
            P(("dp", "seq"), None),
            P(("dp", "seq"), None),
            P(("dp", "seq")),
            P(("dp", "seq"), None),
            P(("dp", "seq"), None),
            P(("dp", "seq")),
            P(("dp", "seq"), None),
            P(("dp", "seq"), None),
            P("dp", "seq", None),
            P("dp", "seq", None),
            P("dp", None),
            P(("dp", "seq"), None),
            P("dp", None),
        ),
        out_specs=(
            P(("dp", "seq"), None),
            P(("dp", "seq"), None),
            P(("dp", "seq")),
            P(("dp", "seq"), None),
            P(("dp", "seq"), None),
            P(("dp", "seq")),
            P(("dp", "seq"), None),
            P(("dp", "seq"), None),
            P(("dp", "seq")),
            P(("dp", "seq"), None),
            P(("dp", "seq"), None),
            P("dp", "seq", None),
            P("dp", "seq", None),
        ),
        check_vma=False,
    )
```

profile of v0, /device:TPU:25, one launch (start us, length us, event | category | flops | bytes accessed | tf_op | source)
XLA Modules:
  0.0 3456.2 jit_solution(7299172222709190716)
XLA Ops:
  22.2 39.6 %all-reduce.19 = (bf16[2048]{0:T(1024)(128)(2,1)S(1)}, bf16[512]{0:T(512)(128)(2,1)S(1)}, bf16[2048]{0:T(1024)(128)(2,1)S(1)}) all-reduce(bf16[2048]{0:T(1024)(128)(2,1)S(1)} %dynamic-update-slice, bf16[512]{0:T(512)(128)(2,1)S(1)} %dynamic-update-slice.1, ...), channel_id=1, replica_groups=mesh['dp'=4,'seq'=8] {'dp','seq'}, use_global_device_ids=true, to_apply=%add.11 | all-reduce | flops 4608 | bytes 18432
  72.5 60.3 %all-gather.13.cloned.1.call-done = bf16[512,4096]{1,0:T(8,128)(2,1)} async-done(((bf16[16,4096]{1,0:T(8,128)(2,1)}), bf16[512,4096]{1,0:T(8,128)(2,1)}) %all-gather.13.cloned.1.call-update) | async-done | bytes 4194320 | tf_op jit(solution)/shard_map/all_gather | solution.py:205
  138.4 91.5 %all-gather.9.cloned.1.call-done = bf16[2048,3072]{1,0:T(8,128)(2,1)} async-done(((bf16[64,3072]{1,0:T(8,128)(2,1)}), bf16[2048,3072]{1,0:T(8,128)(2,1)}) %all-gather.9.cloned.1.call-update) | async-done | bytes 12582928 | tf_op jit(solution)/shard_map/all_gather | solution.py:202
  255.4 19.5 all-to-all-done
  285.4 16.3 while.27
  347.3 45.3 %all-to-all-done.4 = bf16[8,2,96,2048]{3,2,1,0:T(8,128)(2,1)} async-done(((bf16[8,2,96,2048]{3,2,1,0:T(8,128)(2,1)}), bf16[8,2,96,2048]{3,2,1,0:T(8,128)(2,1)}, u32[]{:S(2)}, u32[]{:S(2)}) %all-to-all-start.4) | async-done | bytes 6291488 | tf_op jit(solution)/shard_map/all_to_all | solution.py:320
  416.4 52.5 %all-to-all-done.2 = bf16[8,2,96,2048]{3,2,1,0:T(8,128)(2,1)} async-done(((bf16[8,2,96,2048]{3,2,1,0:T(8,128)(2,1)}), bf16[8,2,96,2048]{3,2,1,0:T(8,128)(2,1)}, u32[]{:S(2)}, u32[]{:S(2)}) %all-to-all-start.2) | async-done | bytes 6291488 | tf_op jit(solution)/shard_map/all_to_all | solution.py:291
  491.6 213.3 %all-gather.21.cloned.1.call-done = bf16[2048,2,2816]{2,0,1:T(8,128)(2,1)} async-done(((bf16[512,2,2816]{2,0,1:T(8,128)(2,1)}), bf16[2048,2,2816]{2,0,1:T(8,128)(2,1)}) %all-gather.21.cloned.1.call-update) | async-done | bytes 23068688 | tf_op jit(solution)/shard_map/all_gather | solution.py:294
  704.9 17.5 fusion.51
  722.4 183.2 %all-gather.23.cloned.1.call-done = bf16[1408,2,2048]{2,0,1:T(8,128)(2,1)} async-done(((bf16[352,2,2048]{2,0,1:T(8,128)(2,1)}), bf16[1408,2,2048]{2,0,1:T(8,128)(2,1)}) %all-gather.23.cloned.1.call-update) | async-done | bytes 11534352 | tf_op jit(solution)/shard_map/all_gather | solution.py:295
  905.6 19.4 fusion.80
  935.7 29.1 copy.233
  966.7 22.2 convert_bitcast_fusion
  989.3 15.3 convolution_convert_fusion.2
  1037.0 86.9 %all_to_all.80 = bf16[8,2,96,2048]{3,2,1,0:T(8,128)(2,1)} all-to-all(bf16[8,2,96,2048]{3,2,1,0:T(8,128)(2,1)S(1)} %get-tuple-element.424), channel_id=1, replica_groups=mesh['dp'=4,'seq'=8] {'seq'}, dimensions={0} | all-to-all | bytes 12582912 | tf_op jit(solution)/shard_map/all_to_all | solution.py:350
  1146.0 65.7 %all-to-all-done.3 = bf16[8,2,96,2048]{3,2,1,0:T(8,128)(2,1)} async-done(((bf16[8,2,96,2048]{3,2,1,0:T(8,128)(2,1)}), bf16[8,2,96,2048]{3,2,1,0:T(8,128)(2,1)}, u32[]{:S(2)}, u32[]{:S(2)}) %all-to-all-start.3) | async-done | bytes 6291488 | tf_op jit(solution)/shard_map/all_to_all | solution.py:306
  1245.0 12.5 fusion.133
  1257.5 10.8 fusion.86
  1268.4 15.0 multiply_reduce_fusion.2
  1307.9 34.9 %while.28 = (s32[]{:T(128)}, f32[1,1024,2,192]{1,3,2,0:T(8,128)}, f32[1,1024,2,128]{1,3,2,0:T(8,128)}, bf16[2,1,512,2,192]{2,4,3,1,0:T(8,128)(2,1)}, s32[2]{0:T(...) while((s32[]{:T(128)}, f32[1,1024,2,192]{1,3,2,0:T(8,128)}, ...), condition=%wide.region_21.24_spmd.clone, body=%wide.region_19.23_spmd.clone.sunk | while | flops 1762982912 | bytes 91265448 | solution.py:162
  1350.0 31.8 all_to_all.81
  1434.5 19.8 fusion.85
  1478.5 104.3 %all-reduce.22.cloned.1.call-done = bf16[1408,2,2048]{2,1,0:T(2,128)(2,1)} async-done(((bf16[1408,2,2048]{2,1,0:T(2,128)(2,1)}), bf16[1408,2,2048]{2,1,0:T(2,128)(2,1)}) %all-reduce.22.cloned.1.call-update) | async-done | bytes 11534352
  1601.9 44.0 %all-reduce.18 = (f32[2048]{0:T(1024)S(1)}, f32[512]{0:T(512)S(1)}, f32[2048]{0:T(1024)S(1)}) all-reduce(f32[2048]{0:T(1024)S(1)} %get-tuple-element.352, f32[512]{0:T(512)S(1)} %get-tuple-element.354, f32[2048]{0:T(1024)S(1)} %copy-done.53), channel_id=2, replica_groups=mesh['dp'=4,'seq'=8] {'dp','seq'}, use_global_device_ids=true, to_apply=%region_26.29.clone | all-reduce | flops 4608 | bytes 36864
  1649.0 319.5 %reduce-scatter.20.cloned.1.call-done = bf16[512,2,2816]{0,2,1:T(8,128)(2,1)} async-done(((bf16[2048,2,2816]{0,2,1:T(8,128)(2,1)}), bf16[512,2,2816]{0,2,1:T(8,128)(2,1)}) %reduce-scatter.20.cloned.1.call-update) | async-done | bytes 5767184 | tf_op jit(solution)/shard_map/reduce_scatter | solution.py:343
  1968.5 15.6 copy.234
  1984.1 114.0 %reduce-scatter.10.cloned.1.call-done = f32[64,576]{1,0:T(8,128)} async-done(((f32[2048,576]{1,0:T(8,128)}), f32[64,576]{1,0:T(8,128)}) %reduce-scatter.10.cloned.1.call-update) | async-done | bytes 147472 | tf_op jit(solution)/shard_map/reduce_scatter | solution.py:400
  2098.2 148.6 %reduce-scatter.12.cloned.1.call-done = f32[16,4096]{1,0:T(8,128)} async-done(((f32[512,4096]{1,0:T(8,128)}), f32[16,4096]{1,0:T(8,128)}) %reduce-scatter.12.cloned.1.call-update) | async-done | bytes 262160 | tf_op jit(solution)/shard_map/reduce_scatter | solution.py:402
  2246.8 198.4 %reduce-scatter.14.cloned.1.call-done = f32[64,2048]{1,0:T(8,128)} async-done(((f32[2048,2048]{1,0:T(8,128)}), f32[64,2048]{1,0:T(8,128)}) %reduce-scatter.14.cloned.1.call-update) | async-done | bytes 524304 | tf_op jit(solution)/shard_map/reduce_scatter | solution.py:403
  2445.2 253.4 %reduce-scatter.8.cloned.1.call-done = f32[64,3072]{1,0:T(8,128)} async-done(((f32[2048,3072]{1,0:T(8,128)}), f32[64,3072]{1,0:T(8,128)}) %reduce-scatter.8.cloned.1.call-update) | async-done | bytes 786448 | tf_op jit(solution)/shard_map/reduce_scatter | solution.py:399
  2698.6 252.3 %reduce-scatter.18.cloned.1.call-done = f32[88,2048]{1,0:T(8,128)} async-done(((f32[2816,2048]{1,0:T(8,128)}), f32[88,2048]{1,0:T(8,128)}) %reduce-scatter.18.cloned.1.call-update) | async-done | bytes 720912 | tf_op jit(solution)/shard_map/reduce_scatter | solution.py:367
  2950.8 498.4 %reduce-scatter.16.cloned.1.call-done = f32[64,5632]{1,0:T(8,128)} async-done(((f32[2048,5632]{1,0:T(8,128)}), f32[64,5632]{1,0:T(8,128)}) %reduce-scatter.16.cloned.1.call-update) | async-done | bytes 1441808 | tf_op jit(solution)/shard_map/reduce_scatter | solution.py:366
  (409 shorter events, 437.0 us)
Async XLA Ops:
  7.2 62.1 %all-gather.11.cloned.1.call-start = ((), (), s32[]{:S(2)}) async-start(), calls=%async_computation.16 | async-start | bytes 2703360 | tf_op jit(solution)/shard_map/all_gather | solution.py:203
  7.9 124.8 %all-gather.13.cloned.1.call-start = ((), (), s32[]{:S(2)}) async-start(), calls=%async_computation.17 | async-start | bytes 4325376 | tf_op jit(solution)/shard_map/all_gather | solution.py:205
  8.7 221.2 %all-gather.9.cloned.1.call-start = ((), (), s32[]{:S(2)}) async-start(), calls=%async_computation.15 | async-start | bytes 12976128 | tf_op jit(solution)/shard_map/all_gather | solution.py:202
  9.4 315.4 %all-gather.15.cloned.1.call-start = ((), (), s32[]{:S(2)}) async-start(), calls=%async_computation.18 | async-start | bytes 8650752 | tf_op jit(solution)/shard_map/all_gather | solution.py:206
  10.0 694.9 %all-gather.21.cloned.1.call-start = ((), (), s32[]{:S(2)}) async-start(), calls=%async_computation.21 | async-start | bytes 28835840 | tf_op jit(solution)/shard_map/all_gather | solution.py:294
  16.0 889.6 %all-gather.23.cloned.1.call-start = ((), (), s32[]{:S(2)}) async-start(), calls=%async_computation.22 | async-start | bytes 14417920 | tf_op jit(solution)/shard_map/all_gather | solution.py:295
  20.7 1224.4 %all-gather.17.cloned.1.call-start = ((), (), s32[]{:S(2)}) async-start(), calls=%async_computation.19 | async-start | bytes 23789568 | tf_op jit(solution)/shard_map/all_gather | solution.py:208
  61.8 168.1 %copy-start.34 = (f32[2048]{0:T(1024)}, f32[2048]{0:T(1024)S(1)}, u32[]{:S(2)}) copy-start(f32[2048]{0:T(1024)S(1)} %convert_element_type.173) | copy-start | bytes 24580
  61.8 75.0 %copy-start.44 = (f32[512]{0:T(512)}, f32[512]{0:T(512)S(1)}, u32[]{:S(2)}) copy-start(f32[512]{0:T(512)S(1)} %convert_element_type.176) | copy-start | bytes 6148
  62.1 167.8 %copy-start.54 = (f32[128]{0:T(128)}, f32[128]{0:T(128)S(1)}, u32[]{:S(2)}) copy-start(f32[128]{0:T(128)S(1)} %fusion.110) | copy-start | bytes 1540
  62.2 175.9 %copy-start.36 = (f32[128,32]{0,1:T(8,128)}, f32[128,32]{0,1:T(8,128)S(1)}, u32[]{:S(2)}) copy-start(f32[128,32]{0,1:T(8,128)S(1)} %get-tuple-element.432) | copy-start | bytes 49156
  62.2 175.9 %copy-start.38 = (f32[128,32]{0,1:T(8,128)}, f32[128,32]{0,1:T(8,128)S(1)}, u32[]{:S(2)}) copy-start(f32[128,32]{0,1:T(8,128)S(1)} %get-tuple-element.433) | copy-start | bytes 49156
  72.2 165.8 %copy-start.16 = (f32[128,576]{0,1:T(8,128)}, f32[128,576]{0,1:T(8,128)S(1)}, u32[]{:S(2)}) copy-start(f32[128,576]{0,1:T(8,128)S(1)} %fusion.127) | copy-start | bytes 884740
  72.5 165.5 %copy-start.70 = (f32[128]{0:T(128)}, f32[128]{0:T(128)S(1)}, u32[]{:S(2)}) copy-start(f32[128]{0:T(128)S(1)} %multiply_reduce_fusion.7) | copy-start | bytes 1540
  72.5 165.5 %copy-start.56 = (f32[128]{0:T(128)}, f32[128]{0:T(128)S(1)}, u32[]{:S(2)}) copy-start(f32[128]{0:T(128)S(1)} %fusion.111) | copy-start | bytes 1540
  239.8 35.1 %all-to-all-start = ((bf16[1,128,16,512]{1,3,0,2:T(8,128)(2,1)}), bf16[1,128,16,512]{1,3,0,2:T(8,128)(2,1)}, u32[]{:S(2)}, u32[]{:S(2)}) async-start(bf16[1,128,16,512]{1,3,0,2:T(8,128)(2,1)} %bitcast.274), calls=%async_computation | async-start | bytes 4194304 | tf_op jit(solution)/shard_map/all_to_all | solution.py:238
  244.3 1013.2 %all-gather.19.cloned.1.call-start = ((), (), s32[]{:S(2)}) async-start(), calls=%async_computation.20 | async-start | bytes 11894784 | tf_op jit(solution)/shard_map/all_gather | solution.py:209
  303.0 15.9 all-to-all-start.1
  318.9 73.6 %all-to-all-start.4 = ((bf16[8,2,96,2048]{3,2,1,0:T(8,128)(2,1)}), bf16[8,2,96,2048]{3,2,1,0:T(8,128)(2,1)}, u32[]{:S(2)}, u32[]{:S(2)}) async-start(bf16[8,2,96,2048]{3,2,1,0:T(8,128)(2,1)} %multiply_convert_fusion.1), calls=%async_computation.4 | async-start | bytes 12582912 | tf_op jit(solution)/shard_map/all_to_all | solution.py:320
  392.5 76.4 %all-to-all-start.2 = ((bf16[8,2,96,2048]{3,2,1,0:T(8,128)(2,1)}), bf16[8,2,96,2048]{3,2,1,0:T(8,128)(2,1)}, u32[]{:S(2)}, u32[]{:S(2)}) async-start(bf16[8,2,96,2048]{3,2,1,0:T(8,128)(2,1)} %select_select_fusion), calls=%async_computation.2 | async-start | bytes 12582912 | tf_op jit(solution)/shard_map/all_to_all | solution.py:291
  400.8 1182.0 %all-reduce.22.cloned.1.call-start = ((), (), s32[]{:S(2)}) async-start(), calls=%async_computation.30 | async-start | bytes 23068672
  491.6 414.0 %copy-start.26 = (bf16[2,384,2048]{1,2,0:T(8,128)(2,1)S(1)}, bf16[2,384,2048]{1,2,0:T(8,128)(2,1)}, u32[]{:S(2)}) copy-start(bf16[2,384,2048]{1,2,0:T(8,128)(2,1)} %copy.220) | copy-start | bytes 9437188
  964.9 1003.7 %reduce-scatter.20.cloned.1.call-start = ((), (), s32[]{:S(2)}) async-start(), calls=%async_computation.29 | async-start | bytes 28835840 | tf_op jit(solution)/shard_map/reduce_scatter | solution.py:343
  1123.9 87.8 %all-to-all-start.3 = ((bf16[8,2,96,2048]{3,2,1,0:T(8,128)(2,1)}), bf16[8,2,96,2048]{3,2,1,0:T(8,128)(2,1)}, u32[]{:S(2)}, u32[]{:S(2)}) async-start(bf16[8,2,96,2048]{3,2,1,0:T(8,128)(2,1)} %get-tuple-element.425), calls=%async_computation.3 | async-start | bytes 12582912 | tf_op jit(solution)/shard_map/all_to_all | solution.py:306
  1293.5 13.5 all-to-all-start.6
  1299.9 798.3 %reduce-scatter.10.cloned.1.call-start = ((), (), s32[]{:S(2)}) async-start(), calls=%async_computation.24 | async-start | bytes 5406720 | tf_op jit(solution)/shard_map/reduce_scatter | solution.py:400
  1394.5 852.3 %reduce-scatter.12.cloned.1.call-start = ((), (), s32[]{:S(2)}) async-start(), calls=%async_computation.25 | async-start | bytes 8650752 | tf_op jit(solution)/shard_map/reduce_scatter | solution.py:402
  1399.4 1045.8 %reduce-scatter.14.cloned.1.call-start = ((), (), s32[]{:S(2)}) async-start(), calls=%async_computation.26 | async-start | bytes 17301504 | tf_op jit(solution)/shard_map/reduce_scatter | solution.py:403
  1408.9 1289.7 %reduce-scatter.8.cloned.1.call-start = ((), (), s32[]{:S(2)}) async-start(), calls=%async_computation.23 | async-start | bytes 25952256 | tf_op jit(solution)/shard_map/reduce_scatter | solution.py:399
  1422.9 1527.9 %reduce-scatter.18.cloned.1.call-start = ((), (), s32[]{:S(2)}) async-start(), calls=%async_computation.28 | async-start | bytes 23789568 | tf_op jit(solution)/shard_map/reduce_scatter | solution.py:367
  1434.5 2014.8 %reduce-scatter.16.cloned.1.call-start = ((), (), s32[]{:S(2)}) async-start(), calls=%async_computation.27 | async-start | bytes 47579136 | tf_op jit(solution)/shard_map/reduce_scatter | solution.py:366
  1600.7 47.0 %copy-start.69 = (f32[128]{0:T(128)S(1)}, f32[128]{0:T(128)}, u32[]{:S(2)}) copy-start(f32[128]{0:T(128)} %copy-done.68) | copy-start | bytes 1540
  (72 other events, 448.9 us)
Sparse Core Ops, SparseCore 0:
  10.8 58.3 all-gather.10
  72.1 60.5 all-gather.12
  135.6 94.1 all-gather.8
  232.6 83.6 all-gather.14
  318.2 386.6 all-gather.20
  706.3 199.2 all-gather.22
  908.4 144.1 all-gather.16
  1055.5 117.6 all-gather.18
  1175.6 407.1 all-reduce.21
  1585.1 383.4 reduce-scatter.19
  1971.5 126.6 reduce-scatter.9
  2101.0 145.7 reduce-scatter.11
  2249.7 195.3 reduce-scatter.13
  2453.2 245.3 reduce-scatter.7
  2701.3 249.4 reduce-scatter.17
  2953.6 495.6 reduce-scatter.15
where the time goes:
time: 3470 us; the launch traced here: 3460 us
  waiting for transfers between devices  2640 us (76%)
  matrix products  275 us (8%)
  local copies, waits for them, and re-layouts  202 us (6%)
  blocking collectives  202 us (6%)
  other arithmetic  80.1 us (2%)
  starting transfers between devices  38.7 us (1%)
    reduce_scatter x1, waiting for transfers between devices, body(): lax.psum_scatter(grad_gate_up, ('dp', 'seq'), scatter_dimension=0, tiled=...  498 us
    reduce_scatter x1, waiting for transfers between devices, body(): lax.psum_scatter(grad_expert_in.astype(jnp.bfloat16), 'dp', scatter_dimen...  320 us
    reduce_scatter x1, waiting for transfers between devices, body(): lax.psum_scatter(grad_q, ('dp', 'seq'), scatter_dimension=0, tiled=True)  253 us
    reduce_scatter x1, waiting for transfers between devices, body(): lax.psum_scatter(grad_shared, ('dp', 'seq'), scatter_dimension=0, tiled=T...  252 us
    all_gather x1, waiting for transfers between devices, body(): lax.all_gather(expert_gate_up, 'dp', axis=0, tiled=True)  213 us
    reduce_scatter x1, waiting for transfers between devices, body(): lax.psum_scatter(grad_out_weight, ('dp', 'seq'), scatter_dimension=0, til...  198 us
    all_gather x1, waiting for transfers between devices, body(): lax.all_gather(expert_down, 'dp', axis=0, tiled=True)  183 us
    reduce_scatter x1, waiting for transfers between devices, body(): lax.psum_scatter(grad_kv_up, ('dp', 'seq'), scatter_dimension=0, tiled=True)  149 us
  transfers between devices with their start and end apart: 22, of which 18 were waited for; matrix products, arithmetic and copies ran while one was open for 16% of the time, Pallas kernels for 0%

commit v1 on v0

v1 whole, which is shorter than its diff:
```python
import jax
import jax.numpy as jnp
from jax import lax
from jax.sharding import PartitionSpec as P

H = 16
NOPE = 128
ROPE = 64
VD = 128
KV_RANK = 512
TOP = 6

EPS = 1e-06
THETA = 10000.0
GATE_UNIT = 16384.0

BOTH = ("dp", "seq")
F32 = jnp.float32
BF16 = jnp.bfloat16


def contract(left_side, right_side, left_dim, right_dim):
    return lax.dot_general(
        left_side,
        right_side,
        (((left_dim,), (right_dim,)), ((), ())),
        preferred_element_type=F32,
    )


def matmul(left_side, right_side):
    return contract(left_side, right_side, left_side.ndim - 1, 0)


def lead_dot(left_side, right_side):
    return contract(left_side, right_side, 0, 0)


def tail_dot(left_side, right_side):
    return contract(left_side, right_side, 1, 1)


def rms_scale(values):
    return lax.rsqrt(jnp.mean(values * values, axis=-1, keepdims=True) + EPS)


def rms_back(values, gain, grad):
    scale = rms_scale(values)
    unit = values * scale
    weighted = grad * gain
    centre = jnp.mean(weighted * unit, axis=-1, keepdims=True)
    return scale * (weighted - unit * centre), jnp.sum(grad * unit, axis=0)


def swiglu(gate, up):
    return jax.nn.silu(gate) * up


def swiglu_back(gate, up, grad):
    sig = jax.nn.sigmoid(gate)
    return grad * up * sig * (1.0 + gate * (1.0 - sig)), grad * (gate * sig)


def rotary_tables(positions):
    half_width = ROPE // 2
    frequency = THETA ** (-jnp.arange(half_width, dtype=F32) * 2.0 / ROPE)
    angles = positions.astype(F32)[:, None] * frequency[None, :]
    return jnp.cos(angles), jnp.sin(angles)


def rotate(values, cosine, sine):
    half_width = values.shape[-1] // 2
    lead = values[..., :half_width]
    trail = values[..., half_width:]
    return jnp.concatenate([lead * cosine - trail * sine, trail * cosine + lead * sine], axis=-1)


def rotate_back(grads, cosine, sine):
    return rotate(grads, cosine, -sine)


def scatter_sum(values, axis_name, parts):
    moved = lax.all_to_all(values.astype(BF16), axis_name, split_axis=0, concat_axis=0, tiled=True)
    return jnp.sum(moved.reshape((parts, -1) + values.shape[1:]).astype(F32), axis=0)


def body(
    hidden,
    cotangent,
    attn_gain,
    q_weight,
    kv_down,
    kv_gain,
    kv_up,
    out_weight,
    ffn_gain,
    shared_gate_up,
    shared_down,
    expert_gate_up,
    expert_down,
    expert_ids,
    gate_fix,
    block_ids,
):
    n_dp = lax.axis_size("dp")
    n_seq = lax.axis_size("seq")
    n_all = n_dp * n_seq
    dp_index = lax.axis_index("dp")
    seq_index = lax.axis_index("seq")
    tokens, width = hidden.shape
    sequences, length = block_ids.shape
    part = length // n_seq
    group = n_seq * tokens
    heads = H // n_seq
    per_device = expert_gate_up.shape[1]
    experts = per_device * n_seq
    capacity = TOP * tokens // per_device
    ff_parts = n_dp // per_device
    expert_bit = dp_index % per_device
    down_rows = kv_down.shape[0]
    down_width = kv_down.shape[1]
    q_width = heads * (NOPE + ROPE)
    e_width = heads * (NOPE + VD)

    labels = jnp.arange(experts, dtype=jnp.int32)
    hits = jnp.sum((expert_ids[:, :, None] == labels).astype(jnp.int32), axis=1)
    earlier = jnp.arange(group, dtype=jnp.int32)[:, None] < seq_index * tokens
    before_own = jnp.sum(jnp.where(earlier, hits, 0), axis=0)
    own_hits = lax.dynamic_slice_in_dim(hits, seq_index * tokens, tokens, 0)
    own_picks = lax.dynamic_slice_in_dim(expert_ids, seq_index * tokens, tokens, 0)
    own_slot = before_own[None, :] + jnp.cumsum(own_hits, axis=0) - own_hits
    code = jnp.where((own_hits > 0) & (own_slot < capacity), own_slot + 1, 0)
    gates = jnp.sum(
        gate_fix[:, :, None] * (own_picks[:, :, None] == labels).astype(jnp.int32), axis=1
    )
    pieces = jnp.stack([code // 16, code % 16, gates // 128, gates % 128], axis=0)
    pieces = jnp.transpose(pieces, (2, 0, 1)).reshape(experts, 4 * tokens).astype(BF16)

    def wide_row(vector):
        return jnp.pad(vector, (0, down_width - 4 * tokens - vector.shape[0]))[None]

    extras = jnp.concatenate([wide_row(attn_gain), wide_row(ffn_gain), wide_row(kv_gain)], axis=0)
    extras = jnp.pad(extras, ((0, experts - 3), (0, 0)))
    message = jnp.concatenate(
        [kv_down, jnp.concatenate([pieces, extras], axis=1)], axis=0
    )
    spread = lax.all_gather(message, BOTH, axis=0, tiled=False)
    weight_down = spread[:, :down_rows].reshape(-1, down_width)
    spread_tail = spread[:, down_rows:]
    first = 4 * tokens
    gain_attn = spread_tail[:, 0, first : first + attn_gain.shape[0]].reshape(-1).astype(F32)
    gain_ffn = spread_tail[:, 1, first : first + ffn_gain.shape[0]].reshape(-1).astype(F32)
    gain_kv = spread_tail[:, 2, first : first + kv_gain.shape[0]].reshape(-1).astype(F32)
    own_expert = per_device * seq_index + expert_bit
    routing = lax.dynamic_index_in_dim(spread_tail, own_expert, axis=1, keepdims=False)
    routing = routing[:, :first].reshape(n_all, 4, tokens).astype(jnp.int32)
    slot_code = (routing[:, 0] * 16 + routing[:, 1]).reshape(n_dp, group)
    gate_of = (routing[:, 2] * 128 + routing[:, 3]).astype(F32).reshape(n_dp, group) / GATE_UNIT

    q_rows = lax.all_to_all(q_weight, "seq", split_axis=1, concat_axis=0, tiled=True)
    up_rows = lax.all_to_all(kv_up, "seq", split_axis=1, concat_axis=0, tiled=True)
    up_shape = up_rows.shape
    joined = jnp.concatenate([q_rows, up_rows.reshape(q_rows.shape[0], -1)], axis=1)
    joined = lax.all_gather(joined, "dp", axis=0, tiled=True)
    weight_q = joined[:, :q_width]
    weight_up = joined[:, q_width:].reshape(n_dp * up_shape[0], up_shape[1])
    weight_out = lax.all_gather(out_weight, BOTH, axis=0, tiled=True)

    units = shared_down.shape[0]
    gate_up_parts = shared_gate_up.reshape(-1, 2, n_all, units)
    gate_up_parts = jnp.transpose(gate_up_parts, (2, 0, 1, 3)).reshape(n_all, -1, 2 * units)
    weight_shared_in = lax.all_to_all(
        gate_up_parts, BOTH, split_axis=0, concat_axis=0, tiled=True
    ).reshape(-1, 2 * units)

    ff_width = expert_gate_up.shape[2] // 2
    ff_part = ff_width // ff_parts
    expert_rows = expert_gate_up.shape[0]
    in_parts = expert_gate_up.reshape(expert_rows, per_device, 2, ff_parts, ff_part)
    in_parts = jnp.transpose(in_parts, (3, 1, 0, 2, 4)).reshape(n_dp, expert_rows, 2 * ff_part)
    weight_in = lax.all_to_all(in_parts, "dp", split_axis=0, concat_axis=0, tiled=True)
    weight_in = weight_in.reshape(-1, 2 * ff_part)
    swap = [(i, i ^ 1) for i in range(n_dp)]
    down_kept = lax.dynamic_index_in_dim(expert_down, expert_bit, 1, keepdims=False)
    down_sent = lax.dynamic_index_in_dim(expert_down, 1 - expert_bit, 1, keepdims=False)
    down_got = lax.ppermute(down_sent, "dp", swap)
    is_low = expert_bit == 0
    weight_back = jnp.concatenate(
        [jnp.where(is_low, down_kept, down_got), jnp.where(is_low, down_got, down_kept)], axis=0
    )

    cot_all = lax.all_gather(cotangent, BOTH, axis=0, tiled=True)

    hidden_group = lax.all_gather(hidden, "seq", axis=0, tiled=True)
    rows_group = hidden_group.astype(F32)
    normed_group = (rows_group * rms_scale(rows_group) * gain_attn).astype(BF16)
    group_row = jnp.arange(group, dtype=jnp.int32)
    positions = group_row // tokens * part + group_row % part
    cosine, sine = rotary_tables(positions)

    def to_sequence(values):
        split = values.reshape((n_seq, sequences, part) + values.shape[1:])
        return jnp.swapaxes(split, 0, 1).reshape((sequences, length) + values.shape[1:])

    def to_rows(values):
        split = values.reshape((sequences, n_seq, part) + values.shape[2:])
        return jnp.swapaxes(split, 0, 1).reshape((group,) + values.shape[2:])

    query_raw = matmul(normed_group, weight_q).reshape(group, heads, NOPE + ROPE)
    latent_in = matmul(normed_group, weight_down)
    latent_raw = latent_in[:, :KV_RANK]
    latent = (latent_raw * rms_scale(latent_raw) * gain_kv).astype(BF16)
    expanded = matmul(latent, weight_up).reshape(group, heads, NOPE + VD)
    rope_query = rotate(query_raw[..., NOPE:], cosine[:, None], sine[:, None])
    rope_key = rotate(latent_in[:, KV_RANK:], cosine, sine)
    rope_key = jnp.broadcast_to(rope_key[:, None], (group, heads, ROPE))
    queries = to_sequence(
        jnp.concatenate([query_raw[..., :NOPE], rope_query], axis=-1).astype(BF16)
    )
    keys = to_sequence(
        jnp.concatenate([expanded[..., :NOPE], rope_key], axis=-1).astype(BF16)
    )
    values = to_sequence(expanded[..., NOPE:].astype(BF16))
    score_scale = (NOPE + ROPE) ** (-0.5)
    scores = jnp.einsum("bqhd,bkhd->bhqk", queries, keys, preferred_element_type=F32) * score_scale
    allowed = block_ids[:, None, None, :] <= block_ids[:, None, :, None]
    scores = jnp.where(allowed, scores, -1e30)
    weights = jnp.exp(scores - jnp.max(scores, axis=-1, keepdims=True))
    probs = weights / jnp.sum(weights, axis=-1, keepdims=True)
    shares = probs.astype(BF16)
    attended = jnp.einsum("bhqk,bkhd->bqhd", shares, values, preferred_element_type=F32)
    attended = to_rows(attended.astype(BF16)).reshape(group, heads * VD)
    heads_out = lax.all_to_all(attended, "seq", split_axis=0, concat_axis=1, tiled=True)

    rows = hidden.astype(F32)
    residual = rows + matmul(heads_out, weight_out)
    normed_ffn = (residual * rms_scale(residual) * gain_ffn).astype(BF16)
    ffn_all = lax.all_gather(normed_ffn, BOTH, axis=0, tiled=True)

    shared_in = matmul(ffn_all, weight_shared_in)
    shared_gate, shared_up = shared_in[:, :units], shared_in[:, units:]
    shared_act = swiglu(shared_gate, shared_up).astype(BF16)
    shared_act_grad = tail_dot(cot_all, shared_down)
    grad_shared_down = lead_dot(shared_act, cot_all)
    shared_in_grad = jnp.concatenate(
        swiglu_back(shared_gate, shared_up, shared_act_grad), axis=1
    ).astype(BF16)
    grad_shared_in = lead_dot(ffn_all, shared_in_grad)

    slots = jnp.arange(1, capacity + 1, dtype=jnp.int32)
    placed = (slot_code[:, :, None] == slots).astype(BF16)
    slot_gate = jnp.sum(
        jnp.where(slot_code[:, :, None] == slots, gate_of[:, :, None], 0.0), axis=1
    )[..., None]
    slot_rows = jnp.einsum(
        "gtc,gtd->gcd", placed, ffn_all.reshape(n_dp, group, width), preferred_element_type=F32
    ).astype(BF16)
    slot_cot = jnp.einsum(
        "gtc,gtd->gcd", placed, cot_all.reshape(n_dp, group, width), preferred_element_type=F32
    )
    slot_cot = (slot_cot * slot_gate).astype(BF16)
    slot_rows = slot_rows.reshape(n_dp * capacity, width)
    slot_cot = slot_cot.reshape(n_dp * capacity, width)
    expert_in = matmul(slot_rows, weight_in)
    expert_gate, expert_up = expert_in[:, :ff_part], expert_in[:, ff_part:]
    expert_act = swiglu(expert_gate, expert_up).astype(BF16)
    expert_act_grad = tail_dot(slot_cot, weight_back)
    grad_back = lead_dot(expert_act, slot_cot)
    expert_in_grad = jnp.concatenate(
        swiglu_back(expert_gate, expert_up, expert_act_grad), axis=1
    ).astype(BF16)
    grad_in = lead_dot(slot_rows, expert_in_grad)
    slot_grad = tail_dot(expert_in_grad, weight_in).astype(BF16)
    expert_out = matmul(expert_act, weight_back).reshape(n_dp, capacity, width)
    expert_out = (expert_out * slot_gate).astype(BF16)

    dn_part = jnp.einsum(
        "gtc,gcd->gtd",
        placed,
        slot_grad.reshape(n_dp, capacity, width),
        preferred_element_type=F32,
    ).reshape(n_all * tokens, width) + tail_dot(shared_in_grad, weight_shared_in)
    ffn_grad = lax.psum_scatter(dn_part.astype(BF16), BOTH, scatter_dimension=0, tiled=True)
    ffn_grad = ffn_grad.astype(F32)
    out_part = jnp.einsum(
        "gtc,gcd->gtd", placed, expert_out, preferred_element_type=F32
    ).reshape(n_all * tokens, width) + matmul(shared_act, shared_down)
    out_sum = lax.psum_scatter(out_part.astype(BF16), BOTH, scatter_dimension=0, tiled=True)
    output = (residual + out_sum.astype(F32)).astype(BF16)

    in_back = lax.all_to_all(
        grad_in.astype(BF16).reshape(n_dp, expert_rows, 2 * ff_part),
        "dp",
        split_axis=0,
        concat_axis=0,
        tiled=True,
    ).reshape(ff_parts, per_device, expert_rows, 2, ff_part)
    grad_expert_in = jnp.transpose(in_back, (2, 1, 3, 0, 4)).reshape(expert_gate_up.shape)
    grad_expert_in = grad_expert_in.astype(F32)
    half = expert_down.shape[0]
    low_half, high_half = grad_back[:half], grad_back[half:]
    grad_kept = jnp.where(is_low, low_half, high_half)
    grad_sent = jnp.where(is_low, high_half, low_half).astype(BF16)
    grad_got = lax.ppermute(grad_sent, "dp", swap).astype(F32)
    grad_expert_down = jnp.stack(
        [jnp.where(is_low, grad_kept, grad_got), jnp.where(is_low, grad_got, grad_kept)], axis=1
    )

    shared_back = lax.all_to_all(
        grad_shared_in.astype(BF16).reshape(n_all, -1, 2 * units),
        BOTH,
        split_axis=0,
        concat_axis=0,
        tiled=True,
    ).reshape(n_all, -1, 2, units)
    grad_shared_gate_up = jnp.transpose(shared_back, (1, 2, 0, 3)).reshape(shared_gate_up.shape)
    grad_shared_gate_up = grad_shared_gate_up.astype(F32)

    from_norm, gain_ffn_grad = rms_back(residual, gain_ffn, ffn_grad)
    residual_grad = cotangent.astype(F32) + from_norm
    residual_low = residual_grad.astype(BF16)
    heads_grad = tail_dot(residual_low, weight_out).astype(BF16)
    heads_grad = lax.all_to_all(heads_grad, "seq", split_axis=1, concat_axis=0, tiled=True)
    residual_group = lax.all_gather(residual_low, "seq", axis=0, tiled=True)
    grad_out_heads = lead_dot(attended, residual_group)
    out_shard = scatter_sum(grad_out_heads, "dp", n_dp)
    home = [
        (d * n_seq + s, s * n_dp + d) for d in range(n_dp) for s in range(n_seq)
    ]
    grad_out_weight = lax.ppermute(out_shard, BOTH, home)

    grad_o = to_sequence(heads_grad.reshape(group, heads, VD))
    prob_grad = jnp.einsum("bqhd,bkhd->bhqk", grad_o, values, preferred_element_type=F32)
    centre = jnp.sum(probs * prob_grad, axis=-1, keepdims=True)
    score_grad = (probs * (prob_grad - centre)).astype(BF16)
    query_grad = jnp.einsum("bhqk,bkhd->bqhd", score_grad, keys, preferred_element_type=F32)
    key_grad = jnp.einsum("bhqk,bqhd->bkhd", score_grad, queries, preferred_element_type=F32)
    value_grad = jnp.einsum("bhqk,bqhd->bkhd", shares, grad_o, preferred_element_type=F32)
    query_grad = to_rows((query_grad * score_scale).astype(BF16)).astype(F32)
    key_grad = to_rows((key_grad * score_scale).astype(BF16)).astype(F32)
    value_grad = to_rows(value_grad.astype(BF16))
    query_low = jnp.concatenate(
        [
            query_grad[..., :NOPE],
            rotate_back(query_grad[..., NOPE:], cosine[:, None], sine[:, None]),
        ],
        axis=-1,
    ).astype(BF16).reshape(group, q_width)
    rope_grad = rotate_back(jnp.sum(key_grad[..., NOPE:], axis=1), cosine, sine)
    expand_low = jnp.concatenate(
        [key_grad[..., :NOPE].astype(BF16), value_grad], axis=-1
    ).reshape(group, e_width)

    latent_part = tail_dot(expand_low, weight_up)
    latent_sum = scatter_sum(jnp.concatenate([latent_part, rope_grad], axis=1), "seq", n_seq)
    normed_sum = scatter_sum(tail_dot(query_low, weight_q), "seq", n_seq)
    grad_q = scatter_sum(lead_dot(normed_group, query_low), "dp", n_dp)
    grad_q = lax.all_to_all(grad_q, "seq", split_axis=0, concat_axis=1, tiled=True)
    grad_up = scatter_sum(lead_dot(latent, expand_low), "dp", n_dp)
    grad_up = lax.all_to_all(grad_up, "seq", split_axis=0, concat_axis=1, tiled=True)

    own_latent = lax.dynamic_slice_in_dim(latent_raw, seq_index * tokens, tokens, 0)
    latent_grad, gain_kv_grad = rms_back(own_latent, gain_kv, latent_sum[:, :KV_RANK])
    down_low = jnp.concatenate([latent_grad, latent_sum[:, KV_RANK:]], axis=1).astype(BF16)
    down_group = lax.all_gather(down_low, "seq", axis=0, tiled=True)
    normed_cols = normed_group.reshape(group, n_dp, n_seq, down_rows)
    normed_cols = lax.dynamic_index_in_dim(normed_cols, seq_index, 2, keepdims=False)
    grad_down = lead_dot(normed_cols.reshape(group, n_dp * down_rows), down_group)
    grad_down = scatter_sum(grad_down, "dp", n_dp)

    normed_grad = normed_sum + tail_dot(down_low, weight_down)
    rows_from_norm, gain_attn_grad = rms_back(rows, gain_attn, normed_grad)
    input_grad = residual_grad + rows_from_norm

    gain_grads = jnp.concatenate(
        [
            gain_attn_grad.reshape(n_all, -1),
            gain_ffn_grad.reshape(n_all, -1),
            gain_kv_grad.reshape(n_all, -1),
        ],
        axis=1,
    )
    gain_grads = lax.all_to_all(gain_grads, BOTH, split_axis=0, concat_axis=0, tiled=True)
    gain_grads = jnp.sum(gain_grads, axis=0)
    attn_end = attn_gain.shape[0]
    ffn_end = attn_end + ffn_gain.shape[0]

    return (
        output,
        input_grad,
        gain_grads[:attn_end],
        grad_q,
        grad_down,
        gain_grads[ffn_end:],
        grad_up,
        grad_out_weight,
        gain_grads[attn_end:ffn_end],
        grad_shared_gate_up,
        grad_shared_down,
        grad_expert_in,
        grad_expert_down,
    )


def solution(mesh):
    rows = P(BOTH, None)
    return jax.shard_map(
        body,
        mesh=mesh,
        in_specs=(
            rows,
            rows,
            P(BOTH),
            rows,
            rows,
            P(BOTH),
            rows,
            rows,
            P(BOTH),
            rows,
            rows,
            P("dp", "seq", None),
            P("dp", "seq", None),
            P("dp", None),
            rows,
            P("dp", None),
        ),
        out_specs=(
            rows,
            rows,
            P(BOTH),
            rows,
            rows,
            P(BOTH),
            rows,
            rows,
            P(BOTH),
            rows,
            rows,
            P("dp", "seq", None),
            P("dp", "seq", None),
        ),
        check_vma=False,
    )
```

time: 3470 us -> 1560 us (0.45)
  waiting for transfers between devices: 2640 us -> 935 us
  blocking collectives: 202 us -> 0 us
  starting transfers between devices: 38.7 us -> 116 us
  local copies, waits for them, and re-layouts: 202 us -> 138 us
    reduce_scatter x7 -> x2, waiting for transfers between devices: 1780 us -> 183 us  [the longest x1 183 us: body(): lax.psum_scatter(dn_part.astype(BF16), BOTH, scatter_dimension=0, tiled=T...]
    all_gather x8, waiting for transfers between devices: 555 us -> 262 us  [the longest x1 89.7 us: body(): ffn_all = lax.all_gather(normed_ffn, BOTH, axis=0, tiled=True)]
    ppermute x0 -> x3, waiting for transfers between devices: none -> 208 us  [the longest x1 173 us: body(): down_got = lax.ppermute(down_sent, 'dp', swap)]
    all_to_all x2 -> x0, blocking collectives: 119 us -> none  [the longest x1 86.9 us: body(): lax.all_to_all(pick_rows(slot_grad, back_index, back_live), 'seq', split_...]
    unnamed x17 -> x10, waiting for transfers between devices: 108 us -> 1.85 us
    all_to_all x6 -> x17, waiting for transfers between devices: 190 us -> 280 us  [the longest x1 187 us: body(): lax.all_to_all(grad_in.astype(BF16).reshape(n_dp, expert_rows, 2 * ff_par...]
    unnamed x2 -> x0, blocking collectives: 83.6 us -> none
    gather x13 -> x0, local copies, waits for them, and re-layouts: 80.4 us -> none  [the longest x6 50.5 us: pick_rows(): jnp.take(flat, row_index.reshape(-1), axis=0)]
  transfers between devices with their start and end apart: 22 -> 30, of which waited for: 18 -> 20; matrix products, arithmetic and copies ran while one was open for 16% -> 25% of each run, Pallas kernels for 0% -> 0%
where the time goes in v1:
time: 1560 us; the launch traced here: 1540 us
  waiting for transfers between devices  935 us (60%)
  matrix products  279 us (18%)
  local copies, waits for them, and re-layouts  138 us (9%)
  starting transfers between devices  116 us (7%)
  other arithmetic  59.5 us (4%)
  between operations  16 us (1%)
    dot_general x24, matrix products, contract(): lax.dot_general(left_side, right_side, (((left_dim,), (right_dim,)), ((),...  193 us
    all_to_all x1, waiting for transfers between devices, body(): lax.all_to_all(grad_in.astype(BF16).reshape(n_dp, expert_rows, 2 * ff_par...  187 us
    reduce_scatter x1, waiting for transfers between devices, body(): lax.psum_scatter(dn_part.astype(BF16), BOTH, scatter_dimension=0, tiled=T...  183 us
    ppermute x1, waiting for transfers between devices, body(): down_got = lax.ppermute(down_sent, 'dp', swap)  173 us
    all_gather x1, waiting for transfers between devices, body(): ffn_all = lax.all_gather(normed_ffn, BOTH, axis=0, tiled=True)  89.7 us
    all_gather x1, waiting for transfers between devices, body(): spread = lax.all_gather(message, BOTH, axis=0, tiled=False)  60.3 us
    unnamed x170, local copies, waits for them, and re-layouts  55.2 us
    all_to_all x6, waiting for transfers between devices, scatter_sum(): lax.all_to_all(values.astype(BF16), axis_name, split_axis=0, concat_axis=...  45.4 us
  transfers between devices with their start and end apart: 30, of which 20 were waited for; matrix products, arithmetic and copies ran while one was open for 25% of the time, Pallas kernels for 0%

profile of v1, /device:TPU:25, one launch (start us, length us, event | category | flops | bytes accessed | tf_op | source)
XLA Modules:
  0.0 1543.9 jit_solution(2052242703261144764)
XLA Ops:
  35.7 38.4 %all-gather.12.cloned.1.call-done = bf16[2048,512]{1,0:T(8,128)(2,1)} async-done(((bf16[512,512]{1,0:T(8,128)(2,1)}), bf16[2048,512]{1,0:T(8,128)(2,1)}) %all-gather.12.cloned.1.call-update) | async-done | bytes 2097168 | tf_op jit(solution)/shard_map/all_gather | solution.py:164
  76.5 60.3 %all-gather.24.cloned.1.call-done = bf16[2560,576]{1,0:T(8,128)(2,1)} async-done(((bf16[80,576]{1,0:T(8,128)(2,1)}), bf16[2560,576]{1,0:T(8,128)(2,1)}) %all-gather.24.cloned.1.call-update) | async-done | bytes 2949136 | tf_op jit(solution)/shard_map/all_gather | solution.py:147
  142.3 34.4 %all-gather.10.cloned.1.call-done = bf16[1024,2048]{0,1:T(8,128)(2,1)} async-done(((bf16[128,2048]{0,1:T(8,128)(2,1)}), bf16[1024,2048]{0,1:T(8,128)(2,1)}) %all-gather.10.cloned.1.call-update) | async-done | bytes 4194320 | tf_op jit(solution)/shard_map/all_gather | solution.py:194
  209.2 9.8 all-to-all-done.2
  219.0 39.1 %all-gather.14.cloned.1.call-done = bf16[2048,2048]{1,0:T(8,128)(2,1)} async-done(((bf16[64,2048]{1,0:T(8,128)(2,1)}), bf16[2048,2048]{1,0:T(8,128)(2,1)}) %all-gather.14.cloned.1.call-update) | async-done | bytes 8388624 | tf_op jit(solution)/shard_map/all_gather | solution.py:167
  264.0 14.9 copy.220
  291.4 10.2 constant_dynamic-slice_fusion.2
  309.0 173.2 %collective-permute-done = bf16[352,2048]{1,0:T(8,128)(2,1)} collective-permute-done((bf16[352,2048]{1,0:T(8,128)(2,1)}, bf16[352,2048]{1,0:T(8,128)(2,1)}, u32[]{:S(2)}, u32[]{:S(2)}) %collective-permute-start) | collective-permute-done | bytes 1441824 | tf_op jit(solution)/shard_map/ppermute | solution.py:186
  504.6 12.3 multiply_convert_fusion
  516.8 89.7 %all-gather.16.cloned.1.call-done = bf16[4096,2048]{1,0:T(8,128)(2,1)} async-done(((bf16[128,2048]{1,0:T(8,128)(2,1)}), bf16[4096,2048]{1,0:T(8,128)(2,1)}) %all-gather.16.cloned.1.call-update) | async-done | bytes 16777232 | tf_op jit(solution)/shard_map/all_gather | solution.py:238
  606.6 12.3 fusion.19
  618.9 14.3 fusion.147
  633.2 12.5 multiply_convert_fusion.5
  645.7 10.4 convolution_convert_fusion.1
  656.2 14.8 fusion.3
  671.0 13.1 fusion.148
  684.2 12.0 multiply_convert_fusion.11
  697.2 19.2 %fusion.1 = bf16[4096,2048]{1,0:T(8,128)(2,1)} fusion(f32[4,1024,2048]{2,1,0:T(8,128)} %fusion.3, bf16[2048,176]{1,0:T(8,128)(2,1)S(1)} %bitcast.222, bf16[4096,88]{0,1:T(8,128)(2,1)S(1)} %get-tuple-element.105, bf16[4096,88]{0,1:T(8,128)(2,1)S(1)} %get-tuple-element.104), kind=kOutput, calls=%fused_computation.2 | convolution fusion | flops 2972450816 | bytes 52494336 | tf_op jit(solution)/shard_map/dot_general | solution.py:23
  716.5 183.0 %reduce-scatter.5.cloned.1.call-done = bf16[128,2048]{1,0:T(8,128)(2,1)} async-done(((bf16[4096,2048]{1,0:T(8,128)(2,1)}), bf16[128,2048]{1,0:T(8,128)(2,1)}) %reduce-scatter.5.cloned.1.call-update) | async-done | bytes 524304 | tf_op jit(solution)/shard_map/reduce_scatter | solution.py:283
  950.6 12.3 all-to-all-done.7
  966.9 10.5 fusion.41
  977.4 20.0 %fusion.7 = f32[4,1024,2048]{2,1,0:T(8,128)} fusion(f32[4,384,2048]{2,1,0:T(8,128)} %bitcast.218, f32[4,384]{1,0:T(4,128)S(1)} %copy-done.48, s32[384]{0:T(512)S(1)} %iota_add_fusion, s32[4,1024]{1,0:T(4,128)S(1)} %add.295), kind=kOutput, calls=%fused_computation.9 | convolution fusion | flops 6450315264 | bytes 46161408 | tf_op jit(solution)/shard_map/gtc,gcd->gtd/dot_general | solution.py:285
  997.4 17.9 %fusion.2 = bf16[4096,2048]{1,0:T(8,128)(2,1)} fusion(f32[4,1024,2048]{2,1,0:T(8,128)} %fusion.7, bf16[4096,88]{0,1:T(8,128)(2,1)S(1)} %get-tuple-element.108, bf16[88,2048]{1,0:T(8,128)(2,1)S(1)} %copy-done), kind=kOutput, calls=%fused_computation.4 | convolution fusion | flops 1493172224 | bytes 51412992 | tf_op jit(solution)/shard_map/dot_general | solution.py:23
  1036.0 15.0 convolution_convert_fusion
  1059.4 13.5 all-to-all-done.15
  1084.3 187.3 %all-to-all-done.16 = bf16[4,512,1408]{1,2,0:T(8,128)(2,1)} async-done(((bf16[4,512,1408]{1,2,0:T(8,128)(2,1)}), bf16[4,512,1408]{1,2,0:T(8,128)(2,1)}, u32[]{:S(2)}, u32[]{:S(2)}) %all-to-all-start.16) | async-done | bytes 5767200 | tf_op jit(solution)/shard_map/all_to_all | solution.py:291
  1297.0 29.0 %all-to-all-done.9 = bf16[4,512,384]{2,1,0:T(8,128)(2,1)S(1)} async-done(((bf16[4,512,384]{2,1,0:T(8,128)(2,1)}), bf16[4,512,384]{2,1,0:T(8,128)(2,1)S(1)}, u32[]{:S(2)}, u32[]{:S(2)}) %all-to-all-start.9) | async-done | bytes 1572896 | tf_op jit(solution)/shard_map/all_to_all | solution.py:83
  1326.0 18.5 %all-to-all-start.13 = ((f32[8,16,512]{2,1,0:T(8,128)}), f32[8,16,512]{2,1,0:T(8,128)S(1)}, u32[]{:S(2)}, u32[]{:S(2)}) async-start(f32[8,16,512]{2,1,0:T(8,128)} %bitcast.64), calls=%async_computation.15 | async-start | bytes 524288 | tf_op jit(solution)/shard_map/all_to_all | solution.py:360
  1414.9 13.1 collective-permute-done.2
  1458.4 9.9 copy.247
  1468.3 17.8 %copy.248 = f32[512,2,2816]{2,1,0:T(2,128)} copy(f32[512,2,2816]{0,2,1:T(8,128)} %bitcast.213) | data formatting | bytes 23068672
  1513.3 21.5 %collective-permute-done.1 = f32[64,2048]{1,0:T(8,128)} collective-permute-done((f32[64,2048]{1,0:T(8,128)S(1)}, f32[64,2048]{1,0:T(8,128)}, u32[]{:S(2)}, u32[]{:S(2)}) %collective-permute-start.1) | collective-permute-done | bytes 524320 | tf_op jit(solution)/shard_map/ppermute | solution.py:330
  (364 shorter events, 367.7 us)
Async XLA Ops:
  7.2 677.0 %copy-start = (bf16[88,2048]{1,0:T(8,128)(2,1)S(1)}, bf16[88,2048]{1,0:T(8,128)(2,1)}, u32[]{:S(2)}) copy-start(bf16[88,2048]{1,0:T(8,128)(2,1)} %param.26) | copy-start | bytes 1081348
  8.9 9.1 all-to-all-start.1
  18.0 10.3 all-to-all-start
  22.2 51.8 %all-gather.12.cloned.1.call-start = ((), (), s32[]{:S(2)}) async-start(), calls=%async_computation.20 | async-start | bytes 2621440 | tf_op jit(solution)/shard_map/all_gather | solution.py:164
  29.1 107.6 %all-gather.24.cloned.1.call-start = ((), (), s32[]{:S(2)}) async-start(), calls=%async_computation.28 | async-start | bytes 3379200 | tf_op jit(solution)/shard_map/all_gather | solution.py:147
  32.2 144.5 %all-gather.10.cloned.1.call-start = ((), (), s32[]{:S(2)}) async-start(), calls=%async_computation.19 | async-start | bytes 4718592 | tf_op jit(solution)/shard_map/all_gather | solution.py:194
  33.3 224.9 %all-gather.14.cloned.1.call-start = ((), (), s32[]{:S(2)}) async-start(), calls=%async_computation.21 | async-start | bytes 8650752 | tf_op jit(solution)/shard_map/all_gather | solution.py:167
  33.8 470.7 %all-gather.18.cloned.1.call-start = ((), (), s32[]{:S(2)}) async-start(), calls=%async_computation.24 | async-start | bytes 17301504 | tf_op jit(solution)/shard_map/all_gather | solution.py:192
  205.5 13.5 all-to-all-start.2
  209.1 397.4 %all-gather.16.cloned.1.call-start = ((), (), s32[]{:S(2)}) async-start(), calls=%async_computation.22 | async-start | bytes 17301504 | tf_op jit(solution)/shard_map/all_gather | solution.py:238
  209.2 692.3 %copy-start.45 = (f32[2048]{0:T(1024)}, f32[2048]{0:T(1024)S(1)}, u32[]{:S(2)}) copy-start(f32[2048]{0:T(1024)S(1)} %reshape.635) | copy-start | bytes 24580
  284.5 205.5 %all-to-all-start.3 = ((bf16[4,512,1408]{1,2,0:T(8,128)(2,1)}), bf16[4,512,1408]{1,2,0:T(8,128)(2,1)}, u32[]{:S(2)}, u32[]{:S(2)}) async-start(bf16[4,512,1408]{1,2,0:T(8,128)(2,1)} %bitcast.216), calls=%async_computation.3 | async-start | bytes 11534336 | tf_op jit(solution)/shard_map/all_to_all | solution.py:181
  303.6 178.6 %collective-permute-start = (bf16[352,2048]{1,0:T(8,128)(2,1)}, bf16[352,2048]{1,0:T(8,128)(2,1)}, u32[]{:S(2)}, u32[]{:S(2)}) collective-permute-start(bf16[352,2048]{1,0:T(8,128)(2,1)} %bitcast.208), channel_id=1, source_target_pairs={{0,8},{8,0},{16,24},{24,16},{1,9},{9,1},{17,25},{25,17},{2,10},{10... | collective-permute-start | bytes 4325384 | tf_op jit(solution)/shard_map/ppermute | solution.py:186
  490.0 181.0 %all-to-all-start.4 = ((bf16[32,64,176]{2,1,0:T(8,128)(2,1)}), bf16[32,64,176]{2,1,0:T(8,128)(2,1)S(1)}, u32[]{:S(2)}, u32[]{:S(2)}) async-start(bf16[32,64,176]{2,1,0:T(8,128)(2,1)} %reshape.617), calls=%async_computation.4 | async-start | bytes 2097152 | tf_op jit(solution)/shard_map/all_to_all | solution.py:172
  496.1 403.3 %reduce-scatter.5.cloned.1.call-start = ((), (), s32[]{:S(2)}) async-start(), calls=%async_computation.25 | async-start | bytes 17301504 | tf_op jit(solution)/shard_map/reduce_scatter | solution.py:283
  910.4 11.4 all-to-all-start.5
  943.1 19.8 %all-to-all-start.7 = ((bf16[8,128,576]{1,2,0:T(8,128)(2,1)}), bf16[8,128,576]{1,2,0:T(8,128)(2,1)S(1)}, u32[]{:S(2)}, u32[]{:S(2)}) async-start(bf16[8,128,576]{1,2,0:T(8,128)(2,1)} %copy.237), calls=%async_computation.9 | async-start | bytes 2359296 | tf_op jit(solution)/shard_map/all_to_all | solution.py:83
  949.6 406.4 %all-gather.20.cloned.1.call-start = ((), (), s32[]{:S(2)}) async-start(), calls=%async_computation.26 | async-start | bytes 1327104 | tf_op jit(solution)/shard_map/all_gather | solution.py:365
  966.1 473.3 %all-gather.22.cloned.1.call-start = ((), (), s32[]{:S(2)}) async-start(), calls=%async_computation.27 | async-start | bytes 4718592 | tf_op jit(solution)/shard_map/all_gather | solution.py:324
  966.8 542.2 %reduce-scatter.3.cloned.1.call-start = ((), (), s32[]{:S(2)}) async-start(), calls=%async_computation.23 | async-start | bytes 17301504 | tf_op jit(solution)/shard_map/reduce_scatter | solution.py:288
  1027.1 45.8 %all-to-all-start.15 = ((bf16[32,64,176]{2,1,0:T(8,128)(2,1)}), bf16[32,64,176]{2,1,0:T(8,128)(2,1)S(1)}, u32[]{:S(2)}, u32[]{:S(2)}) async-start(bf16[32,64,176]{2,1,0:T(8,128)(2,1)} %bitcast.69), calls=%async_computation.17 | async-start | bytes 2097152 | tf_op jit(solution)/shard_map/all_to_all | solution.py:309
  1073.9 197.7 %all-to-all-start.16 = ((bf16[4,512,1408]{1,2,0:T(8,128)(2,1)}), bf16[4,512,1408]{1,2,0:T(8,128)(2,1)}, u32[]{:S(2)}, u32[]{:S(2)}) async-start(bf16[4,512,1408]{1,2,0:T(8,128)(2,1)} %copy.246), calls=%async_computation.18 | async-start | bytes 11534336 | tf_op jit(solution)/shard_map/all_to_all | solution.py:291
  1271.5 16.3 %all-to-all-start.12 = ((bf16[4,128,512]{2,1,0:T(8,128)(2,1)}), bf16[4,128,512]{2,1,0:T(8,128)(2,1)}, u32[]{:S(2)}, u32[]{:S(2)}) async-start(bf16[4,128,512]{2,1,0:T(8,128)(2,1)} %bitcast.260), calls=%async_computation.14 | async-start | bytes 1048576 | tf_op jit(solution)/shard_map/all_to_all | solution.py:83
  1287.8 38.2 %all-to-all-start.9 = ((bf16[4,512,384]{2,1,0:T(8,128)(2,1)}), bf16[4,512,384]{2,1,0:T(8,128)(2,1)S(1)}, u32[]{:S(2)}, u32[]{:S(2)}) async-start(bf16[4,512,384]{2,1,0:T(8,128)(2,1)} %bitcast.246), calls=%async_computation.11 | async-start | bytes 3145728 | tf_op jit(solution)/shard_map/all_to_all | solution.py:83
  1326.0 24.1 %all-to-all-start.13 = ((f32[8,16,512]{2,1,0:T(8,128)}), f32[8,16,512]{2,1,0:T(8,128)S(1)}, u32[]{:S(2)}, u32[]{:S(2)}) async-start(f32[8,16,512]{2,1,0:T(8,128)} %bitcast.64), calls=%async_computation.15 | async-start | bytes 524288 | tf_op jit(solution)/shard_map/all_to_all | solution.py:360
  1350.1 13.9 all-to-all-start.10
  1364.0 10.8 all-to-all-start.11
  1374.8 69.0 %all-to-all-start.6 = ((bf16[8,128,2048]{2,1,0:T(8,128)(2,1)}), bf16[8,128,2048]{2,1,0:T(8,128)(2,1)}, u32[]{:S(2)}, u32[]{:S(2)}) async-start(bf16[8,128,2048]{2,1,0:T(8,128)(2,1)} %bitcast.231), calls=%async_computation.8 | async-start | bytes 8388608 | tf_op jit(solution)/shard_map/all_to_all | solution.py:83
  1394.7 33.4 %collective-permute-start.2 = (bf16[352,2048]{1,0:T(8,128)(2,1)}, bf16[352,2048]{1,0:T(8,128)(2,1)}, u32[]{:S(2)}, u32[]{:S(2)}) collective-permute-start(bf16[352,2048]{1,0:T(8,128)(2,1)} %select_convert_fusion), channel_id=1, source_target_pairs={{0,8},{8,0},{16,24},{24,16},{1,9},{9,1},{17,25},{25,17},{2,10},{10... | collective-permute-start | bytes 4325384 | tf_op jit(solution)/shard_map/ppermute | solution.py:304
  1443.8 53.1 %all-to-all-start.14 = ((bf16[4,64,2048]{2,1,0:T(8,128)(2,1)}), bf16[4,64,2048]{2,1,0:T(8,128)(2,1)}, u32[]{:S(2)}, u32[]{:S(2)}) async-start(bf16[4,64,2048]{2,1,0:T(8,128)(2,1)} %bitcast.68), calls=%async_computation.16 | async-start | bytes 2097152 | tf_op jit(solution)/shard_map/all_to_all | solution.py:83
  1496.9 15.2 all-to-all-start.8
  1505.1 29.7 %collective-permute-start.1 = (f32[64,2048]{1,0:T(8,128)S(1)}, f32[64,2048]{1,0:T(8,128)}, u32[]{:S(2)}, u32[]{:S(2)}) collective-permute-start(f32[64,2048]{1,0:T(8,128)S(1)} %convert_reduce_fusion.3), channel_id=1, source_target_pairs={{0,0},{1,4},{2,8},{3,12},{4,16},{5,20},{6,24},{7,28},{8,1},{9,5},{... | collective-permute-start | bytes 1572872 | tf_op jit(solution)/shard_map/ppermute | solution.py:330
  (78 other events, 3028.6 us)
Sparse Core Ops, SparseCore 0:
  29.3 44.7 all-gather.11
  77.5 59.2 all-gather.23
  139.2 37.4 all-gather.9
  179.4 78.7 all-gather.13
  260.8 215.7 all-gather.17
  479.9 126.6 all-gather.15
  716.6 182.7 reduce-scatter.4
  966.2 26.5 all-gather.19
  994.7 36.7 all-gather.21
  1033.6 270.6 reduce-scatter.2

commit v2 on v1

--- a/solution.py
+++ b/solution.py
@@ -1,5 +1,6 @@
 import jax
 import jax.numpy as jnp
+import numpy as np
 from jax import lax
 from jax.sharding import PartitionSpec as P
 
@@ -79,9 +80,84 @@
     return rotate(grads, cosine, -sine)
 
 
-def scatter_sum(values, axis_name, parts):
-    moved = lax.all_to_all(values.astype(BF16), axis_name, split_axis=0, concat_axis=0, tiled=True)
-    return jnp.sum(moved.reshape((parts, -1) + values.shape[1:]).astype(F32), axis=0)
+def link_orders(n_seq):
+    bits = [1 << j for j in range(1, n_seq.bit_length() - 1)]
+    return bits, bits[::-1]
+
+
+def block_table(n_seq):
+    orders = link_orders(n_seq)
+    steps = len(orders[0])
+    table = np.zeros((n_seq, n_seq), np.int32)
+    for s in range(n_seq):
+        for m in range(n_seq):
+            core = (s & 1) ^ (m >> steps)
+            other = (s & ~1) | core
+            for j in range(steps):
+                if m >> j & 1:
+                    other ^= orders[core][j]
+            table[s, m] = other
+    return table
+
+
+def seq_step(values, n_seq, step):
+    orders = link_orders(n_seq)
+    return lax.ppermute(values, "seq", [(s, s ^ orders[s & 1][step]) for s in range(n_seq)])
+
+
+def core_swap(values, n_seq):
+    return lax.ppermute(values, "seq", [(s, s ^ 1) for s in range(n_seq)])
+
+
+def seq_gather(values, n_seq):
+    current = values
+    for step in range(len(link_orders(n_seq)[0])):
+        current = jnp.concatenate([current, seq_step(current, n_seq, step)], axis=0)
+    return jnp.concatenate([current, core_swap(current, n_seq)], axis=0)
+
+
+def seq_scatter(values, n_seq):
+    values = values.astype(BF16)
+    half = values.shape[0] // 2
+    total = values[:half].astype(F32) + core_swap(values[half:], n_seq).astype(F32)
+    for step in reversed(range(len(link_orders(n_seq)[0]))):
+        half = total.shape[0] // 2
+        sent = seq_step(total[half:].astype(BF16), n_seq, step)
+        total = total[:half] + sent.astype(F32)
+    return total
+
+
+def dp_swap(values, n_dp, step):
+    return lax.ppermute(values, "dp", [(d, d ^ step) for d in range(n_dp)])
+
+
+def dp_block(blocks, index):
+    return lax.dynamic_index_in_dim(blocks, index, 0, keepdims=False)
+
+
+def dp_exchange(blocks, n_dp, dp_index):
+    moved = [dp_block(blocks, dp_index)]
+    for step in range(1, n_dp):
+        moved.append(dp_swap(dp_block(blocks, dp_index ^ step), n_dp, step))
+    return in_order(moved, n_dp, dp_index)
+
+
+def in_order(moved, n_dp, dp_index):
+    return jnp.take(jnp.stack(moved), jnp.arange(n_dp, dtype=jnp.int32) ^ dp_index, axis=0)
+
+
+def dp_gather(values, n_dp, dp_index):
+    moved = [values] + [dp_swap(values, n_dp, step) for step in range(1, n_dp)]
+    return in_order(moved, n_dp, dp_index)
+
+
+def dp_scatter(values, n_dp, dp_index):
+    blocks = values.reshape((n_dp, -1) + values.shape[1:])
+    low = blocks.astype(BF16)
+    total = dp_block(blocks, dp_index).astype(F32)
+    for step in range(1, n_dp):
+        total = total + dp_swap(dp_block(low, dp_index ^ step), n_dp, step).astype(F32)
+    return total
 
 
 def body(
@@ -121,6 +197,26 @@
     down_width = kv_down.shape[1]
     q_width = heads * (NOPE + ROPE)
     e_width = heads * (NOPE + VD)
+    block_at = dp_block(jnp.asarray(block_table(n_seq)), seq_index)
+    block_of = dp_block(jnp.asarray(np.argsort(block_table(n_seq), axis=1)), seq_index)
+
+    def relative(values):
+        return jnp.take(values, block_at, axis=0)
+
+    def absolute(values):
+        return jnp.take(values, block_of, axis=0)
+
+    up_rows = kv_up.reshape(kv_up.shape[0], n_seq, -1, kv_up.shape[0] * e_width // down_rows)
+    up_rows = jnp.swapaxes(up_rows, 1, 2).reshape(down_rows, n_seq, -1)
+    joined = jnp.concatenate([q_weight.reshape(down_rows, n_seq, q_width), up_rows], axis=2)
+    joined_width = joined.shape[2]
+    joined = lax.all_to_all(joined, "seq", split_axis=1, concat_axis=0, tiled=True)
+    joined = joined.reshape(n_seq * down_rows, joined_width)
+    joined = dp_gather(joined, n_dp, dp_index).reshape(-1, joined_width)
+    weight_q = joined[:, :q_width]
+    weight_up = joined[:, q_width:].reshape(KV_RANK, e_width)
+
+    hidden_group = seq_gather(hidden, n_seq)
 
     labels = jnp.arange(experts, dtype=jnp.int32)
     hits = jnp.sum((expert_ids[:, :, None] == labels).astype(jnp.int32), axis=1)
@@ -153,18 +249,25 @@
     gain_kv = spread_tail[:, 2, first : first + kv_gain.shape[0]].reshape(-1).astype(F32)
     own_expert = per_device * seq_index + expert_bit
     routing = lax.dynamic_index_in_dim(spread_tail, own_expert, axis=1, keepdims=False)
-    routing = routing[:, :first].reshape(n_all, 4, tokens).astype(jnp.int32)
-    slot_code = (routing[:, 0] * 16 + routing[:, 1]).reshape(n_dp, group)
-    gate_of = (routing[:, 2] * 128 + routing[:, 3]).astype(F32).reshape(n_dp, group) / GATE_UNIT
-
-    q_rows = lax.all_to_all(q_weight, "seq", split_axis=1, concat_axis=0, tiled=True)
-    up_rows = lax.all_to_all(kv_up, "seq", split_axis=1, concat_axis=0, tiled=True)
-    up_shape = up_rows.shape
-    joined = jnp.concatenate([q_rows, up_rows.reshape(q_rows.shape[0], -1)], axis=1)
-    joined = lax.all_gather(joined, "dp", axis=0, tiled=True)
-    weight_q = joined[:, :q_width]
-    weight_up = joined[:, q_width:].reshape(n_dp * up_shape[0], up_shape[1])
+    routing = routing[:, :first].reshape(n_dp, n_seq, 4, tokens).astype(jnp.int32)
+    slot_code = routing[:, :, 0] * 16 + routing[:, :, 1]
+    gate_of = (routing[:, :, 2] * 128 + routing[:, :, 3]).astype(F32) / GATE_UNIT
+
     weight_out = lax.all_gather(out_weight, BOTH, axis=0, tiled=True)
+
+    ff_width = expert_gate_up.shape[2] // 2
+    ff_part = ff_width // ff_parts
+    expert_rows = expert_gate_up.shape[0]
+    in_parts = expert_gate_up.reshape(expert_rows, per_device, 2, ff_parts, ff_part)
+    in_parts = jnp.transpose(in_parts, (3, 1, 0, 2, 4)).reshape(n_dp, expert_rows, 2 * ff_part)
+    weight_in = dp_exchange(in_parts, n_dp, dp_index).reshape(-1, 2 * ff_part)
+    down_kept = lax.dynamic_index_in_dim(expert_down, expert_bit, 1, keepdims=False)
+    down_sent = lax.dynamic_index_in_dim(expert_down, 1 - expert_bit, 1, keepdims=False)
+    down_got = dp_swap(down_sent, n_dp, 1)
+    is_low = expert_bit == 0
+    weight_back = jnp.concatenate(
+        [jnp.where(is_low, down_kept, down_got), jnp.where(is_low, down_got, down_kept)], axis=0
+    )
 
     units = shared_down.shape[0]
     gate_up_parts = shared_gate_up.reshape(-1, 2, n_all, units)
@@ -173,29 +276,16 @@
         gate_up_parts, BOTH, split_axis=0, concat_axis=0, tiled=True
     ).reshape(-1, 2 * units)
 
-    ff_width = expert_gate_up.shape[2] // 2
-    ff_part = ff_width // ff_parts
-    expert_rows = expert_gate_up.shape[0]
-    in_parts = expert_gate_up.reshape(expert_rows, per_device, 2, ff_parts, ff_part)
-    in_parts = jnp.transpose(in_parts, (3, 1, 0, 2, 4)).reshape(n_dp, expert_rows, 2 * ff_part)
-    weight_in = lax.all_to_all(in_parts, "dp", split_axis=0, concat_axis=0, tiled=True)
-    weight_in = weight_in.reshape(-1, 2 * ff_part)
-    swap = [(i, i ^ 1) for i in range(n_dp)]
-    down_kept = lax.dynamic_index_in_dim(expert_down, expert_bit, 1, keepdims=False)
-    down_sent = lax.dynamic_index_in_dim(expert_down, 1 - expert_bit, 1, keepdims=False)
-    down_got = lax.ppermute(down_sent, "dp", swap)
-    is_low = expert_bit == 0
-    weight_back = jnp.concatenate(
-        [jnp.where(is_low, down_kept, down_got), jnp.where(is_low, down_got, down_kept)], axis=0
-    )
-
-    cot_all = lax.all_gather(cotangent, BOTH, axis=0, tiled=True)
-
-    hidden_group = lax.all_gather(hidden, "seq", axis=0, tiled=True)
+    def chunk_gather(values):
+        sent = [values] + [dp_swap(values, n_dp, step) for step in range(1, n_dp)]
+        return [seq_gather(piece, n_seq) for piece in sent]
+
+    cot_chunks = chunk_gather(cotangent)
+
     rows_group = hidden_group.astype(F32)
     normed_group = (rows_group * rms_scale(rows_group) * gain_attn).astype(BF16)
-    group_row = jnp.arange(group, dtype=jnp.int32)
-    positions = group_row // tokens * part + group_row % part
+    in_part = jnp.arange(tokens, dtype=jnp.int32) % part
+    positions = (block_at[:, None] * part + in_part[None, :]).reshape(group)
     cosine, sine = rotary_tables(positions)
 
     def to_sequence(values):
@@ -221,79 +311,94 @@
         jnp.concatenate([expanded[..., :NOPE], rope_key], axis=-1).astype(BF16)
     )
     values = to_sequence(expanded[..., NOPE:].astype(BF16))
+    blocks = jnp.take(block_ids.reshape(sequences, n_seq, part), block_at, axis=1)
+    blocks = blocks.reshape(sequences, length)
     score_scale = (NOPE + ROPE) ** (-0.5)
     scores = jnp.einsum("bqhd,bkhd->bhqk", queries, keys, preferred_element_type=F32) * score_scale
-    allowed = block_ids[:, None, None, :] <= block_ids[:, None, :, None]
+    allowed = blocks[:, None, None, :] <= blocks[:, None, :, None]
     scores = jnp.where(allowed, scores, -1e30)
     weights = jnp.exp(scores - jnp.max(scores, axis=-1, keepdims=True))
     probs = weights / jnp.sum(weights, axis=-1, keepdims=True)
     shares = probs.astype(BF16)
     attended = jnp.einsum("bhqk,bkhd->bqhd", shares, values, preferred_element_type=F32)
     attended = to_rows(attended.astype(BF16)).reshape(group, heads * VD)
-    heads_out = lax.all_to_all(attended, "seq", split_axis=0, concat_axis=1, tiled=True)
+    heads_out = absolute(attended.reshape(n_seq, tokens, heads * VD))
+    heads_out = lax.all_to_all(heads_out, "seq", split_axis=0, concat_axis=2, tiled=True)
+    heads_out = heads_out.reshape(tokens, H * VD)
 
     rows = hidden.astype(F32)
     residual = rows + matmul(heads_out, weight_out)
     normed_ffn = (residual * rms_scale(residual) * gain_ffn).astype(BF16)
-    ffn_all = lax.all_gather(normed_ffn, BOTH, axis=0, tiled=True)
-
-    shared_in = matmul(ffn_all, weight_shared_in)
-    shared_gate, shared_up = shared_in[:, :units], shared_in[:, units:]
-    shared_act = swiglu(shared_gate, shared_up).astype(BF16)
-    shared_act_grad = tail_dot(cot_all, shared_down)
-    grad_shared_down = lead_dot(shared_act, cot_all)
-    shared_in_grad = jnp.concatenate(
-        swiglu_back(shared_gate, shared_up, shared_act_grad), axis=1
-    ).astype(BF16)
-    grad_shared_in = lead_dot(ffn_all, shared_in_grad)
 
     slots = jnp.arange(1, capacity + 1, dtype=jnp.int32)
-    placed = (slot_code[:, :, None] == slots).astype(BF16)
-    slot_gate = jnp.sum(
-        jnp.where(slot_code[:, :, None] == slots, gate_of[:, :, None], 0.0), axis=1
-    )[..., None]
-    slot_rows = jnp.einsum(
-        "gtc,gtd->gcd", placed, ffn_all.reshape(n_dp, group, width), preferred_element_type=F32
-    ).astype(BF16)
-    slot_cot = jnp.einsum(
-        "gtc,gtd->gcd", placed, cot_all.reshape(n_dp, group, width), preferred_element_type=F32
-    )
-    slot_cot = (slot_cot * slot_gate).astype(BF16)
-    slot_rows = slot_rows.reshape(n_dp * capacity, width)
-    slot_cot = slot_cot.reshape(n_dp * capacity, width)
-    expert_in = matmul(slot_rows, weight_in)
-    expert_gate, expert_up = expert_in[:, :ff_part], expert_in[:, ff_part:]
-    expert_act = swiglu(expert_gate, expert_up).astype(BF16)
-    expert_act_grad = tail_dot(slot_cot, weight_back)
-    grad_back = lead_dot(expert_act, slot_cot)
-    expert_in_grad = jnp.concatenate(
-        swiglu_back(expert_gate, expert_up, expert_act_grad), axis=1
-    ).astype(BF16)
-    grad_in = lead_dot(slot_rows, expert_in_grad)
-    slot_grad = tail_dot(expert_in_grad, weight_in).astype(BF16)
-    expert_out = matmul(expert_act, weight_back).reshape(n_dp, capacity, width)
-    expert_out = (expert_out * slot_gate).astype(BF16)
-
-    dn_part = jnp.einsum(
-        "gtc,gcd->gtd",
-        placed,
-        slot_grad.reshape(n_dp, capacity, width),
-        preferred_element_type=F32,
-    ).reshape(n_all * tokens, width) + tail_dot(shared_in_grad, weight_shared_in)
-    ffn_grad = lax.psum_scatter(dn_part.astype(BF16), BOTH, scatter_dimension=0, tiled=True)
-    ffn_grad = ffn_grad.astype(F32)
-    out_part = jnp.einsum(
-        "gtc,gcd->gtd", placed, expert_out, preferred_element_type=F32
-    ).reshape(n_all * tokens, width) + matmul(shared_act, shared_down)
-    out_sum = lax.psum_scatter(out_part.astype(BF16), BOTH, scatter_dimension=0, tiled=True)
-    output = (residual + out_sum.astype(F32)).astype(BF16)
-
-    in_back = lax.all_to_all(
-        grad_in.astype(BF16).reshape(n_dp, expert_rows, 2 * ff_part),
-        "dp",
-        split_axis=0,
-        concat_axis=0,
-        tiled=True,
+    ffn_chunks = chunk_gather(normed_ffn)
+    ffn_grad = 0.0
+    out_chunks = []
+    grad_shared_down = 0.0
+    grad_shared_in = 0.0
+    kept_rows, kept_cots, kept_acts, kept_grads = [], [], [], []
+    for step in range(n_dp):
+        ffn_rows, cot_rows = ffn_chunks[step], cot_chunks[step]
+        codes = relative(dp_block(slot_code, dp_index ^ step)).reshape(group)
+        chunk_gate = relative(dp_block(gate_of, dp_index ^ step)).reshape(group)
+        here = codes[:, None] == slots
+        placed = here.astype(BF16)
+        slot_gate = jnp.sum(jnp.where(here, chunk_gate[:, None], 0.0), axis=0)[:, None]
+
+        shared_in = matmul(ffn_rows, weight_shared_in)
+        shared_gate, shared_up = shared_in[:, :units], shared_in[:, units:]
+        shared_act = swiglu(shared_gate, shared_up).astype(BF16)
+        shared_act_grad = tail_dot(cot_rows, shared_down)
+        shared_in_grad = jnp.concatenate(
+            swiglu_back(shared_gate, shared_up, shared_act_grad), axis=1
+        ).astype(BF16)
+        grad_shared_down = grad_shared_down + lead_dot(shared_act, cot_rows)
+        grad_shared_in = grad_shared_in + lead_dot(ffn_rows, shared_in_grad)
+
+        slot_cot = (lead_dot(placed, cot_rows) * slot_gate).astype(BF16)
+        slot_rows = lead_dot(placed, ffn_rows).astype(BF16)
+        expert_in = matmul(slot_rows, weight_in)
+        expert_gate, expert_up = expert_in[:, :ff_part], expert_in[:, ff_part:]
+        expert_act = swiglu(expert_gate, expert_up).astype(BF16)
+        expert_act_grad = tail_dot(slot_cot, weight_back)
+        expert_in_grad = jnp.concatenate(
+            swiglu_back(expert_gate, expert_up, expert_act_grad), axis=1
+        ).astype(BF16)
+        slot_grad = tail_dot(expert_in_grad, weight_in).astype(BF16)
+        dn_part = matmul(
+            jnp.concatenate([placed, shared_in_grad], axis=1),
+            jnp.concatenate([slot_grad, weight_shared_in.T], axis=0),
+        )
+        plane_sum = seq_scatter(dn_part, n_seq)
+        if step:
+            plane_sum = dp_swap(plane_sum.astype(BF16), n_dp, step).astype(F32)
+        ffn_grad = ffn_grad + plane_sum
+
+        expert_out = (matmul(expert_act, weight_back) * slot_gate).astype(BF16)
+        out_chunks.append(
+            matmul(
+                jnp.concatenate([placed, shared_act], axis=1),
+                jnp.concatenate([expert_out, shared_down], axis=0),
+            ).astype(BF16)
+        )
+        kept_rows.append(slot_rows)
+        kept_cots.append(slot_cot)
+        kept_acts.append(expert_act)
+        kept_grads.append(expert_in_grad)
+
+    grad_in = lead_dot(jnp.concatenate(kept_rows), jnp.concatenate(kept_grads))
+    grad_back = lead_dot(jnp.concatenate(kept_acts), jnp.concatenate(kept_cots))
+
+    out_sum = 0.0
+    for step in range(n_dp):
+        plane_sum = seq_scatter(out_chunks[step], n_seq)
+        if step:
+            plane_sum = dp_swap(plane_sum.astype(BF16), n_dp, step).astype(F32)
+        out_sum = out_sum + plane_sum
+    output = (residual + out_sum).astype(BF16)
+
+    in_back = dp_exchange(
+        grad_in.astype(BF16).reshape(n_dp, expert_rows, 2 * ff_part), n_dp, dp_index
     ).reshape(ff_parts, per_device, expert_rows, 2, ff_part)
     grad_expert_in = jnp.transpose(in_back, (2, 1, 3, 0, 4)).reshape(expert_gate_up.shape)
     grad_expert_in = grad_expert_in.astype(F32)
@@ -301,7 +406,7 @@
     low_half, high_half = grad_back[:half], grad_back[half:]
     grad_kept = jnp.where(is_low, low_half, high_half)
     grad_sent = jnp.where(is_low, high_half, low_half).astype(BF16)
-    grad_got = lax.ppermute(grad_sent, "dp", swap).astype(F32)
+    grad_got = dp_swap(grad_sent, n_dp, 1).astype(F32)
     grad_expert_down = jnp.stack(
         [jnp.where(is_low, grad_kept, grad_got), jnp.where(is_low, grad_got, grad_kept)], axis=1
     )
@@ -320,10 +425,12 @@
     residual_grad = cotangent.astype(F32) + from_norm
     residual_low = residual_grad.astype(BF16)
     heads_grad = tail_dot(residual_low, weight_out).astype(BF16)
+    heads_grad = heads_grad.reshape(tokens, n_seq, heads * VD)
     heads_grad = lax.all_to_all(heads_grad, "seq", split_axis=1, concat_axis=0, tiled=True)
-    residual_group = lax.all_gather(residual_low, "seq", axis=0, tiled=True)
+    heads_grad = relative(heads_grad.reshape(n_seq, tokens, heads * VD))
+    residual_group = seq_gather(residual_low, n_seq)
     grad_out_heads = lead_dot(attended, residual_group)
-    out_shard = scatter_sum(grad_out_heads, "dp", n_dp)
+    out_shard = dp_scatter(grad_out_heads, n_dp, dp_index)
     home = [
         (d * n_seq + s, s * n_dp + d) for d in range(n_dp) for s in range(n_seq)
     ]
@@ -352,21 +459,24 @@
     ).reshape(group, e_width)
 
     latent_part = tail_dot(expand_low, weight_up)
-    latent_sum = scatter_sum(jnp.concatenate([latent_part, rope_grad], axis=1), "seq", n_seq)
-    normed_sum = scatter_sum(tail_dot(query_low, weight_q), "seq", n_seq)
-    grad_q = scatter_sum(lead_dot(normed_group, query_low), "dp", n_dp)
-    grad_q = lax.all_to_all(grad_q, "seq", split_axis=0, concat_axis=1, tiled=True)
-    grad_up = scatter_sum(lead_dot(latent, expand_low), "dp", n_dp)
-    grad_up = lax.all_to_all(grad_up, "seq", split_axis=0, concat_axis=1, tiled=True)
-
-    own_latent = lax.dynamic_slice_in_dim(latent_raw, seq_index * tokens, tokens, 0)
-    latent_grad, gain_kv_grad = rms_back(own_latent, gain_kv, latent_sum[:, :KV_RANK])
+    latent_sum = seq_scatter(jnp.concatenate([latent_part, rope_grad], axis=1), n_seq)
+    normed_sum = seq_scatter(tail_dot(query_low, weight_q), n_seq)
+    grad_q = lead_dot(normed_group, query_low)
+    grad_up = lead_dot(latent, expand_low).reshape(width, -1)
+    grad_joined = dp_scatter(jnp.concatenate([grad_q, grad_up], axis=1), n_dp, dp_index)
+    grad_joined = grad_joined.reshape(n_seq, down_rows, joined_width)
+    grad_joined = lax.all_to_all(grad_joined, "seq", split_axis=0, concat_axis=0, tiled=True)
+    grad_q = jnp.swapaxes(grad_joined[..., :q_width], 0, 1).reshape(q_weight.shape)
+    grad_up = grad_joined[..., q_width:].reshape(n_seq, kv_up.shape[0], e_width)
+    grad_up = jnp.swapaxes(grad_up, 0, 1).reshape(kv_up.shape)
+
+    latent_grad, gain_kv_grad = rms_back(latent_raw[:tokens], gain_kv, latent_sum[:, :KV_RANK])
     down_low = jnp.concatenate([latent_grad, latent_sum[:, KV_RANK:]], axis=1).astype(BF16)
-    down_group = lax.all_gather(down_low, "seq", axis=0, tiled=True)
+    down_group = seq_gather(down_low, n_seq)
     normed_cols = normed_group.reshape(group, n_dp, n_seq, down_rows)
     normed_cols = lax.dynamic_index_in_dim(normed_cols, seq_index, 2, keepdims=False)
     grad_down = lead_dot(normed_cols.reshape(group, n_dp * down_rows), down_group)
-    grad_down = scatter_sum(grad_down, "dp", n_dp)
+    grad_down = dp_scatter(grad_down, n_dp, dp_index)
 
     normed_grad = normed_sum + tail_dot(down_low, weight_down)
     rows_from_norm, gain_attn_grad = rms_back(rows, gain_attn, normed_grad)

time: 1560 us -> 1440 us (0.923)
  waiting for transfers between devices: 935 us -> 572 us
  local copies, waits for them, and re-layouts: 138 us -> 313 us
  other arithmetic: 59.5 us -> 153 us
  matrix products: 279 us -> 224 us
  starting transfers between devices: 116 us -> 152 us
    ppermute x2 -> x95, waiting for transfers between devices: 186 us -> 491 us  [the longest x32 376 us: dp_swap(): return lax.ppermute(values, 'dp', [(d, d ^ step) for d in range(n_dp)])]
    all_to_all x13 -> x3, waiting for transfers between devices: 261 us -> 0.01 us  [the longest x1 0.01 us: body(): lax.all_to_all(joined, 'seq', split_axis=1, concat_axis=0, tiled=True)]
    reduce_scatter x2 -> x0, waiting for transfers between devices: 183 us -> none  [the longest x1 183 us: body(): lax.psum_scatter(dn_part.astype(BF16), BOTH, scatter_dimension=0, tiled=T...]
    all_gather x6 -> x0, waiting for transfers between devices: 163 us -> none  [the longest x1 89.7 us: body(): ffn_all = lax.all_gather(normed_ffn, BOTH, axis=0, tiled=True)]
    ppermute x2 -> x95, starting transfers between devices: 0.57 us -> 104 us  [the longest x42 48 us: seq_step(): lax.ppermute(values, 'seq', [(s, s ^ orders[s & 1][step]) for s in range(...]
    all_to_all x13 -> x3, starting transfers between devices: 85.1 us -> 14.1 us  [the longest x1 5.48 us: body(): lax.all_to_all(grad_joined, 'seq', split_axis=0, concat_axis=0, tiled=True)]
    all_gather x1, waiting for transfers between devices: 60.3 us -> 0.01 us  [body(): spread = lax.all_gather(message, BOTH, axis=0, tiled=False)]
    dot_general x4 -> x0, matrix products: 59.4 us -> none  [the longest x1 20 us: body(): jnp.einsum('gtc,gcd->gtd', placed, expert_out, preferred_element_type=F32)]
  transfers between devices with their start and end apart: 30 -> 105, of which waited for: 20 -> 35; matrix products, arithmetic and copies ran while one was open for 25% -> 45% of each run, Pallas kernels for 0% -> 0%
where the time goes in v2:
time: 1440 us; the launch traced here: 1430 us
  waiting for transfers between devices  572 us (40%)
  local copies, waits for them, and re-layouts  313 us (22%)
  matrix products  224 us (16%)
  other arithmetic  153 us (11%)
  starting transfers between devices  152 us (11%)
  between operations  17.7 us (1%)
    ppermute x32, waiting for transfers between devices, dp_swap(): return lax.ppermute(values, 'dp', [(d, d ^ step) for d in range(n_dp)])  376 us
    dot_general x62, matrix products, contract(): lax.dot_general(left_side, right_side, (((left_dim,), (right_dim,)), ((),...  201 us
    ppermute x42, waiting for transfers between devices, seq_step(): lax.ppermute(values, 'seq', [(s, s ^ orders[s & 1][step]) for s in range(...  115 us
    unnamed x504, local copies, waits for them, and re-layouts  112 us
    all_to_all x1, waiting for transfers between devices, body(): lax.all_to_all(grad_shared_in.astype(BF16).reshape(n_all, -1, 2 * units),...  49.6 us
    ppermute x42, starting transfers between devices, seq_step(): lax.ppermute(values, 'seq', [(s, s ^ orders[s & 1][step]) for s in range(...  48 us
    ppermute x32, starting transfers between devices, dp_swap(): return lax.ppermute(values, 'dp', [(d, d ^ step) for d in range(n_dp)])  38 us
  transfers between devices with their start and end apart: 105, of which 35 were waited for; matrix products, arithmetic and copies ran while one was open for 45% of the time, Pallas kernels for 0%

profile of v2, /device:TPU:25, one launch (start us, length us, event | category | flops | bytes accessed | tf_op | source)
XLA Modules:
  0.0 1432.1 jit_solution(3305973522841548783)
XLA Ops:
  33.3 15.0 %copy.340 = bf16[512,2,2816]{0,2,1:T(8,128)(2,1)} copy(bf16[512,2,2816]{2,1,0:T(2,128)(2,1)} %param.37) | data formatting | bytes 11534336 | tf_op args[11]
  54.4 11.5 constant_dynamic-slice_fusion.13
  104.7 62.1 %collective-permute-done.5 = bf16[512,512]{1,0:T(8,128)(2,1)S(1)} collective-permute-done((bf16[512,512]{1,0:T(8,128)(2,1)}, bf16[512,512]{1,0:T(8,128)(2,1)S(1)}, u32[]{:S(2)}, u32[]{:S(2)}) %collective-permute-start.5) | collective-permute-done | bytes 524320 | tf_op jit(solution)/shard_map/ppermute | solution.py:131
  166.9 9.5 collective-permute-done.4
  176.7 16.4 %collective-permute-done.3 = bf16[512,512]{1,0:T(8,128)(2,1)S(1)} collective-permute-done((bf16[512,512]{1,0:T(8,128)(2,1)}, bf16[512,512]{1,0:T(8,128)(2,1)S(1)}, u32[]{:S(2)}, u32[]{:S(2)}) %collective-permute-start.3) | collective-permute-done | bytes 524320 | tf_op jit(solution)/shard_map/ppermute | solution.py:131
  223.4 16.8 %collective-permute-done.11 = bf16[512,1408]{0,1:T(8,128)(2,1)} collective-permute-done((bf16[512,1408]{0,1:T(8,128)(2,1)}, bf16[512,1408]{0,1:T(8,128)(2,1)}, u32[]{:S(2)}, u32[]{:S(2)}) %collective-permute-start.11) | collective-permute-done | bytes 1441824 | tf_op jit(solution)/shard_map/ppermute | solution.py:131
  241.7 82.8 %collective-permute-done.10 = bf16[512,1408]{0,1:T(8,128)(2,1)} collective-permute-done((bf16[512,1408]{0,1:T(8,128)(2,1)}, bf16[512,1408]{0,1:T(8,128)(2,1)}, u32[]{:S(2)}, u32[]{:S(2)}) %collective-permute-start.10) | collective-permute-done | bytes 1441824 | tf_op jit(solution)/shard_map/ppermute | solution.py:131
  349.2 8.3 copy.342
  477.1 30.2 %collective-permute-done.24 = bf16[128,2048]{1,0:T(8,128)(2,1)S(1)} collective-permute-done((bf16[128,2048]{1,0:T(8,128)(2,1)S(1)}, bf16[128,2048]{1,0:T(8,128)(2,1)S(1)}, u32[]{:S(2)}, u32[]{:S(2)}) %collective-permute-start.24) | collective-permute-done | bytes 524320 | tf_op jit(solution)/shard_map/ppermute | solution.py:131
  518.5 8.1 collective-permute-done.17
  538.2 7.4 collective-permute-done.26
  547.2 9.4 collective-permute-done.18
  696.7 14.9 %convolution_convert_fusion = bf16[2048,1408]{1,0:T(8,128)(2,1)} fusion(bf16[384,2048]{1,0:T(8,128)(2,1)S(1)} %copy-done.207, bf16[384,2048]{1,0:T(8,128)(2,1)} %fusion.58, bf16[384,2048]{1,0:T(8,128)(2,1)} %copy-done.209, bf16[384,2048]{1,0:T(8,128)(2,1)} %copy-done.218, bf16[384,1408]{1,0:T(8,128)(2,1)S(1)} %pad_maximum_fusion.38, ...), kind=kOutput, calls=%fused_computation.24 | convolution fusion | flops 8903720960 | bytes 16384000 | tf_op jit(solution)/shard_map/dot_general | solution.py:24
  787.8 49.6 %all-to-all-done.6 = bf16[32,64,176]{2,1,0:T(8,128)(2,1)} async-done(((bf16[32,64,176]{2,1,0:T(8,128)(2,1)}), bf16[32,64,176]{2,1,0:T(8,128)(2,1)}, u32[]{:S(2)}, u32[]{:S(2)}) %all-to-all-start.6) | async-done | bytes 720928 | tf_op jit(solution)/shard_map/all_to_all | solution.py:414
  847.1 52.1 %collective-permute-done.93 = bf16[512,1408]{1,0:T(8,128)(2,1)} collective-permute-done((bf16[512,1408]{1,0:T(8,128)(2,1)}, bf16[512,1408]{1,0:T(8,128)(2,1)}, u32[]{:S(2)}, u32[]{:S(2)}) %collective-permute-start.93) | collective-permute-done | bytes 1441824 | tf_op jit(solution)/shard_map/ppermute | solution.py:131
  911.9 8.0 select_convert_fusion
  919.9 13.4 collective-permute-done.95
  943.7 12.0 copy.382
  955.6 10.0 copy.383
  965.6 18.2 %copy.384 = f32[512,2,2816]{2,1,0:T(2,128)} copy(f32[512,2,2816]{0,2,1:T(8,128)} %bitcast.381) | data formatting | bytes 23068672
  1035.1 8.3 collective-permute-done.37
  1046.3 13.9 collective-permute-done.59
  1063.2 13.7 collective-permute-done.29
  1078.6 15.2 %collective-permute-done.51 = bf16[256,2048]{1,0:T(8,128)(2,1)S(1)} collective-permute-done((bf16[256,2048]{1,0:T(8,128)(2,1)}, bf16[256,2048]{1,0:T(8,128)(2,1)S(1)}, u32[]{:S(2)}, u32[]{:S(2)}) %collective-permute-start.51) | collective-permute-done | bytes 1048608 | tf_op jit(solution)/shard_map/ppermute | solution.py:105
  1095.9 11.9 collective-permute-done.60
  1124.2 28.7 %collective-permute-done.61 = bf16[128,2048]{1,0:T(8,128)(2,1)S(1)} collective-permute-done((bf16[128,2048]{1,0:T(8,128)(2,1)S(1)}, bf16[128,2048]{1,0:T(8,128)(2,1)S(1)}, u32[]{:S(2)}, u32[]{:S(2)}) %collective-permute-start.61) | collective-permute-done | bytes 524320 | tf_op jit(solution)/shard_map/ppermute | solution.py:131
  1247.2 14.1 collective-permute-done.77
  1305.4 7.4 collective-permute-start.82
  1332.3 28.6 %collective-permute-done.89 = bf16[64,2048]{1,0:T(8,128)(2,1)S(1)} collective-permute-done((bf16[64,2048]{1,0:T(8,128)(2,1)S(1)}, bf16[64,2048]{1,0:T(8,128)(2,1)S(1)}, u32[]{:S(2)}, u32[]{:S(2)}) %collective-permute-start.89) | collective-permute-done | bytes 262176 | tf_op jit(solution)/shard_map/ppermute | solution.py:131
  1369.8 10.9 all-to-all-start.4
  1380.8 8.7 collective-permute-done.31
  1393.9 28.1 %all-to-all-done.4 = f32[32,1,144]{2,1,0:T(1,128)S(1)} async-done(((f32[32,1,144]{2,1,0:T(1,128)}), f32[32,1,144]{2,1,0:T(1,128)S(1)}, u32[]{:S(2)}, u32[]{:S(2)}) %all-to-all-start.4) | async-done | bytes 18464 | tf_op jit(solution)/shard_map/all_to_all | solution.py:493
  (1029 shorter events, 769.1 us)
Async XLA Ops:
  7.2 377.3 %all-gather.6.cloned.1.call-start = ((), (), s32[]{:S(2)}) async-start(), calls=%async_computation.8 | async-start | bytes 3379200 | tf_op jit(solution)/shard_map/all_gather | solution.py:243
  13.2 70.6 %collective-permute-start.46 = (bf16[128,2048]{1,0:T(8,128)(2,1)}, bf16[128,2048]{1,0:T(8,128)(2,1)S(1)}, u32[]{:S(2)}, u32[]{:S(2)}) collective-permute-start(bf16[128,2048]{1,0:T(8,128)(2,1)} %param.27), channel_id=1, source_target_pairs={{0,8},{8,0},{16,24},{24,16},{1,9},{9,1},{17,25},{25,17},{2,10},{10... | collective-permute-start | bytes 1572872 | tf_op jit(solution)/shard_map/ppermute | solution.py:131
  13.4 83.8 %collective-permute-start.40 = (bf16[128,2048]{1,0:T(8,128)(2,1)}, bf16[128,2048]{1,0:T(8,128)(2,1)}, u32[]{:S(2)}, u32[]{:S(2)}) collective-permute-start(bf16[128,2048]{1,0:T(8,128)(2,1)} %param.27), channel_id=1, source_target_pairs={{0,2},{1,5},{2,0},{3,7},{4,6},{5,1},{6,4},{7,3},{8,10},{9,13},{10,... | collective-permute-start | bytes 1572872 | tf_op jit(solution)/shard_map/ppermute | solution.py:105
  14.6 77.3 %collective-permute-start.62 = (bf16[128,2048]{1,0:T(8,128)(2,1)}, bf16[128,2048]{1,0:T(8,128)(2,1)}, u32[]{:S(2)}, u32[]{:S(2)}) collective-permute-start(bf16[128,2048]{1,0:T(8,128)(2,1)} %param.27), channel_id=1, source_target_pairs={{0,24},{8,16},{16,8},{24,0},{1,25},{9,17},{17,9},{25,1},{2,26},{10... | collective-permute-start | bytes 1572872 | tf_op jit(solution)/shard_map/ppermute | solution.py:131
  15.7 78.3 %collective-permute-start.54 = (bf16[128,2048]{1,0:T(8,128)(2,1)}, bf16[128,2048]{1,0:T(8,128)(2,1)}, u32[]{:S(2)}, u32[]{:S(2)}) collective-permute-start(bf16[128,2048]{1,0:T(8,128)(2,1)} %param.27), channel_id=1, source_target_pairs={{0,16},{8,24},{16,0},{24,8},{1,17},{9,25},{17,1},{25,9},{2,18},{10... | collective-permute-start | bytes 1572872 | tf_op jit(solution)/shard_map/ppermute | solution.py:131
  20.2 65.5 %all-to-all-start = ((bf16[64,8,512]{2,0,1:T(8,128)(2,1)}), bf16[64,8,512]{2,0,1:T(8,128)(2,1)S(1)}, u32[]{:S(2)}, u32[]{:S(2)}) async-start(bf16[64,8,512]{2,0,1:T(8,128)(2,1)} %copy.332), calls=%async_computation | async-start | bytes 1048576 | tf_op jit(solution)/shard_map/all_to_all | solution.py:213
  25.4 428.8 %all-gather.4.cloned.1.call-start = ((), (), s32[]{:S(2)}) async-start(), calls=%async_computation.7 | async-start | bytes 8650752 | tf_op jit(solution)/shard_map/all_gather | solution.py:256
  25.6 77.9 %collective-permute-start = (bf16[128,2048]{0,1:T(8,128)(2,1)S(1)}, bf16[128,2048]{0,1:T(8,128)(2,1)S(1)}, u32[]{:S(2)}, u32[]{:S(2)}) collective-permute-start(bf16[128,2048]{0,1:T(8,128)(2,1)S(1)} %copy.326), channel_id=1, source_target_pairs={{0,2},{1,5},{2,0},{3,7},{4,6},{5,1},{6,4},{7,3},{8,10},{9,13},{10,... | collective-permute-start | bytes 1572872 | tf_op jit(solution)/shard_map/ppermute | solution.py:105
  83.8 260.4 %collective-permute-start.12 = (bf16[352,2048]{1,0:T(8,128)(2,1)}, bf16[352,2048]{1,0:T(8,128)(2,1)}, u32[]{:S(2)}, u32[]{:S(2)}) collective-permute-start(bf16[352,2048]{1,0:T(8,128)(2,1)} %bitcast.439), channel_id=1, source_target_pairs={{0,8},{8,0},{16,24},{24,16},{1,9},{9,1},{17,25},{25,17},{2,10},{10... | collective-permute-start | bytes 4325384 | tf_op jit(solution)/shard_map/ppermute | solution.py:131
  86.5 135.7 %all-to-all-start.2 = ((bf16[32,64,176]{2,1,0:T(8,128)(2,1)}), bf16[32,64,176]{2,1,0:T(8,128)(2,1)S(1)}, u32[]{:S(2)}, u32[]{:S(2)}) async-start(bf16[32,64,176]{2,1,0:T(8,128)(2,1)} %reshape.715), calls=%async_computation.2 | async-start | bytes 2097152 | tf_op jit(solution)/shard_map/all_to_all | solution.py:275
  92.0 74.9 %collective-permute-start.5 = (bf16[512,512]{1,0:T(8,128)(2,1)}, bf16[512,512]{1,0:T(8,128)(2,1)S(1)}, u32[]{:S(2)}, u32[]{:S(2)}) collective-permute-start(bf16[512,512]{1,0:T(8,128)(2,1)} %bitcast.434), channel_id=1, source_target_pairs={{0,24},{8,16},{16,8},{24,0},{1,25},{9,17},{17,9},{25,1},{2,26},{10... | collective-permute-start | bytes 1572872 | tf_op jit(solution)/shard_map/ppermute | solution.py:131
  94.0 82.4 %collective-permute-start.4 = (bf16[512,512]{1,0:T(8,128)(2,1)}, bf16[512,512]{1,0:T(8,128)(2,1)S(1)}, u32[]{:S(2)}, u32[]{:S(2)}) collective-permute-start(bf16[512,512]{1,0:T(8,128)(2,1)} %bitcast.435), channel_id=1, source_target_pairs={{0,16},{8,24},{16,0},{24,8},{1,17},{9,25},{17,1},{25,9},{2,18},{10... | collective-permute-start | bytes 1572872 | tf_op jit(solution)/shard_map/ppermute | solution.py:131
  97.2 95.9 %collective-permute-start.3 = (bf16[512,512]{1,0:T(8,128)(2,1)}, bf16[512,512]{1,0:T(8,128)(2,1)S(1)}, u32[]{:S(2)}, u32[]{:S(2)}) collective-permute-start(bf16[512,512]{1,0:T(8,128)(2,1)} %bitcast.436), channel_id=1, source_target_pairs={{0,8},{8,0},{16,24},{24,16},{1,9},{9,1},{17,25},{25,17},{2,10},{10... | collective-permute-start | bytes 1572872 | tf_op jit(solution)/shard_map/ppermute | solution.py:131
  103.6 136.7 %collective-permute-start.11 = (bf16[512,1408]{0,1:T(8,128)(2,1)}, bf16[512,1408]{0,1:T(8,128)(2,1)}, u32[]{:S(2)}, u32[]{:S(2)}) collective-permute-start(bf16[512,1408]{0,1:T(8,128)(2,1)} %get-tuple-element.119), channel_id=1, source_target_pairs={{0,24},{8,16},{16,8},{24,0},{1,25},{9,17},{17,9},{25,1},{2,26},{10... | collective-permute-start | bytes 4325384 | tf_op jit(solution)/shard_map/ppermute | solution.py:131
  166.9 157.6 %collective-permute-start.10 = (bf16[512,1408]{0,1:T(8,128)(2,1)}, bf16[512,1408]{0,1:T(8,128)(2,1)}, u32[]{:S(2)}, u32[]{:S(2)}) collective-permute-start(bf16[512,1408]{0,1:T(8,128)(2,1)} %get-tuple-element.120), channel_id=1, source_target_pairs={{0,16},{8,24},{16,0},{24,8},{1,17},{9,25},{17,1},{25,9},{2,18},{10... | collective-permute-start | bytes 4325384 | tf_op jit(solution)/shard_map/ppermute | solution.py:131
  206.4 119.4 %collective-permute-start.9 = (bf16[512,1408]{0,1:T(8,128)(2,1)}, bf16[512,1408]{0,1:T(8,128)(2,1)}, u32[]{:S(2)}, u32[]{:S(2)}) collective-permute-start(bf16[512,1408]{0,1:T(8,128)(2,1)} %get-tuple-element.121), channel_id=1, source_target_pairs={{0,8},{8,0},{16,24},{24,16},{1,9},{9,1},{17,25},{25,17},{2,10},{10... | collective-permute-start | bytes 4325384 | tf_op jit(solution)/shard_map/ppermute | solution.py:131
  217.2 140.3 %collective-permute-start.1 = (bf16[256,2048]{0,1:T(8,128)(2,1)}, bf16[256,2048]{0,1:T(8,128)(2,1)}, u32[]{:S(2)}, u32[]{:S(2)}) collective-permute-start(bf16[256,2048]{0,1:T(8,128)(2,1)} %pad_maximum_fusion.39), channel_id=1, source_target_pairs={{0,4},{1,3},{2,6},{3,1},{4,0},{5,7},{6,2},{7,5},{8,12},{9,11},{10,... | collective-permute-start | bytes 3145736 | tf_op jit(solution)/shard_map/ppermute | solution.py:105
  240.2 120.2 %collective-permute-start.41 = (bf16[256,2048]{1,0:T(8,128)(2,1)}, bf16[256,2048]{1,0:T(8,128)(2,1)}, u32[]{:S(2)}, u32[]{:S(2)}) collective-permute-start(bf16[256,2048]{1,0:T(8,128)(2,1)} %pad_maximum_fusion.44), channel_id=1, source_target_pairs={{0,4},{1,3},{2,6},{3,1},{4,0},{5,7},{6,2},{7,5},{8,12},{9,11},{10,... | collective-permute-start | bytes 3145736 | tf_op jit(solution)/shard_map/ppermute | solution.py:105
  556.7 90.8 %collective-permute-start.19 = (bf16[512,2048]{1,0:T(8,128)(2,1)S(1)}, bf16[512,2048]{1,0:T(8,128)(2,1)}, u32[]{:S(2)}, u32[]{:S(2)}) collective-permute-start(bf16[512,2048]{1,0:T(8,128)(2,1)S(1)} %pad_maximum_fusion.22), channel_id=1, source_target_pairs={{0,1},{1,0},{2,3},{3,2},{4,5},{5,4},{6,7},{7,6},{8,9},{9,8},{10,11... | collective-permute-start | bytes 6291464 | tf_op jit(solution)/shard_map/ppermute | solution.py:109
  593.2 390.7 %collective-permute-start.43 = (bf16[512,2048]{1,0:T(8,128)(2,1)}, bf16[512,2048]{1,0:T(8,128)(2,1)}, u32[]{:S(2)}, u32[]{:S(2)}) collective-permute-start(bf16[512,2048]{1,0:T(8,128)(2,1)} %slice.583), channel_id=1, source_target_pairs={{0,1},{1,0},{2,3},{3,2},{4,5},{5,4},{6,7},{7,6},{8,9},{9,8},{10,11... | collective-permute-start | bytes 6291464 | tf_op jit(solution)/shard_map/ppermute | solution.py:109
  593.7 393.5 %collective-permute-start.13 = (bf16[512,2048]{1,0:T(8,128)(2,1)}, bf16[512,2048]{1,0:T(8,128)(2,1)}, u32[]{:S(2)}, u32[]{:S(2)}) collective-permute-start(bf16[512,2048]{1,0:T(8,128)(2,1)} %slice.547), channel_id=1, source_target_pairs={{0,1},{1,0},{2,3},{3,2},{4,5},{5,4},{6,7},{7,6},{8,9},{9,8},{10,11... | collective-permute-start | bytes 6291464 | tf_op jit(solution)/shard_map/ppermute | solution.py:109
  746.4 91.0 %all-to-all-start.6 = ((bf16[32,64,176]{2,1,0:T(8,128)(2,1)}), bf16[32,64,176]{2,1,0:T(8,128)(2,1)}, u32[]{:S(2)}, u32[]{:S(2)}) async-start(bf16[32,64,176]{2,1,0:T(8,128)(2,1)} %bitcast.122), calls=%async_computation.6 | async-start | bytes 2097152 | tf_op jit(solution)/shard_map/all_to_all | solution.py:414
  757.4 88.9 %collective-permute-start.94 = (bf16[512,1408]{1,0:T(8,128)(2,1)}, bf16[512,1408]{1,0:T(8,128)(2,1)}, u32[]{:S(2)}, u32[]{:S(2)}) collective-permute-start(bf16[512,1408]{1,0:T(8,128)(2,1)} %get-tuple-element.115), channel_id=1, source_target_pairs={{0,24},{8,16},{16,8},{24,0},{1,25},{9,17},{17,9},{25,1},{2,26},{10... | collective-permute-start | bytes 4325384 | tf_op jit(solution)/shard_map/ppermute | solution.py:131
  757.4 141.8 %collective-permute-start.93 = (bf16[512,1408]{1,0:T(8,128)(2,1)}, bf16[512,1408]{1,0:T(8,128)(2,1)}, u32[]{:S(2)}, u32[]{:S(2)}) collective-permute-start(bf16[512,1408]{1,0:T(8,128)(2,1)} %get-tuple-element.116), channel_id=1, source_target_pairs={{0,16},{8,24},{16,0},{24,8},{1,17},{9,25},{17,1},{25,9},{2,18},{10... | collective-permute-start | bytes 4325384 | tf_op jit(solution)/shard_map/ppermute | solution.py:131
  758.8 141.0 %collective-permute-start.92 = (bf16[512,1408]{1,0:T(8,128)(2,1)}, bf16[512,1408]{1,0:T(8,128)(2,1)}, u32[]{:S(2)}, u32[]{:S(2)}) collective-permute-start(bf16[512,1408]{1,0:T(8,128)(2,1)} %get-tuple-element.117), channel_id=1, source_target_pairs={{0,8},{8,0},{16,24},{24,16},{1,9},{9,1},{17,25},{25,17},{2,10},{10... | collective-permute-start | bytes 4325384 | tf_op jit(solution)/shard_map/ppermute | solution.py:131
  846.3 146.5 %collective-permute-start.66 = (bf16[512,2048]{1,0:T(8,128)(2,1)}, bf16[512,2048]{1,0:T(8,128)(2,1)}, u32[]{:S(2)}, u32[]{:S(2)}) collective-permute-start(bf16[512,2048]{1,0:T(8,128)(2,1)} %slice.601), channel_id=1, source_target_pairs={{0,1},{1,0},{2,3},{3,2},{4,5},{5,4},{6,7},{7,6},{8,9},{9,8},{10,11... | collective-permute-start | bytes 6291464 | tf_op jit(solution)/shard_map/ppermute | solution.py:109
  899.2 96.1 %collective-permute-start.36 = (bf16[512,2048]{1,0:T(8,128)(2,1)}, bf16[512,2048]{1,0:T(8,128)(2,1)}, u32[]{:S(2)}, u32[]{:S(2)}) collective-permute-start(bf16[512,2048]{1,0:T(8,128)(2,1)} %slice.577), channel_id=1, source_target_pairs={{0,1},{1,0},{2,3},{3,2},{4,5},{5,4},{6,7},{7,6},{8,9},{9,8},{10,11... | collective-permute-start | bytes 6291464 | tf_op jit(solution)/shard_map/ppermute | solution.py:109
  933.3 68.2 %collective-permute-start.58 = (bf16[512,2048]{1,0:T(8,128)(2,1)}, bf16[512,2048]{1,0:T(8,128)(2,1)}, u32[]{:S(2)}, u32[]{:S(2)}) collective-permute-start(bf16[512,2048]{1,0:T(8,128)(2,1)} %slice.595), channel_id=1, source_target_pairs={{0,1},{1,0},{2,3},{3,2},{4,5},{5,4},{6,7},{7,6},{8,9},{9,8},{10,11... | collective-permute-start | bytes 6291464 | tf_op jit(solution)/shard_map/ppermute | solution.py:109
  1020.9 72.9 %collective-permute-start.51 = (bf16[256,2048]{1,0:T(8,128)(2,1)}, bf16[256,2048]{1,0:T(8,128)(2,1)S(1)}, u32[]{:S(2)}, u32[]{:S(2)}) collective-permute-start(bf16[256,2048]{1,0:T(8,128)(2,1)} %slice.864), channel_id=1, source_target_pairs={{0,4},{1,3},{2,6},{3,1},{4,0},{5,7},{6,2},{7,5},{8,12},{9,11},{10,... | collective-permute-start | bytes 3145736 | tf_op jit(solution)/shard_map/ppermute | solution.py:105
  1032.1 86.1 %collective-permute-start.21 = (bf16[256,2048]{1,0:T(8,128)(2,1)}, bf16[256,2048]{1,0:T(8,128)(2,1)S(1)}, u32[]{:S(2)}, u32[]{:S(2)}) collective-permute-start(bf16[256,2048]{1,0:T(8,128)(2,1)} %slice.868), channel_id=1, source_target_pairs={{0,4},{1,3},{2,6},{3,1},{4,0},{5,7},{6,2},{7,5},{8,12},{9,11},{10,... | collective-permute-start | bytes 3145736 | tf_op jit(solution)/shard_map/ppermute | solution.py:105
  1043.4 80.9 %collective-permute-start.45 = (bf16[128,2048]{1,0:T(8,128)(2,1)S(1)}, bf16[128,2048]{1,0:T(8,128)(2,1)S(1)}, u32[]{:S(2)}, u32[]{:S(2)}) collective-permute-start(bf16[128,2048]{1,0:T(8,128)(2,1)S(1)} %slice.874), channel_id=1, source_target_pairs={{0,2},{1,5},{2,0},{3,7},{4,6},{5,1},{6,4},{7,3},{8,10},{9,13},{10,... | collective-permute-start | bytes 1572872 | tf_op jit(solution)/shard_map/ppermute | solution.py:105
  1167.5 74.6 %collective-permute-start.85 = (bf16[128,2048]{1,0:T(8,128)(2,1)S(1)}, bf16[128,2048]{1,0:T(8,128)(2,1)}, u32[]{:S(2)}, u32[]{:S(2)}) collective-permute-start(bf16[128,2048]{1,0:T(8,128)(2,1)S(1)} %fusion.304), channel_id=1, source_target_pairs={{0,2},{1,5},{2,0},{3,7},{4,6},{5,1},{6,4},{7,3},{8,10},{9,13},{10,... | collective-permute-start | bytes 1572872 | tf_op jit(solution)/shard_map/ppermute | solution.py:105
  (308 other events, 7070.1 us)
Sparse Core Ops, SparseCore 0:
  13.3 83.2 all-gather.5
  99.4 185.5 all-gather.3

commit v3 on v2

--- a/solution.py
+++ b/solution.py
@@ -2,6 +2,8 @@
 import jax.numpy as jnp
 import numpy as np
 from jax import lax
+from jax.experimental import pallas as pl
+from jax.experimental.pallas import tpu as pltpu
 from jax.sharding import PartitionSpec as P
 
 H = 16
@@ -117,14 +119,21 @@
 
 
 def seq_scatter(values, n_seq):
+    stages = []
+    half = values.shape[0] // 2
     values = values.astype(BF16)
-    half = values.shape[0] // 2
     total = values[:half].astype(F32) + core_swap(values[half:], n_seq).astype(F32)
+    stages.append(total)
     for step in reversed(range(len(link_orders(n_seq)[0]))):
         half = total.shape[0] // 2
         sent = seq_step(total[half:].astype(BF16), n_seq, step)
         total = total[:half] + sent.astype(F32)
-    return total
+        stages.append(total)
+    return stages
+
+
+def hold(value, *until):
+    return lax.optimization_barrier((value,) + until)[0]
 
 
 def dp_swap(values, n_dp, step):
@@ -139,11 +148,14 @@
     moved = [dp_block(blocks, dp_index)]
     for step in range(1, n_dp):
         moved.append(dp_swap(dp_block(blocks, dp_index ^ step), n_dp, step))
-    return in_order(moved, n_dp, dp_index)
+    return moved
 
 
 def in_order(moved, n_dp, dp_index):
-    return jnp.take(jnp.stack(moved), jnp.arange(n_dp, dtype=jnp.int32) ^ dp_index, axis=0)
+    result = jnp.zeros((n_dp,) + moved[0].shape, moved[0].dtype)
+    for step in range(n_dp):
+        result = lax.dynamic_update_index_in_dim(result, moved[step], dp_index ^ step, 0)
+    return result
 
 
 def dp_gather(values, n_dp, dp_index):
@@ -158,6 +170,41 @@
     for step in range(1, n_dp):
         total = total + dp_swap(dp_block(low, dp_index ^ step), n_dp, step).astype(F32)
     return total
+
+
+def assemble_kernel(index_ref, *refs):
+    pieces, out_ref = refs[:-1], refs[-1]
+    count = len(pieces)
+    per_device = out_ref.shape[1]
+    part = pieces[0].shape[1] // 2
+    values = [piece[...].astype(F32) for piece in pieces]
+    for expert in range(per_device):
+        gates, ups = [], []
+        for ff in range(count // per_device):
+            step = index_ref[0] ^ (ff * per_device + expert)
+            chosen = values[0]
+            for j in range(1, count):
+                chosen = jnp.where(step == j, values[j], chosen)
+            gates.append(chosen[:, :part])
+            ups.append(chosen[:, part:])
+        out_ref[:, expert, :] = jnp.concatenate(gates + ups, axis=1)
+
+
+def assemble(pieces, dp_index, out_shape):
+    rows, piece_width = pieces[0].shape
+    step_rows = 64
+    return pl.pallas_call(
+        assemble_kernel,
+        out_shape=jax.ShapeDtypeStruct(out_shape, F32),
+        grid_spec=pltpu.PrefetchScalarGridSpec(
+            num_scalar_prefetch=1,
+            grid=(rows // step_rows,),
+            in_specs=[pl.BlockSpec((step_rows, piece_width), lambda i, index: (i, 0))] * len(pieces),
+            out_specs=pl.BlockSpec((step_rows,) + out_shape[1:], lambda i, index: (i, 0, 0)),
+        ),
+        compiler_params=pltpu.CompilerParams(vmem_limit_bytes=48 * 2**20),
+        name="assemble",
+    )(jnp.reshape(dp_index, (1,)).astype(jnp.int32), *pieces)
 
 
 def body(
@@ -201,10 +248,10 @@
     block_of = dp_block(jnp.asarray(np.argsort(block_table(n_seq), axis=1)), seq_index)
 
     def relative(values):
-        return jnp.take(values, block_at, axis=0)
+        return jnp.take(values, block_at, axis=0, mode="clip")
 
     def absolute(values):
-        return jnp.take(values, block_of, axis=0)
+        return jnp.take(values, block_of, axis=0, mode="clip")
 
     up_rows = kv_up.reshape(kv_up.shape[0], n_seq, -1, kv_up.shape[0] * e_width // down_rows)
     up_rows = jnp.swapaxes(up_rows, 1, 2).reshape(down_rows, n_seq, -1)
@@ -253,25 +300,24 @@
     slot_code = routing[:, :, 0] * 16 + routing[:, :, 1]
     gate_of = (routing[:, :, 2] * 128 + routing[:, :, 3]).astype(F32) / GATE_UNIT
 
-    weight_out = lax.all_gather(out_weight, BOTH, axis=0, tiled=True)
+    weight_out = lax.all_gather(hold(out_weight, spread), BOTH, axis=0, tiled=True)
+    cot_all = lax.all_gather(hold(cotangent, weight_out), BOTH, axis=0, tiled=True)
 
     ff_width = expert_gate_up.shape[2] // 2
     ff_part = ff_width // ff_parts
     expert_rows = expert_gate_up.shape[0]
     in_parts = expert_gate_up.reshape(expert_rows, per_device, 2, ff_parts, ff_part)
     in_parts = jnp.transpose(in_parts, (3, 1, 0, 2, 4)).reshape(n_dp, expert_rows, 2 * ff_part)
-    weight_in = dp_exchange(in_parts, n_dp, dp_index).reshape(-1, 2 * ff_part)
+    in_moved = dp_exchange(hold(in_parts, joined), n_dp, dp_index)
     down_kept = lax.dynamic_index_in_dim(expert_down, expert_bit, 1, keepdims=False)
     down_sent = lax.dynamic_index_in_dim(expert_down, 1 - expert_bit, 1, keepdims=False)
-    down_got = dp_swap(down_sent, n_dp, 1)
+    down_got = dp_swap(hold(down_sent, joined), n_dp, 1)
     is_low = expert_bit == 0
-    weight_back = jnp.concatenate(
-        [jnp.where(is_low, down_kept, down_got), jnp.where(is_low, down_got, down_kept)], axis=0
-    )
 
     units = shared_down.shape[0]
     gate_up_parts = shared_gate_up.reshape(-1, 2, n_all, units)
     gate_up_parts = jnp.transpose(gate_up_parts, (2, 0, 1, 3)).reshape(n_all, -1, 2 * units)
+    gate_up_parts = hold(gate_up_parts, joined)
     weight_shared_in = lax.all_to_all(
         gate_up_parts, BOTH, split_axis=0, concat_axis=0, tiled=True
     ).reshape(-1, 2 * units)
@@ -279,8 +325,6 @@
     def chunk_gather(values):
         sent = [values] + [dp_swap(values, n_dp, step) for step in range(1, n_dp)]
         return [seq_gather(piece, n_seq) for piece in sent]
-
-    cot_chunks = chunk_gather(cotangent)
 
     rows_group = hidden_group.astype(F32)
     normed_group = (rows_group * rms_scale(rows_group) * gain_attn).astype(BF16)
@@ -311,7 +355,7 @@
         jnp.concatenate([expanded[..., :NOPE], rope_key], axis=-1).astype(BF16)
     )
     values = to_sequence(expanded[..., NOPE:].astype(BF16))
-    blocks = jnp.take(block_ids.reshape(sequences, n_seq, part), block_at, axis=1)
+    blocks = jnp.take(block_ids.reshape(sequences, n_seq, part), block_at, axis=1, mode="clip")
     blocks = blocks.reshape(sequences, length)
     score_scale = (NOPE + ROPE) ** (-0.5)
     scores = jnp.einsum("bqhd,bkhd->bhqk", queries, keys, preferred_element_type=F32) * score_scale
@@ -331,95 +375,99 @@
     normed_ffn = (residual * rms_scale(residual) * gain_ffn).astype(BF16)
 
     slots = jnp.arange(1, capacity + 1, dtype=jnp.int32)
+    all_codes = slot_code.reshape(n_dp, group)
+    all_here = all_codes[:, :, None] == slots
+    slot_gate = jnp.where(all_here, gate_of.reshape(n_dp, group)[:, :, None], 0.0)
+    slot_gate = jnp.sum(slot_gate, axis=1)[:, :, None]
+    all_placed = lax.optimization_barrier(all_here.astype(BF16))
+    cot_rows = cot_all.reshape(n_dp, group, width)
+    slot_cot = jnp.einsum("gtc,gtd->gcd", all_placed, cot_rows, preferred_element_type=F32)
+    slot_cot = (slot_cot * slot_gate).astype(BF16)
+    down_kept, down_got = hold((down_kept, down_got), normed_ffn)
+    weight_back = jnp.concatenate(
+        [jnp.where(is_low, down_kept, down_got), jnp.where(is_low, down_got, down_kept)], axis=0
+    )
+    expert_act_grad = contract(slot_cot, weight_back, 2, 1)
+    shared_act_grad = contract(cot_rows, shared_down, 2, 1)
+
+    in_moved = hold(in_moved, normed_ffn)
+    weight_in = in_order(in_moved, n_dp, dp_index).reshape(-1, 2 * ff_part)
     ffn_chunks = chunk_gather(normed_ffn)
-    ffn_grad = 0.0
-    out_chunks = []
-    grad_shared_down = 0.0
+    shared_in_back = weight_shared_in.T
     grad_shared_in = 0.0
-    kept_rows, kept_cots, kept_acts, kept_grads = [], [], [], []
+    kept_rows, kept_acts, kept_grads = [], [], []
+    kept_shared, shared_acts, planes = [], [], []
+    dn_part = None
     for step in range(n_dp):
-        ffn_rows, cot_rows = ffn_chunks[step], cot_chunks[step]
+        ffn_rows = ffn_chunks[step]
         codes = relative(dp_block(slot_code, dp_index ^ step)).reshape(group)
-        chunk_gate = relative(dp_block(gate_of, dp_index ^ step)).reshape(group)
-        here = codes[:, None] == slots
-        placed = here.astype(BF16)
-        slot_gate = jnp.sum(jnp.where(here, chunk_gate[:, None], 0.0), axis=0)[:, None]
+        placed = lax.optimization_barrier((codes[:, None] == slots).astype(BF16))
 
         shared_in = matmul(ffn_rows, weight_shared_in)
         shared_gate, shared_up = shared_in[:, :units], shared_in[:, units:]
-        shared_act = swiglu(shared_gate, shared_up).astype(BF16)
-        shared_act_grad = tail_dot(cot_rows, shared_down)
+        act_grad = dp_block(shared_act_grad, dp_index ^ step)
+        act_grad = relative(act_grad.reshape(n_seq, tokens, units)).reshape(group, units)
         shared_in_grad = jnp.concatenate(
-            swiglu_back(shared_gate, shared_up, shared_act_grad), axis=1
+            swiglu_back(shared_gate, shared_up, act_grad), axis=1
         ).astype(BF16)
-        grad_shared_down = grad_shared_down + lead_dot(shared_act, cot_rows)
-        grad_shared_in = grad_shared_in + lead_dot(ffn_rows, shared_in_grad)
-
-        slot_cot = (lead_dot(placed, cot_rows) * slot_gate).astype(BF16)
+        kept_shared.append(shared_in_grad)
+        shared_acts.append(swiglu(shared_gate, shared_up).astype(BF16))
+
         slot_rows = lead_dot(placed, ffn_rows).astype(BF16)
         expert_in = matmul(slot_rows, weight_in)
         expert_gate, expert_up = expert_in[:, :ff_part], expert_in[:, ff_part:]
-        expert_act = swiglu(expert_gate, expert_up).astype(BF16)
-        expert_act_grad = tail_dot(slot_cot, weight_back)
         expert_in_grad = jnp.concatenate(
-            swiglu_back(expert_gate, expert_up, expert_act_grad), axis=1
+            swiglu_back(expert_gate, expert_up, dp_block(expert_act_grad, dp_index ^ step)), axis=1
         ).astype(BF16)
         slot_grad = tail_dot(expert_in_grad, weight_in).astype(BF16)
+        for age in range(1, min(step, 3) + 1):
+            placed = hold(placed, planes[step - age][age - 1])
         dn_part = matmul(
             jnp.concatenate([placed, shared_in_grad], axis=1),
-            jnp.concatenate([slot_grad, weight_shared_in.T], axis=0),
-        )
-        plane_sum = seq_scatter(dn_part, n_seq)
-        if step:
-            plane_sum = dp_swap(plane_sum.astype(BF16), n_dp, step).astype(F32)
-        ffn_grad = ffn_grad + plane_sum
-
-        expert_out = (matmul(expert_act, weight_back) * slot_gate).astype(BF16)
-        out_chunks.append(
-            matmul(
-                jnp.concatenate([placed, shared_act], axis=1),
-                jnp.concatenate([expert_out, shared_down], axis=0),
-            ).astype(BF16)
-        )
+            jnp.concatenate([slot_grad, shared_in_back], axis=0),
+        ).astype(BF16)
+        planes.append(seq_scatter(dn_part, n_seq))
+
         kept_rows.append(slot_rows)
-        kept_cots.append(slot_cot)
-        kept_acts.append(expert_act)
+        kept_acts.append(swiglu(expert_gate, expert_up).astype(BF16))
         kept_grads.append(expert_in_grad)
-
-    grad_in = lead_dot(jnp.concatenate(kept_rows), jnp.concatenate(kept_grads))
-    grad_back = lead_dot(jnp.concatenate(kept_acts), jnp.concatenate(kept_cots))
-
-    out_sum = 0.0
-    for step in range(n_dp):
-        plane_sum = seq_scatter(out_chunks[step], n_seq)
-        if step:
-            plane_sum = dp_swap(plane_sum.astype(BF16), n_dp, step).astype(F32)
-        out_sum = out_sum + plane_sum
-    output = (residual + out_sum).astype(BF16)
-
-    in_back = dp_exchange(
-        grad_in.astype(BF16).reshape(n_dp, expert_rows, 2 * ff_part), n_dp, dp_index
-    ).reshape(ff_parts, per_device, expert_rows, 2, ff_part)
-    grad_expert_in = jnp.transpose(in_back, (2, 1, 3, 0, 4)).reshape(expert_gate_up.shape)
-    grad_expert_in = grad_expert_in.astype(F32)
+    ffn_grad = planes[0][-1]
+    for step in range(1, n_dp):
+        ffn_grad = ffn_grad + dp_swap(planes[step][-1].astype(BF16), n_dp, step).astype(F32)
+
+    kept_rows, kept_acts, kept_grads, shared_acts, ffn_chunks = hold(
+        (kept_rows, kept_acts, kept_grads, shared_acts, ffn_chunks), dn_part
+    )
+    grad_in = lead_dot(jnp.concatenate(kept_rows), jnp.concatenate(kept_grads)).astype(BF16)
+    in_back = dp_exchange(grad_in.reshape(n_dp, expert_rows, 2 * ff_part), n_dp, dp_index)
+    expert_act = in_order(kept_acts, n_dp, dp_index)
+    grad_back = lead_dot(
+        expert_act.reshape(n_dp * capacity, ff_part), slot_cot.reshape(n_dp * capacity, width)
+    )
     half = expert_down.shape[0]
     low_half, high_half = grad_back[:half], grad_back[half:]
     grad_kept = jnp.where(is_low, low_half, high_half)
     grad_sent = jnp.where(is_low, high_half, low_half).astype(BF16)
-    grad_got = dp_swap(grad_sent, n_dp, 1).astype(F32)
-    grad_expert_down = jnp.stack(
-        [jnp.where(is_low, grad_kept, grad_got), jnp.where(is_low, grad_got, grad_kept)], axis=1
-    )
-
-    shared_back = lax.all_to_all(
-        grad_shared_in.astype(BF16).reshape(n_all, -1, 2 * units),
-        BOTH,
-        split_axis=0,
-        concat_axis=0,
-        tiled=True,
-    ).reshape(n_all, -1, 2, units)
-    grad_shared_gate_up = jnp.transpose(shared_back, (1, 2, 0, 3)).reshape(shared_gate_up.shape)
-    grad_shared_gate_up = grad_shared_gate_up.astype(F32)
+    grad_got = dp_swap(grad_sent, n_dp, 1)
+    shared_act = in_order(
+        [absolute(act.reshape(n_seq, tokens, units)) for act in shared_acts], n_dp, dp_index
+    ).reshape(n_dp, group, units)
+    expert_out = (contract(expert_act, weight_back, 2, 0) * slot_gate).astype(BF16)
+    out_part = jnp.einsum(
+        "gtk,gkd->gtd",
+        jnp.concatenate([all_placed, shared_act], axis=2),
+        jnp.concatenate(
+            [expert_out, jnp.broadcast_to(shared_down, (n_dp, units, width))], axis=1
+        ),
+        preferred_element_type=F32,
+    ).astype(BF16)
+    out_sum = lax.psum_scatter(
+        out_part.reshape(n_all * tokens, width), BOTH, scatter_dimension=0, tiled=True
+    )
+    output = (residual + out_sum.astype(F32)).astype(BF16)
+    grad_shared_down = lead_dot(shared_act.reshape(n_all * tokens, units), cot_all)
+    for step in range(n_dp):
+        grad_shared_in = grad_shared_in + lead_dot(ffn_chunks[step], kept_shared[step])
 
     from_norm, gain_ffn_grad = rms_back(residual, gain_ffn, ffn_grad)
     residual_grad = cotangent.astype(F32) + from_norm
@@ -427,8 +475,12 @@
     heads_grad = tail_dot(residual_low, weight_out).astype(BF16)
     heads_grad = heads_grad.reshape(tokens, n_seq, heads * VD)
     heads_grad = lax.all_to_all(heads_grad, "seq", split_axis=1, concat_axis=0, tiled=True)
+    residual_group = seq_gather(hold(residual_low, heads_grad), n_seq)
+    grad_shared_in = hold(grad_shared_in.astype(BF16), heads_grad)
+    shared_back = lax.all_to_all(
+        grad_shared_in.reshape(n_all, -1, 2 * units), BOTH, split_axis=0, concat_axis=0, tiled=True
+    )
     heads_grad = relative(heads_grad.reshape(n_seq, tokens, heads * VD))
-    residual_group = seq_gather(residual_low, n_seq)
     grad_out_heads = lead_dot(attended, residual_group)
     out_shard = dp_scatter(grad_out_heads, n_dp, dp_index)
     home = [
@@ -459,8 +511,8 @@
     ).reshape(group, e_width)
 
     latent_part = tail_dot(expand_low, weight_up)
-    latent_sum = seq_scatter(jnp.concatenate([latent_part, rope_grad], axis=1), n_seq)
-    normed_sum = seq_scatter(tail_dot(query_low, weight_q), n_seq)
+    latent_sum = seq_scatter(jnp.concatenate([latent_part, rope_grad], axis=1), n_seq)[-1]
+    normed_sum = seq_scatter(tail_dot(query_low, weight_q), n_seq)[-1]
     grad_q = lead_dot(normed_group, query_low)
     grad_up = lead_dot(latent, expand_low).reshape(width, -1)
     grad_joined = dp_scatter(jnp.concatenate([grad_q, grad_up], axis=1), n_dp, dp_index)
@@ -477,6 +529,15 @@
     normed_cols = lax.dynamic_index_in_dim(normed_cols, seq_index, 2, keepdims=False)
     grad_down = lead_dot(normed_cols.reshape(group, n_dp * down_rows), down_group)
     grad_down = dp_scatter(grad_down, n_dp, dp_index)
+
+    in_back, grad_got, shared_back = hold((in_back, grad_got, shared_back), down_low)
+    grad_expert_in = assemble(in_back, dp_index, expert_gate_up.shape)
+    grad_got = grad_got.astype(F32)
+    grad_expert_down = jnp.stack(
+        [jnp.where(is_low, grad_kept, grad_got), jnp.where(is_low, grad_got, grad_kept)], axis=1
+    )
+    shared_back = shared_back.reshape(n_all, -1, 2, units).astype(F32)
+    grad_shared_gate_up = jnp.transpose(shared_back, (1, 2, 0, 3)).reshape(shared_gate_up.shape)
 
     normed_grad = normed_sum + tail_dot(down_low, weight_down)
     rows_from_norm, gain_attn_grad = rms_back(rows, gain_attn, normed_grad)

time: 1440 us -> 1420 us (0.986)
  local copies, waits for them, and re-layouts: 313 us -> 245 us
  waiting for transfers between devices: 572 us -> 630 us
  other arithmetic: 153 us -> 124 us
  starting transfers between devices: 152 us -> 167 us
    all_gather x1 -> x2, waiting for transfers between devices: 0.02 us -> 78.8 us  [the longest x1 78.8 us: body(): lax.all_gather(hold(out_weight, spread), BOTH, axis=0, tiled=True)]
    all_gather x1, waiting for transfers between devices: 0.01 us -> 59.6 us  [body(): spread = lax.all_gather(message, BOTH, axis=0, tiled=False)]
    all_to_all x1, waiting for transfers between devices: 49.6 us -> 0.01 us  [body(): lax.all_to_all(grad_shared_in.reshape(n_all, -1, 2 * units), BOTH, split_...]
    unnamed x504 -> x415, local copies, waits for them, and re-layouts: 112 us -> 62.8 us
    dot_general x62 -> x42, matrix products: 201 us -> 155 us  [contract(): lax.dot_general(left_side, right_side, (((left_dim,), (right_dim,)), ((),...]
    ppermute x32 -> x26, waiting for transfers between devices: 376 us -> 331 us  [dp_swap(): return lax.ppermute(values, 'dp', [(d, d ^ step) for d in range(n_dp)])]
    convert_element_type x10 -> x0, local copies, waits for them, and re-layouts: 37.3 us -> none  [the longest x2 22 us: body(): grad_expert_in = grad_expert_in.astype(F32)]
    dot_general x0 -> x2, matrix products: none -> 30.2 us  [the longest x1 15.2 us: body(): jnp.einsum('gtk,gkd->gtd', jnp.concatenate([all_placed, shared_act], axis...]
  transfers between devices with their start and end apart: 105 -> 77, of which waited for: 35 -> 29; matrix products, arithmetic and copies ran while one was open for 45% -> 30% of each run, Pallas kernels for 0% -> 1%
where the time goes in v3:
time: 1420 us; the launch traced here: 1400 us
  waiting for transfers between devices  630 us (44%)
  local copies, waits for them, and re-layouts  245 us (17%)
  matrix products  211 us (15%)
  starting transfers between devices  167 us (12%)
  other arithmetic  124 us (9%)
  between operations  17.4 us (1%)
    ppermute x26, waiting for transfers between devices, dp_swap(): return lax.ppermute(values, 'dp', [(d, d ^ step) for d in range(n_dp)])  331 us
    dot_general x42, matrix products, contract(): lax.dot_general(left_side, right_side, (((left_dim,), (right_dim,)), ((),...  155 us
    ppermute x26, waiting for transfers between devices, seq_step(): lax.ppermute(values, 'seq', [(s, s ^ orders[s & 1][step]) for s in range(...  126 us
    all_gather x1, waiting for transfers between devices, body(): lax.all_gather(hold(out_weight, spread), BOTH, axis=0, tiled=True)  78.8 us
    unnamed x415, local copies, waits for them, and re-layouts  62.8 us
    all_gather x1, waiting for transfers between devices, body(): spread = lax.all_gather(message, BOTH, axis=0, tiled=False)  59.6 us
    ppermute x26, starting transfers between devices, dp_swap(): return lax.ppermute(values, 'dp', [(d, d ^ step) for d in range(n_dp)])  45.8 us
    dynamic_slice x15, local copies, waits for them, and re-layouts, dp_block(): return lax.dynamic_index_in_dim(blocks, index, 0, keepdims=False)  37.1 us
  transfers between devices with their start and end apart: 77, of which 29 were waited for; matrix products, arithmetic and copies ran while one was open for 30% of the time, Pallas kernels for 1%

profile of v3, /device:TPU:25, one launch (start us, length us, event | category | flops | bytes accessed | tf_op | source)
XLA Modules:
  0.0 1404.6 jit_solution(6856646968340531097)
XLA Ops:
  13.2 59.6 %all-gather.9.cloned.1.call-done = bf16[2560,576]{1,0:T(8,128)(2,1)} async-done(((bf16[80,576]{1,0:T(8,128)(2,1)}), bf16[2560,576]{1,0:T(8,128)(2,1)}) %all-gather.9.cloned.1.call-update) | async-done | bytes 2949136 | tf_op jit(solution)/shard_map/all_gather | solution.py:290
  72.9 78.8 %all-gather.5.cloned.1.call-done = bf16[2048,2048]{1,0:T(8,128)(2,1)} async-done(((bf16[64,2048]{1,0:T(8,128)(2,1)}), bf16[2048,2048]{1,0:T(8,128)(2,1)}) %all-gather.5.cloned.1.call-update) | async-done | bytes 8388624 | tf_op jit(solution)/shard_map/all_gather | solution.py:303
  171.0 11.2 constant_dynamic-slice_fusion.8
  202.0 15.0 %copy.375 = bf16[512,2,2816]{0,2,1:T(8,128)(2,1)} copy(bf16[512,2,2816]{2,1,0:T(2,128)(2,1)} %param.29) | data formatting | bytes 11534336 | tf_op args[11]
  235.8 54.1 %collective-permute-done.4 = bf16[512,512]{1,0:T(8,128)(2,1)S(1)} collective-permute-done((bf16[512,512]{1,0:T(8,128)(2,1)}, bf16[512,512]{1,0:T(8,128)(2,1)S(1)}, u32[]{:S(2)}, u32[]{:S(2)}) %collective-permute-start.4) | collective-permute-done | bytes 524320 | tf_op jit(solution)/shard_map/ppermute | solution.py:140
  291.6 30.2 %all-to-all-start.2 = ((bf16[32,64,176]{2,1,0:T(8,128)(2,1)}), bf16[32,64,176]{2,1,0:T(8,128)(2,1)S(1)}, u32[]{:S(2)}, u32[]{:S(2)}) async-start(bf16[32,64,176]{2,1,0:T(8,128)(2,1)} %reshape.695), calls=%async_computation.2 | async-start | bytes 2097152 | tf_op jit(solution)/shard_map/all_to_all | solution.py:321
  370.9 8.0 fusion.253
  409.1 23.5 %collective-permute-done.21 = bf16[512,1408]{1,0:T(8,128)(2,1)} collective-permute-done((bf16[512,1408]{1,0:T(8,128)(2,1)}, bf16[512,1408]{1,0:T(8,128)(2,1)}, u32[]{:S(2)}, u32[]{:S(2)}) %collective-permute-start.21) | collective-permute-done | bytes 1441824 | tf_op jit(solution)/shard_map/ppermute | solution.py:140
  434.2 29.3 %collective-permute-done.23 = bf16[512,1408]{1,0:T(8,128)(2,1)} collective-permute-done((bf16[512,1408]{1,0:T(8,128)(2,1)}, bf16[512,1408]{1,0:T(8,128)(2,1)}, u32[]{:S(2)}, u32[]{:S(2)}) %collective-permute-start.23) | collective-permute-done | bytes 1441824 | tf_op jit(solution)/shard_map/ppermute | solution.py:140
  475.9 40.2 %collective-permute-done.13 = bf16[128,2048]{1,0:T(8,128)(2,1)S(1)} collective-permute-done((bf16[128,2048]{1,0:T(8,128)(2,1)S(1)}, bf16[128,2048]{1,0:T(8,128)(2,1)S(1)}, u32[]{:S(2)}, u32[]{:S(2)}) %collective-permute-start.13) | collective-permute-done | bytes 524320 | tf_op jit(solution)/shard_map/ppermute | solution.py:140
  526.7 9.9 collective-permute-done.10
  546.1 8.1 collective-permute-done.15
  554.6 10.6 collective-permute-done.11
  603.7 15.0 %multiply_convert_fusion.1 = bf16[4,384,2048]{2,1,0:T(8,128)(2,1)} fusion(f32[4,384]{1,0:T(4,128)S(1)} %copy-done.171, bf16[4,1024,384]{1,2,0:T(8,128)(2,1)} %compare_convert_fusion, bf16[4,1024,2048]{2,1,0:T(8,128)(2,1)} %bitcast.518), kind=kOutput, calls=%fused_computation.18 | convolution fusion | flops 6448742400 | bytes 26220544 | tf_op jit(solution)/shard_map/gtc,gtd->gcd/dot_general | solution.py:384
  640.9 8.2 convolution_convert_fusion.10
  745.0 8.9 collective-permute-done.29
  785.0 15.2 %convolution_convert_fusion = bf16[4,1024,2048]{2,1,0:T(8,128)(2,1)} fusion(bf16[4,88,2048]{2,1,0:T(8,128)(2,1)} %broadcast_in_dim.215, bf16[4,384,2048]{2,1,0:T(8,128)(2,1)} %multiply_convert_fusion, bf16[4,1024,88]{1,2,0:T(8,128)(2,1)} %copy.443, bf16[4,1024,384]{1,2,0:T(8,128)(2,1)} %compare_convert_fusion), kind=kOutput, calls=%fused_computation.16 | convolution fusion | flops 7950434304 | bytes 28377088 | tf_op jit(solution)/shard_map/gtk,gkd->gtd/dot_general | solution.py:456
  810.7 10.5 collective-permute-start.32
  827.3 10.4 collective-permute-start.36
  840.0 12.3 convolution_convert_fusion.1
  877.3 39.8 %collective-permute-done.37 = bf16[256,2048]{1,0:T(8,128)(2,1)} collective-permute-done((bf16[256,2048]{1,0:T(8,128)(2,1)}, bf16[256,2048]{1,0:T(8,128)(2,1)}, u32[]{:S(2)}, u32[]{:S(2)}) %collective-permute-start.37) | collective-permute-done | bytes 1048608 | tf_op jit(solution)/shard_map/ppermute | solution.py:107
  921.1 11.8 collective-permute-done.38
  934.6 73.5 %collective-permute-done.35 = bf16[128,2048]{1,0:T(8,128)(2,1)S(1)} collective-permute-done((bf16[128,2048]{1,0:T(8,128)(2,1)S(1)}, bf16[128,2048]{1,0:T(8,128)(2,1)S(1)}, u32[]{:S(2)}, u32[]{:S(2)}) %collective-permute-start.35) | collective-permute-done | bytes 524320 | tf_op jit(solution)/shard_map/ppermute | solution.py:140
  1084.7 17.4 %collective-permute-start.47 = (bf16[512,512]{1,0:T(8,128)(2,1)}, bf16[512,512]{1,0:T(8,128)(2,1)}, u32[]{:S(2)}, u32[]{:S(2)}) collective-permute-start(bf16[512,512]{1,0:T(8,128)(2,1)} %bitcast.600), channel_id=1, source_target_pairs={{0,16},{8,24},{16,0},{24,8},{1,17},{9,25},{17,1},{25,9},{2,18},{10... | collective-permute-start | bytes 1572872 | tf_op jit(solution)/shard_map/ppermute | solution.py:140
  1131.6 45.7 %collective-permute-done.47 = bf16[512,512]{1,0:T(8,128)(2,1)} collective-permute-done((bf16[512,512]{1,0:T(8,128)(2,1)}, bf16[512,512]{1,0:T(8,128)(2,1)}, u32[]{:S(2)}, u32[]{:S(2)}) %collective-permute-start.47) | collective-permute-done | bytes 524320 | tf_op jit(solution)/shard_map/ppermute | solution.py:140
  1177.3 47.1 %collective-permute-done.46 = bf16[512,512]{1,0:T(8,128)(2,1)S(1)} collective-permute-done((bf16[512,512]{1,0:T(8,128)(2,1)}, bf16[512,512]{1,0:T(8,128)(2,1)S(1)}, u32[]{:S(2)}, u32[]{:S(2)}) %collective-permute-start.46) | collective-permute-done | bytes 524320 | tf_op jit(solution)/shard_map/ppermute | solution.py:140
  1245.8 13.2 collective-permute-done.50
  1285.1 9.6 copy.435
  1294.8 9.9 assemble.1
  1333.8 13.4 collective-permute-done.59
  1349.4 8.1 collective-permute-start.61
  1363.8 27.8 %all-to-all-done.4 = f32[32,1,144]{2,1,0:T(1,128)S(1)} async-done(((f32[32,1,144]{2,1,0:T(1,128)}), f32[32,1,144]{2,1,0:T(1,128)S(1)}, u32[]{:S(2)}, u32[]{:S(2)}) %all-to-all-start.4) | async-done | bytes 18464 | tf_op jit(solution)/shard_map/all_to_all | solution.py:554
  (860 shorter events, 610.7 us)
Async XLA Ops:
  7.2 65.6 %all-gather.9.cloned.1.call-start = ((), (), s32[]{:S(2)}) async-start(), calls=%async_computation.11 | async-start | bytes 3379200 | tf_op jit(solution)/shard_map/all_gather | solution.py:290
  13.2 138.6 %all-gather.5.cloned.1.call-start = ((), (), s32[]{:S(2)}) async-start(), calls=%async_computation.8 | async-start | bytes 8650752 | tf_op jit(solution)/shard_map/all_gather | solution.py:303
  72.9 530.8 %all-gather.7.cloned.1.call-start = ((), (), s32[]{:S(2)}) async-start(), calls=%async_computation.9 | async-start | bytes 17301504 | tf_op jit(solution)/shard_map/all_gather | solution.py:304
  162.7 67.0 %collective-permute-start.1 = (bf16[256,2048]{0,1:T(8,128)(2,1)}, bf16[256,2048]{0,1:T(8,128)(2,1)S(1)}, u32[]{:S(2)}, u32[]{:S(2)}) collective-permute-start(bf16[256,2048]{0,1:T(8,128)(2,1)} %pad_maximum_fusion.23), channel_id=1, source_target_pairs={{0,4},{1,3},{2,6},{3,1},{4,0},{5,7},{6,2},{7,5},{8,12},{9,11},{10,... | collective-permute-start | bytes 3145736 | tf_op jit(solution)/shard_map/ppermute | solution.py:107
  185.6 48.3 %collective-permute-start.3 = (bf16[512,512]{1,0:T(8,128)(2,1)}, bf16[512,512]{1,0:T(8,128)(2,1)}, u32[]{:S(2)}, u32[]{:S(2)}) collective-permute-start(bf16[512,512]{1,0:T(8,128)(2,1)} %bitcast.16), channel_id=1, source_target_pairs={{0,8},{8,0},{16,24},{24,16},{1,9},{9,1},{17,25},{25,17},{2,10},{10... | collective-permute-start | bytes 1572872 | tf_op jit(solution)/shard_map/ppermute | solution.py:140
  223.1 66.8 %collective-permute-start.4 = (bf16[512,512]{1,0:T(8,128)(2,1)}, bf16[512,512]{1,0:T(8,128)(2,1)S(1)}, u32[]{:S(2)}, u32[]{:S(2)}) collective-permute-start(bf16[512,512]{1,0:T(8,128)(2,1)} %bitcast.16), channel_id=1, source_target_pairs={{0,16},{8,24},{16,0},{24,8},{1,17},{9,25},{17,1},{25,9},{2,18},{10... | collective-permute-start | bytes 1572872 | tf_op jit(solution)/shard_map/ppermute | solution.py:140
  223.2 67.6 %collective-permute-start.5 = (bf16[512,512]{1,0:T(8,128)(2,1)}, bf16[512,512]{1,0:T(8,128)(2,1)S(1)}, u32[]{:S(2)}, u32[]{:S(2)}) collective-permute-start(bf16[512,512]{1,0:T(8,128)(2,1)} %bitcast.16), channel_id=1, source_target_pairs={{0,24},{8,16},{16,8},{24,0},{1,25},{9,17},{17,9},{25,1},{2,26},{10... | collective-permute-start | bytes 1572872 | tf_op jit(solution)/shard_map/ppermute | solution.py:140
  231.3 119.8 %collective-permute-start.2 = (bf16[512,2048]{0,1:T(8,128)(2,1)}, bf16[512,2048]{0,1:T(8,128)(2,1)}, u32[]{:S(2)}, u32[]{:S(2)}) collective-permute-start(bf16[512,2048]{0,1:T(8,128)(2,1)} %pad_maximum_fusion.12), channel_id=1, source_target_pairs={{0,1},{1,0},{2,3},{3,2},{4,5},{5,4},{6,7},{7,6},{8,9},{9,8},{10,11... | collective-permute-start | bytes 6291464 | tf_op jit(solution)/shard_map/ppermute | solution.py:111
  291.6 58.3 %all-to-all-start.2 = ((bf16[32,64,176]{2,1,0:T(8,128)(2,1)}), bf16[32,64,176]{2,1,0:T(8,128)(2,1)S(1)}, u32[]{:S(2)}, u32[]{:S(2)}) async-start(bf16[32,64,176]{2,1,0:T(8,128)(2,1)} %reshape.695), calls=%async_computation.2 | async-start | bytes 2097152 | tf_op jit(solution)/shard_map/all_to_all | solution.py:321
  330.7 78.0 %collective-permute-start.24 = (bf16[352,2048]{1,0:T(8,128)(2,1)}, bf16[352,2048]{1,0:T(8,128)(2,1)}, u32[]{:S(2)}, u32[]{:S(2)}) collective-permute-start(bf16[352,2048]{1,0:T(8,128)(2,1)} %bitcast.576), channel_id=1, source_target_pairs={{0,8},{8,0},{16,24},{24,16},{1,9},{9,1},{17,25},{25,17},{2,10},{10... | collective-permute-start | bytes 4325384 | tf_op jit(solution)/shard_map/ppermute | solution.py:140
  341.2 91.4 %collective-permute-start.21 = (bf16[512,1408]{1,0:T(8,128)(2,1)}, bf16[512,1408]{1,0:T(8,128)(2,1)}, u32[]{:S(2)}, u32[]{:S(2)}) collective-permute-start(bf16[512,1408]{1,0:T(8,128)(2,1)} %bitcast.579), channel_id=1, source_target_pairs={{0,8},{8,0},{16,24},{24,16},{1,9},{9,1},{17,25},{25,17},{2,10},{10... | collective-permute-start | bytes 4325384 | tf_op jit(solution)/shard_map/ppermute | solution.py:140
  345.0 87.6 %collective-permute-start.22 = (bf16[512,1408]{1,0:T(8,128)(2,1)}, bf16[512,1408]{1,0:T(8,128)(2,1)}, u32[]{:S(2)}, u32[]{:S(2)}) collective-permute-start(bf16[512,1408]{1,0:T(8,128)(2,1)} %bitcast.578), channel_id=1, source_target_pairs={{0,16},{8,24},{16,0},{24,8},{1,17},{9,25},{17,1},{25,9},{2,18},{10... | collective-permute-start | bytes 4325384 | tf_op jit(solution)/shard_map/ppermute | solution.py:140
  347.8 115.7 %collective-permute-start.23 = (bf16[512,1408]{1,0:T(8,128)(2,1)}, bf16[512,1408]{1,0:T(8,128)(2,1)}, u32[]{:S(2)}, u32[]{:S(2)}) collective-permute-start(bf16[512,1408]{1,0:T(8,128)(2,1)} %bitcast.577), channel_id=1, source_target_pairs={{0,24},{8,16},{16,8},{24,0},{1,25},{9,17},{17,9},{25,1},{2,26},{10... | collective-permute-start | bytes 4325384 | tf_op jit(solution)/shard_map/ppermute | solution.py:140
  391.1 1001.8 %reduce-scatter.2.cloned.1.call-start = ((), (), s32[]{:S(2)}) async-start(), calls=%async_computation.10 | async-start | bytes 17301504 | tf_op jit(solution)/shard_map/reduce_scatter | solution.py:464
  407.5 67.2 %collective-permute-start.17 = (bf16[128,2048]{1,0:T(8,128)(2,1)S(1)}, bf16[128,2048]{1,0:T(8,128)(2,1)S(1)}, u32[]{:S(2)}, u32[]{:S(2)}) collective-permute-start(bf16[128,2048]{1,0:T(8,128)(2,1)S(1)} %multiply_convert_fusion.11), channel_id=1, source_target_pairs={{0,24},{8,16},{16,8},{24,0},{1,25},{9,17},{17,9},{25,1},{2,26},{10... | collective-permute-start | bytes 1572872 | tf_op jit(solution)/shard_map/ppermute | solution.py:140
  408.7 107.4 %collective-permute-start.13 = (bf16[128,2048]{1,0:T(8,128)(2,1)S(1)}, bf16[128,2048]{1,0:T(8,128)(2,1)S(1)}, u32[]{:S(2)}, u32[]{:S(2)}) collective-permute-start(bf16[128,2048]{1,0:T(8,128)(2,1)S(1)} %multiply_convert_fusion.11), channel_id=1, source_target_pairs={{0,16},{8,24},{16,0},{24,8},{1,17},{9,25},{17,1},{25,9},{2,18},{10... | collective-permute-start | bytes 1572872 | tf_op jit(solution)/shard_map/ppermute | solution.py:140
  432.6 84.7 %collective-permute-start.9 = (bf16[128,2048]{1,0:T(8,128)(2,1)S(1)}, bf16[128,2048]{1,0:T(8,128)(2,1)S(1)}, u32[]{:S(2)}, u32[]{:S(2)}) collective-permute-start(bf16[128,2048]{1,0:T(8,128)(2,1)S(1)} %multiply_convert_fusion.11), channel_id=1, source_target_pairs={{0,8},{8,0},{16,24},{24,16},{1,9},{9,1},{17,25},{25,17},{2,10},{10... | collective-permute-start | bytes 1572872 | tf_op jit(solution)/shard_map/ppermute | solution.py:140
  473.3 64.7 %collective-permute-start.7 = (bf16[256,2048]{1,0:T(8,128)(2,1)S(1)}, bf16[256,2048]{1,0:T(8,128)(2,1)S(1)}, u32[]{:S(2)}, u32[]{:S(2)}) collective-permute-start(bf16[256,2048]{1,0:T(8,128)(2,1)S(1)} %pad_maximum_fusion.24), channel_id=1, source_target_pairs={{0,4},{1,3},{2,6},{3,1},{4,0},{5,7},{6,2},{7,5},{8,12},{9,11},{10,... | collective-permute-start | bytes 3145736 | tf_op jit(solution)/shard_map/ppermute | solution.py:107
  810.7 123.9 %collective-permute-start.32 = (bf16[128,2048]{1,0:T(8,128)(2,1)S(1)}, bf16[128,2048]{1,0:T(8,128)(2,1)}, u32[]{:S(2)}, u32[]{:S(2)}) collective-permute-start(bf16[128,2048]{1,0:T(8,128)(2,1)S(1)} %fusion.125), channel_id=1, source_target_pairs={{0,8},{8,0},{16,24},{24,16},{1,9},{9,1},{17,25},{25,17},{2,10},{10... | collective-permute-start | bytes 1572872 | tf_op jit(solution)/shard_map/ppermute | solution.py:140
  854.5 273.2 %collective-permute-start.62 = (bf16[512,1408]{1,0:T(8,128)(2,1)}, bf16[512,1408]{1,0:T(8,128)(2,1)S(1)}, u32[]{:S(2)}, u32[]{:S(2)}) collective-permute-start(bf16[512,1408]{1,0:T(8,128)(2,1)} %get-tuple-element.194), channel_id=1, source_target_pairs={{0,8},{8,0},{16,24},{24,16},{1,9},{9,1},{17,25},{25,17},{2,10},{10... | collective-permute-start | bytes 4325384 | tf_op jit(solution)/shard_map/ppermute | solution.py:140
  854.5 385.8 %collective-permute-start.63 = (bf16[512,1408]{1,0:T(8,128)(2,1)}, bf16[512,1408]{1,0:T(8,128)(2,1)}, u32[]{:S(2)}, u32[]{:S(2)}) collective-permute-start(bf16[512,1408]{1,0:T(8,128)(2,1)} %get-tuple-element.193), channel_id=1, source_target_pairs={{0,16},{8,24},{16,0},{24,8},{1,17},{9,25},{17,1},{25,9},{2,18},{10... | collective-permute-start | bytes 4325384 | tf_op jit(solution)/shard_map/ppermute | solution.py:140
  867.8 49.3 %collective-permute-start.37 = (bf16[256,2048]{1,0:T(8,128)(2,1)}, bf16[256,2048]{1,0:T(8,128)(2,1)}, u32[]{:S(2)}, u32[]{:S(2)}) collective-permute-start(bf16[256,2048]{1,0:T(8,128)(2,1)} %slice.696), channel_id=1, source_target_pairs={{0,4},{1,3},{2,6},{3,1},{4,0},{5,7},{6,2},{7,5},{8,12},{9,11},{10,... | collective-permute-start | bytes 3145736 | tf_op jit(solution)/shard_map/ppermute | solution.py:107
  921.0 87.0 %collective-permute-start.35 = (bf16[128,2048]{1,0:T(8,128)(2,1)S(1)}, bf16[128,2048]{1,0:T(8,128)(2,1)S(1)}, u32[]{:S(2)}, u32[]{:S(2)}) collective-permute-start(bf16[128,2048]{1,0:T(8,128)(2,1)S(1)} %fusion.124), channel_id=1, source_target_pairs={{0,16},{8,24},{16,0},{24,8},{1,17},{9,25},{17,1},{25,9},{2,18},{10... | collective-permute-start | bytes 1572872 | tf_op jit(solution)/shard_map/ppermute | solution.py:140
  933.1 75.0 %collective-permute-start.39 = (bf16[128,2048]{1,0:T(8,128)(2,1)S(1)}, bf16[128,2048]{1,0:T(8,128)(2,1)S(1)}, u32[]{:S(2)}, u32[]{:S(2)}) collective-permute-start(bf16[128,2048]{1,0:T(8,128)(2,1)S(1)} %fusion.123), channel_id=1, source_target_pairs={{0,24},{8,16},{16,8},{24,0},{1,25},{9,17},{17,9},{25,1},{2,26},{10... | collective-permute-start | bytes 1572872 | tf_op jit(solution)/shard_map/ppermute | solution.py:140
  1084.7 92.6 %collective-permute-start.47 = (bf16[512,512]{1,0:T(8,128)(2,1)}, bf16[512,512]{1,0:T(8,128)(2,1)}, u32[]{:S(2)}, u32[]{:S(2)}) collective-permute-start(bf16[512,512]{1,0:T(8,128)(2,1)} %bitcast.600), channel_id=1, source_target_pairs={{0,16},{8,24},{16,0},{24,8},{1,17},{9,25},{17,1},{25,9},{2,18},{10... | collective-permute-start | bytes 1572872 | tf_op jit(solution)/shard_map/ppermute | solution.py:140
  1121.1 114.7 %all-to-all-start.6 = ((bf16[32,64,176]{2,1,0:T(8,128)(2,1)}), bf16[32,64,176]{2,1,0:T(8,128)(2,1)}, u32[]{:S(2)}, u32[]{:S(2)}) async-start(bf16[32,64,176]{2,1,0:T(8,128)(2,1)} %bitcast.557), calls=%async_computation.7 | async-start | bytes 2097152 | tf_op jit(solution)/shard_map/all_to_all | solution.py:480
  1127.7 114.1 %collective-permute-start.64 = (bf16[512,1408]{1,0:T(8,128)(2,1)}, bf16[512,1408]{1,0:T(8,128)(2,1)}, u32[]{:S(2)}, u32[]{:S(2)}) collective-permute-start(bf16[512,1408]{1,0:T(8,128)(2,1)} %get-tuple-element.192), channel_id=1, source_target_pairs={{0,24},{8,16},{16,8},{24,0},{1,25},{9,17},{17,9},{25,1},{2,26},{10... | collective-permute-start | bytes 4325384 | tf_op jit(solution)/shard_map/ppermute | solution.py:140
  1127.8 114.0 %collective-permute-start.65 = (bf16[352,2048]{1,0:T(8,128)(2,1)}, bf16[352,2048]{1,0:T(8,128)(2,1)}, u32[]{:S(2)}, u32[]{:S(2)}) collective-permute-start(bf16[352,2048]{1,0:T(8,128)(2,1)} %select_convert_fusion), channel_id=1, source_target_pairs={{0,8},{8,0},{16,24},{24,16},{1,9},{9,1},{17,25},{25,17},{2,10},{10... | collective-permute-start | bytes 4325384 | tf_op jit(solution)/shard_map/ppermute | solution.py:140
  1128.3 96.1 %collective-permute-start.46 = (bf16[512,512]{1,0:T(8,128)(2,1)}, bf16[512,512]{1,0:T(8,128)(2,1)S(1)}, u32[]{:S(2)}, u32[]{:S(2)}) collective-permute-start(bf16[512,512]{1,0:T(8,128)(2,1)} %bitcast.603), channel_id=1, source_target_pairs={{0,8},{8,0},{16,24},{24,16},{1,9},{9,1},{17,25},{25,17},{2,10},{10... | collective-permute-start | bytes 1572872 | tf_op jit(solution)/shard_map/ppermute | solution.py:140
  1177.3 48.7 %collective-permute-start.55 = (bf16[128,2048]{1,0:T(8,128)(2,1)S(1)}, bf16[128,2048]{1,0:T(8,128)(2,1)S(1)}, u32[]{:S(2)}, u32[]{:S(2)}) collective-permute-start(bf16[128,2048]{1,0:T(8,128)(2,1)S(1)} %fusion.251), channel_id=1, source_target_pairs={{0,2},{1,5},{2,0},{3,7},{4,6},{5,1},{6,4},{7,3},{8,10},{9,13},{10,... | collective-permute-start | bytes 1572872 | tf_op jit(solution)/shard_map/ppermute | solution.py:107
  1235.8 74.5 %all-to-all-start.5 = ((f32[8,64,512]{2,1,0:T(8,128)}), f32[8,64,512]{2,1,0:T(8,128)}, u32[]{:S(2)}, u32[]{:S(2)}) async-start(f32[8,64,512]{2,1,0:T(8,128)} %bitcast.554), calls=%async_computation.6 | async-start | bytes 2097152 | tf_op jit(solution)/shard_map/all_to_all | solution.py:520
  1264.5 55.0 %collective-permute-start.57 = (bf16[512,2048]{1,0:T(8,128)(2,1)}, bf16[512,2048]{1,0:T(8,128)(2,1)}, u32[]{:S(2)}, u32[]{:S(2)}) collective-permute-start(bf16[512,2048]{1,0:T(8,128)(2,1)} %pad_maximum_fusion.17), channel_id=1, source_target_pairs={{0,1},{1,0},{2,3},{3,2},{4,5},{5,4},{6,7},{7,6},{8,9},{9,8},{10,11... | collective-permute-start | bytes 6291464 | tf_op jit(solution)/shard_map/ppermute | solution.py:111
  (239 other events, 4871.6 us)
Sparse Core Ops, SparseCore 0:
  13.3 59.5 all-gather.8
  75.7 76.0 all-gather.4
  154.6 165.0 all-gather.6
  800.4 249.5 reduce-scatter.1

commit v4 on v3

--- a/solution.py
+++ b/solution.py
@@ -144,11 +144,11 @@
     return lax.dynamic_index_in_dim(blocks, index, 0, keepdims=False)
 
 
-def dp_exchange(blocks, n_dp, dp_index):
-    moved = [dp_block(blocks, dp_index)]
-    for step in range(1, n_dp):
-        moved.append(dp_swap(dp_block(blocks, dp_index ^ step), n_dp, step))
-    return moved
+def dp_exchange(blocks, n_dp, dp_index, steps, until):
+    blocks = hold(blocks, until)
+    return {
+        step: dp_swap(dp_block(blocks, dp_index ^ step), n_dp, step) for step in steps
+    }
 
 
 def in_order(moved, n_dp, dp_index):
@@ -258,6 +258,7 @@
     joined = jnp.concatenate([q_weight.reshape(down_rows, n_seq, q_width), up_rows], axis=2)
     joined_width = joined.shape[2]
     joined = lax.all_to_all(joined, "seq", split_axis=1, concat_axis=0, tiled=True)
+    joined_here = joined
     joined = joined.reshape(n_seq * down_rows, joined_width)
     joined = dp_gather(joined, n_dp, dp_index).reshape(-1, joined_width)
     weight_q = joined[:, :q_width]
@@ -300,15 +301,19 @@
     slot_code = routing[:, :, 0] * 16 + routing[:, :, 1]
     gate_of = (routing[:, :, 2] * 128 + routing[:, :, 3]).astype(F32) / GATE_UNIT
 
-    weight_out = lax.all_gather(hold(out_weight, spread), BOTH, axis=0, tiled=True)
-    cot_all = lax.all_gather(hold(cotangent, weight_out), BOTH, axis=0, tiled=True)
+    weight_out = lax.all_gather(hold(out_weight, joined_here), BOTH, axis=0, tiled=True)
+    cot_all = lax.all_gather(hold(cotangent, joined, hidden_group), BOTH, axis=0, tiled=True)
 
     ff_width = expert_gate_up.shape[2] // 2
     ff_part = ff_width // ff_parts
     expert_rows = expert_gate_up.shape[0]
     in_parts = expert_gate_up.reshape(expert_rows, per_device, 2, ff_parts, ff_part)
     in_parts = jnp.transpose(in_parts, (3, 1, 0, 2, 4)).reshape(n_dp, expert_rows, 2 * ff_part)
-    in_moved = dp_exchange(hold(in_parts, joined), n_dp, dp_index)
+    even_steps, odd_steps = range(2, n_dp, 2), range(1, n_dp, 2)
+    in_even = dp_exchange(in_parts, n_dp, dp_index, even_steps, joined)
+    in_odd = dp_exchange(in_parts, n_dp, dp_index, odd_steps, in_even)
+    in_moved = in_even | in_odd
+    in_moved[0] = dp_block(in_parts, dp_index)
     down_kept = lax.dynamic_index_in_dim(expert_down, expert_bit, 1, keepdims=False)
     down_sent = lax.dynamic_index_in_dim(expert_down, 1 - expert_bit, 1, keepdims=False)
     down_got = dp_swap(hold(down_sent, joined), n_dp, 1)
@@ -317,13 +322,14 @@
     units = shared_down.shape[0]
     gate_up_parts = shared_gate_up.reshape(-1, 2, n_all, units)
     gate_up_parts = jnp.transpose(gate_up_parts, (2, 0, 1, 3)).reshape(n_all, -1, 2 * units)
-    gate_up_parts = hold(gate_up_parts, joined)
+    gate_up_parts = hold(gate_up_parts, joined_here)
     weight_shared_in = lax.all_to_all(
         gate_up_parts, BOTH, split_axis=0, concat_axis=0, tiled=True
     ).reshape(-1, 2 * units)
 
     def chunk_gather(values):
-        sent = [values] + [dp_swap(values, n_dp, step) for step in range(1, n_dp)]
+        far = hold(values, in_odd)
+        sent = [values] + [dp_swap(far, n_dp, step) for step in range(1, n_dp)]
         return [seq_gather(piece, n_seq) for piece in sent]
 
     rows_group = hidden_group.astype(F32)
@@ -366,6 +372,7 @@
     shares = probs.astype(BF16)
     attended = jnp.einsum("bhqk,bkhd->bqhd", shares, values, preferred_element_type=F32)
     attended = to_rows(attended.astype(BF16)).reshape(group, heads * VD)
+    attended = hold(attended, in_even, down_got)
     heads_out = absolute(attended.reshape(n_seq, tokens, heads * VD))
     heads_out = lax.all_to_all(heads_out, "seq", split_axis=0, concat_axis=2, tiled=True)
     heads_out = heads_out.reshape(tokens, H * VD)
@@ -381,23 +388,23 @@
     slot_gate = jnp.sum(slot_gate, axis=1)[:, :, None]
     all_placed = lax.optimization_barrier(all_here.astype(BF16))
     cot_rows = cot_all.reshape(n_dp, group, width)
-    slot_cot = jnp.einsum("gtc,gtd->gcd", all_placed, cot_rows, preferred_element_type=F32)
-    slot_cot = (slot_cot * slot_gate).astype(BF16)
+    slot_cot = jnp.stack(
+        [
+            (lead_dot(all_placed[g], cot_rows[g]) * slot_gate[g]).astype(BF16)
+            for g in range(n_dp)
+        ]
+    )
     down_kept, down_got = hold((down_kept, down_got), normed_ffn)
     weight_back = jnp.concatenate(
         [jnp.where(is_low, down_kept, down_got), jnp.where(is_low, down_got, down_kept)], axis=0
     )
-    expert_act_grad = contract(slot_cot, weight_back, 2, 1)
     shared_act_grad = contract(cot_rows, shared_down, 2, 1)
 
-    in_moved = hold(in_moved, normed_ffn)
-    weight_in = in_order(in_moved, n_dp, dp_index).reshape(-1, 2 * ff_part)
     ffn_chunks = chunk_gather(normed_ffn)
     shared_in_back = weight_shared_in.T
     grad_shared_in = 0.0
-    kept_rows, kept_acts, kept_grads = [], [], []
-    kept_shared, shared_acts, planes = [], [], []
-    dn_part = None
+    kept_rows, kept_cots, kept_acts, kept_grads = [], [], [], []
+    kept_shared, shared_acts, spreads = [], [], []
     for step in range(n_dp):
         ffn_rows = ffn_chunks[step]
         codes = relative(dp_block(slot_code, dp_index ^ step)).reshape(group)
@@ -413,42 +420,53 @@
         kept_shared.append(shared_in_grad)
         shared_acts.append(swiglu(shared_gate, shared_up).astype(BF16))
 
-        slot_rows = lead_dot(placed, ffn_rows).astype(BF16)
-        expert_in = matmul(slot_rows, weight_in)
+        kept_rows.append(lead_dot(placed, ffn_rows).astype(BF16))
+        spreads.append((placed, shared_in_grad))
+
+    in_moved = hold([in_moved[step] for step in range(n_dp)], kept_rows[0])
+    weight_in = in_order(in_moved, n_dp, dp_index).reshape(-1, 2 * ff_part)
+    for step in range(n_dp):
+        expert_in = matmul(kept_rows[step], weight_in)
         expert_gate, expert_up = expert_in[:, :ff_part], expert_in[:, ff_part:]
+        chunk_cot = dp_block(slot_cot, dp_index ^ step)
         expert_in_grad = jnp.concatenate(
-            swiglu_back(expert_gate, expert_up, dp_block(expert_act_grad, dp_index ^ step)), axis=1
+            swiglu_back(expert_gate, expert_up, tail_dot(chunk_cot, weight_back)), axis=1
         ).astype(BF16)
         slot_grad = tail_dot(expert_in_grad, weight_in).astype(BF16)
-        for age in range(1, min(step, 3) + 1):
-            placed = hold(placed, planes[step - age][age - 1])
+        spreads[step] += (slot_grad,)
+        kept_cots.append(chunk_cot)
+        kept_acts.append(swiglu(expert_gate, expert_up).astype(BF16))
+        kept_grads.append(expert_in_grad)
+
+    planes, sums = [], []
+    for step in list(range(1, n_dp)) + [0]:
+        placed, shared_in_grad, slot_grad = spreads[step]
+        for age in range(1, min(len(planes), 3) + 1):
+            placed = hold(placed, planes[-age][age - 1])
         dn_part = matmul(
             jnp.concatenate([placed, shared_in_grad], axis=1),
             jnp.concatenate([slot_grad, shared_in_back], axis=0),
         ).astype(BF16)
         planes.append(seq_scatter(dn_part, n_seq))
-
-        kept_rows.append(slot_rows)
-        kept_acts.append(swiglu(expert_gate, expert_up).astype(BF16))
-        kept_grads.append(expert_in_grad)
-    ffn_grad = planes[0][-1]
-    for step in range(1, n_dp):
-        ffn_grad = ffn_grad + dp_swap(planes[step][-1].astype(BF16), n_dp, step).astype(F32)
-
-    kept_rows, kept_acts, kept_grads, shared_acts, ffn_chunks = hold(
-        (kept_rows, kept_acts, kept_grads, shared_acts, ffn_chunks), dn_part
+        if step:
+            sums.append(dp_swap(planes[-1][-1].astype(BF16), n_dp, step).astype(F32))
+        else:
+            sums.append(planes[-1][-1])
+    ffn_grad = sum(sums[1:], sums[0])
+
+    kept_rows, kept_cots, kept_acts, kept_grads, shared_acts, ffn_chunks = hold(
+        (kept_rows, kept_cots, kept_acts, kept_grads, shared_acts, ffn_chunks), dn_part
     )
     grad_in = lead_dot(jnp.concatenate(kept_rows), jnp.concatenate(kept_grads)).astype(BF16)
-    in_back = dp_exchange(grad_in.reshape(n_dp, expert_rows, 2 * ff_part), n_dp, dp_index)
+    back_parts = grad_in.reshape(n_dp, expert_rows, 2 * ff_part)
+    back_even = dp_exchange(back_parts, n_dp, dp_index, even_steps, ffn_grad)
     expert_act = in_order(kept_acts, n_dp, dp_index)
-    grad_back = lead_dot(
-        expert_act.reshape(n_dp * capacity, ff_part), slot_cot.reshape(n_dp * capacity, width)
-    )
+    grad_back = lead_dot(jnp.concatenate(kept_acts), jnp.concatenate(kept_cots))
     half = expert_down.shape[0]
     low_half, high_half = grad_back[:half], grad_back[half:]
     grad_kept = jnp.where(is_low, low_half, high_half)
     grad_sent = jnp.where(is_low, high_half, low_half).astype(BF16)
-    grad_got = dp_swap(grad_sent, n_dp, 1)
+    grad_got = dp_swap(hold(grad_sent, ffn_grad), n_dp, 1)
     shared_act = in_order(
         [absolute(act.reshape(n_seq, tokens, units)) for act in shared_acts], n_dp, dp_index
     ).reshape(n_dp, group, units)
@@ -462,7 +480,10 @@
         preferred_element_type=F32,
     ).astype(BF16)
     out_sum = lax.psum_scatter(
-        out_part.reshape(n_all * tokens, width), BOTH, scatter_dimension=0, tiled=True
+        hold(out_part.reshape(n_all * tokens, width), ffn_grad),
+        BOTH,
+        scatter_dimension=0,
+        tiled=True,
     )
     output = (residual + out_sum.astype(F32)).astype(BF16)
     grad_shared_down = lead_dot(shared_act.reshape(n_all * tokens, units), cot_all)
@@ -510,12 +531,14 @@
         [key_grad[..., :NOPE].astype(BF16), value_grad], axis=-1
     ).reshape(group, e_width)
 
+    expand_low = hold(expand_low, grad_got, back_even)
     latent_part = tail_dot(expand_low, weight_up)
     latent_sum = seq_scatter(jnp.concatenate([latent_part, rope_grad], axis=1), n_seq)[-1]
     normed_sum = seq_scatter(tail_dot(query_low, weight_q), n_seq)[-1]
     grad_q = lead_dot(normed_group, query_low)
     grad_up = lead_dot(latent, expand_low).reshape(width, -1)
     grad_joined = dp_scatter(jnp.concatenate([grad_q, grad_up], axis=1), n_dp, dp_index)
+    back_odd = dp_exchange(back_parts, n_dp, dp_index, odd_steps, grad_joined)
     grad_joined = grad_joined.reshape(n_seq, down_rows, joined_width)
     grad_joined = lax.all_to_all(grad_joined, "seq", split_axis=0, concat_axis=0, tiled=True)
     grad_q = jnp.swapaxes(grad_joined[..., :q_width], 0, 1).reshape(q_weight.shape)
@@ -530,7 +553,10 @@
     grad_down = lead_dot(normed_cols.reshape(group, n_dp * down_rows), down_group)
     grad_down = dp_scatter(grad_down, n_dp, dp_index)
 
+    in_back = back_even | back_odd
+    in_back[0] = dp_block(back_parts, dp_index)
     in_back, grad_got, shared_back = hold((in_back, grad_got, shared_back), down_low)
+    in_back = [in_back[step] for step in range(n_dp)]
     grad_expert_in = assemble(in_back, dp_index, expert_gate_up.shape)
     grad_got = grad_got.astype(F32)
     grad_expert_down = jnp.stack(

time: 1420 us -> 1230 us (0.87)
  waiting for transfers between devices: 630 us -> 449 us
    ppermute x26, waiting for transfers between devices: 331 us -> 218 us  [dp_swap(): return lax.ppermute(values, 'dp', [(d, d ^ step) for d in range(n_dp)])]
    all_to_all x1, waiting for transfers between devices: 0.01 us -> 86.8 us  [body(): lax.all_to_all(gate_up_parts, BOTH, split_axis=0, concat_axis=0, tiled=True)]
    all_gather x2, waiting for transfers between devices: 78.8 us -> 0.02 us  [the longest x1 0.02 us: body(): lax.all_gather(hold(out_weight, joined_here), BOTH, axis=0, tiled=True)]
    ppermute x26, waiting for transfers between devices: 126 us -> 60.7 us  [seq_step(): lax.ppermute(values, 'seq', [(s, s ^ orders[s & 1][step]) for s in range(...]
    all_gather x1, waiting for transfers between devices: 59.6 us -> 0.01 us  [body(): spread = lax.all_gather(message, BOTH, axis=0, tiled=False)]
    all_to_all x1, waiting for transfers between devices: 0.01 us -> 38.2 us  [body(): lax.all_to_all(grad_shared_in.reshape(n_all, -1, 2 * units), BOTH, split_...]
    all_to_all x1, starting transfers between devices: 30.2 us -> 5.14 us  [body(): lax.all_to_all(gate_up_parts, BOTH, split_axis=0, concat_axis=0, tiled=True)]
    dot_general x42 -> x49, matrix products: 155 us -> 175 us  [contract(): lax.dot_general(left_side, right_side, (((left_dim,), (right_dim,)), ((),...]
  transfers between devices with their start and end apart: 77 -> 76, of which waited for: 29 -> 24; matrix products, arithmetic and copies ran while one was open for 30% -> 39% of each run, Pallas kernels for 1% -> 1%
where the time goes in v4:
time: 1230 us; the launch traced here: 1220 us
  waiting for transfers between devices  449 us (37%)
  local copies, waits for them, and re-layouts  236 us (19%)
  matrix products  215 us (17%)
  starting transfers between devices  154 us (13%)
  other arithmetic  123 us (10%)
  between operations  17.3 us (1%)
  blocking collectives  13.4 us (1%)
    ppermute x26, waiting for transfers between devices, dp_swap(): return lax.ppermute(values, 'dp', [(d, d ^ step) for d in range(n_dp)])  218 us
    dot_general x49, matrix products, contract(): lax.dot_general(left_side, right_side, (((left_dim,), (right_dim,)), ((),...  175 us
    all_to_all x1, waiting for transfers between devices, body(): lax.all_to_all(gate_up_parts, BOTH, split_axis=0, concat_axis=0, tiled=True)  86.8 us
    unnamed x428, local copies, waits for them, and re-layouts  63.6 us
    ppermute x26, waiting for transfers between devices, seq_step(): lax.ppermute(values, 'seq', [(s, s ^ orders[s & 1][step]) for s in range(...  60.7 us
    ppermute x26, starting transfers between devices, dp_swap(): return lax.ppermute(values, 'dp', [(d, d ^ step) for d in range(n_dp)])  58.2 us
    all_to_all x1, waiting for transfers between devices, body(): lax.all_to_all(grad_shared_in.reshape(n_all, -1, 2 * units), BOTH, split_...  38.2 us
    all_to_all x1, waiting for transfers between devices, body(): lax.all_to_all(gain_grads, BOTH, split_axis=0, concat_axis=0, tiled=True)  29.9 us
  transfers between devices with their start and end apart: 76, of which 24 were waited for; matrix products, arithmetic and copies ran while one was open for 39% of the time, Pallas kernels for 1%

profile of v4, /device:TPU:25, one launch (start us, length us, event | category | flops | bytes accessed | tf_op | source)
XLA Modules:
  0.0 1217.6 jit_solution(11094659058464415048)
XLA Ops:
  15.5 13.4 %all_to_all.75 = bf16[64,8,512]{2,0,1:T(8,128)(2,1)S(1)} all-to-all(bf16[64,8,512]{2,0,1:T(8,128)(2,1)S(1)} %copy.383), channel_id=1, replica_groups=mesh['dp'=4,'seq'=8] {'seq'}, dimensions={1} | all-to-all | bytes 1048576 | tf_op jit(solution)/shard_map/all_to_all | solution.py:260
  29.6 8.0 collective-permute-done
  38.8 15.8 %collective-permute-done.1 = bf16[256,2048]{0,1:T(8,128)(2,1)S(1)} collective-permute-done((bf16[256,2048]{0,1:T(8,128)(2,1)S(1)}, bf16[256,2048]{0,1:T(8,128)(2,1)S(1)}, u32[]{:S(2)}, u32[]{:S(2)}) %collective-permute-start.1) | collective-permute-done | bytes 1048608 | tf_op jit(solution)/shard_map/ppermute | solution.py:107
  61.3 30.3 %collective-permute-done.3 = bf16[512,512]{1,0:T(8,128)(2,1)} collective-permute-done((bf16[512,512]{1,0:T(8,128)(2,1)S(1)}, bf16[512,512]{1,0:T(8,128)(2,1)}, u32[]{:S(2)}, u32[]{:S(2)}) %collective-permute-start.3) | collective-permute-done | bytes 524320 | tf_op jit(solution)/shard_map/ppermute | solution.py:140
  93.7 8.6 collective-permute-done.5
  107.0 14.9 %copy.387 = bf16[512,2,2816]{0,2,1:T(8,128)(2,1)} copy(bf16[512,2,2816]{2,1,0:T(2,128)(2,1)} %param.29) | data formatting | bytes 11534336 | tf_op args[11]
  127.5 11.2 constant_dynamic-slice_fusion.4
  141.7 12.6 %collective-permute-start.6 = (bf16[512,1408]{1,0:T(8,128)(2,1)}, bf16[512,1408]{1,0:T(8,128)(2,1)}, u32[]{:S(2)}, u32[]{:S(2)}) collective-permute-start(bf16[512,1408]{1,0:T(8,128)(2,1)} %bitcast.560), channel_id=1, source_target_pairs={{0,16},{8,24},{16,0},{24,8},{1,17},{9,25},{17,1},{25,9},{2,18},{10... | collective-permute-start | bytes 4325384 | tf_op jit(solution)/shard_map/ppermute | solution.py:140
  187.0 86.8 %all-to-all-done.2 = bf16[32,64,176]{2,1,0:T(8,128)(2,1)S(1)} async-done(((bf16[32,64,176]{2,1,0:T(8,128)(2,1)}), bf16[32,64,176]{2,1,0:T(8,128)(2,1)S(1)}, u32[]{:S(2)}, u32[]{:S(2)}) %all-to-all-start.2) | async-done | bytes 720928 | tf_op jit(solution)/shard_map/all_to_all | solution.py:326
  307.5 9.0 fusion.285
  355.4 41.4 %collective-permute-done.12 = bf16[512,1408]{1,0:T(8,128)(2,1)} collective-permute-done((bf16[512,1408]{1,0:T(8,128)(2,1)}, bf16[512,1408]{1,0:T(8,128)(2,1)}, u32[]{:S(2)}, u32[]{:S(2)}) %collective-permute-start.12) | collective-permute-done | bytes 1441824 | tf_op jit(solution)/shard_map/ppermute | solution.py:140
  405.4 26.6 %collective-permute-done.13 = bf16[128,2048]{1,0:T(8,128)(2,1)S(1)} collective-permute-done((bf16[128,2048]{1,0:T(8,128)(2,1)S(1)}, bf16[128,2048]{1,0:T(8,128)(2,1)S(1)}, u32[]{:S(2)}, u32[]{:S(2)}) %collective-permute-start.13) | collective-permute-done | bytes 524320 | tf_op jit(solution)/shard_map/ppermute | solution.py:140
  433.6 9.6 collective-permute-done.21
  454.4 18.6 %collective-permute-start.10 = (bf16[512,2048]{1,0:T(8,128)(2,1)S(1)}, bf16[512,2048]{1,0:T(8,128)(2,1)S(1)}, u32[]{:S(2)}, u32[]{:S(2)}) collective-permute-start(bf16[512,2048]{1,0:T(8,128)(2,1)S(1)} %pad_maximum_fusion.15), channel_id=1, source_target_pairs={{0,1},{1,0},{2,3},{3,2},{4,5},{5,4},{6,7},{7,6},{8,9},{9,8},{10,11... | collective-permute-start | bytes 6291464 | tf_op jit(solution)/shard_map/ppermute | solution.py:111
  473.4 7.6 collective-permute-done.19
  481.2 10.7 collective-permute-done.23
  539.5 11.0 fusion.205
  723.8 7.7 collective-permute-done.38
  733.8 16.2 %convolution_convert_fusion = bf16[4,1024,2048]{2,1,0:T(8,128)(2,1)} fusion(bf16[4,88,2048]{2,1,0:T(8,128)(2,1)S(1)} %broadcast_in_dim.215, bf16[4,384,2048]{2,1,0:T(8,128)(2,1)} %multiply_convert_fusion, bf16[4,1024,88]{1,2,0:T(8,128)(2,1)} %copy.465, bf16[4,1024,384]{1,2,0:T(8,128)(2,1)} %compare_convert_fusion), kind=kOutput, calls=%fused_computation.16 | convolution fusion | flops 7950434304 | bytes 28377088 | tf_op jit(solution)/shard_map/gtk,gkd->gtd/dot_general | solution.py:474
  768.9 10.0 fusion.9
  786.8 15.7 %convolution_convert_fusion.1 = bf16[2048,1408]{1,0:T(8,128)(2,1)} fusion(bf16[384,2048]{1,0:T(8,128)(2,1)} %copy-done.182, bf16[384,2048]{1,0:T(8,128)(2,1)} %copy-done.181, bf16[384,2048]{1,0:T(8,128)(2,1)} %copy-done.180, bf16[384,2048]{1,0:T(8,128)(2,1)} %convolution_convert_fusion.14, bf16[384,1408]{1,0:T(8,128)(2,1)} %pad_maximum_fusion.24, ...), kind=kOutput, calls=%fused_computation.32 | convolution fusion | flops 8903720960 | bytes 16384000 | tf_op jit(solution)/shard_map/dot_general | solution.py:26
  817.5 8.4 all-to-all-done.3
  859.2 50.2 %collective-permute-done.44.refs_2_ = bf16[512,1408]{1,0:T(8,128)(2,1)S(1)} collective-permute-done((bf16[512,1408]{1,0:T(8,128)(2,1)}, bf16[512,1408]{1,0:T(8,128)(2,1)S(1)}, u32[]{:S(2)}, u32[]{:S(2)}) %collective-permute-start.44) | collective-permute-done | bytes 1441824 | tf_op jit(solution)/shard_map/ppermute | solution.py:140
  942.9 16.1 %collective-permute-done.48 = bf16[512,512]{1,0:T(8,128)(2,1)} collective-permute-done((bf16[512,512]{1,0:T(8,128)(2,1)}, bf16[512,512]{1,0:T(8,128)(2,1)}, u32[]{:S(2)}, u32[]{:S(2)}) %collective-permute-start.48) | collective-permute-done | bytes 524320 | tf_op jit(solution)/shard_map/ppermute | solution.py:140
  959.1 22.8 %collective-permute-done.49 = bf16[512,512]{1,0:T(8,128)(2,1)} collective-permute-done((bf16[512,512]{1,0:T(8,128)(2,1)}, bf16[512,512]{1,0:T(8,128)(2,1)}, u32[]{:S(2)}, u32[]{:S(2)}) %collective-permute-start.49) | collective-permute-done | bytes 524320 | tf_op jit(solution)/shard_map/ppermute | solution.py:140
  989.9 11.5 collective-permute-start.64
  1001.6 8.1 all-to-all-start.5
  1021.6 7.8 all-to-all-start.6
  1050.7 38.2 %all-to-all-done.6 = bf16[32,64,176]{2,1,0:T(8,128)(2,1)} async-done(((bf16[32,64,176]{2,1,0:T(8,128)(2,1)}), bf16[32,64,176]{2,1,0:T(8,128)(2,1)}, u32[]{:S(2)}, u32[]{:S(2)}) %all-to-all-start.6) | async-done | bytes 720928 | tf_op jit(solution)/shard_map/all_to_all | solution.py:501
  1118.5 9.9 assemble.1
  1165.6 9.2 all-to-all-start.4
  1174.8 29.9 %all-to-all-done.4 = f32[32,1,144]{2,1,0:T(1,128)S(1)} async-done(((f32[32,1,144]{2,1,0:T(1,128)}), f32[32,1,144]{2,1,0:T(1,128)S(1)}, u32[]{:S(2)}, u32[]{:S(2)}) %all-to-all-start.4) | async-done | bytes 18464 | tf_op jit(solution)/shard_map/all_to_all | solution.py:580
  (879 shorter events, 602.2 us)
Async XLA Ops:
  7.2 278.7 %all-gather.9.cloned.1.call-start = ((), (), s32[]{:S(2)}) async-start(), calls=%async_computation.11 | async-start | bytes 3379200 | tf_op jit(solution)/shard_map/all_gather | solution.py:291
  13.1 334.9 %all-gather.5.cloned.1.call-start = ((), (), s32[]{:S(2)}) async-start(), calls=%async_computation.8 | async-start | bytes 8650752 | tf_op jit(solution)/shard_map/all_gather | solution.py:304
  28.9 510.6 %all-gather.7.cloned.1.call-start = ((), (), s32[]{:S(2)}) async-start(), calls=%async_computation.9 | async-start | bytes 17301504 | tf_op jit(solution)/shard_map/all_gather | solution.py:305
  56.3 46.1 %collective-permute-start.2 = (bf16[512,2048]{0,1:T(8,128)(2,1)}, bf16[512,2048]{0,1:T(8,128)(2,1)}, u32[]{:S(2)}, u32[]{:S(2)}) collective-permute-start(bf16[512,2048]{0,1:T(8,128)(2,1)} %pad_maximum_fusion.14), channel_id=1, source_target_pairs={{0,1},{1,0},{2,3},{3,2},{4,5},{5,4},{6,7},{7,6},{8,9},{9,8},{10,11... | collective-permute-start | bytes 6291464 | tf_op jit(solution)/shard_map/ppermute | solution.py:111
  58.0 44.3 %collective-permute-start.5 = (bf16[512,512]{1,0:T(8,128)(2,1)S(1)}, bf16[512,512]{1,0:T(8,128)(2,1)S(1)}, u32[]{:S(2)}, u32[]{:S(2)}) collective-permute-start(bf16[512,512]{1,0:T(8,128)(2,1)S(1)} %bitcast.551), channel_id=1, source_target_pairs={{0,24},{8,16},{16,8},{24,0},{1,25},{9,17},{17,9},{25,1},{2,26},{10... | collective-permute-start | bytes 1572872 | tf_op jit(solution)/shard_map/ppermute | solution.py:140
  141.7 133.3 %collective-permute-start.6 = (bf16[512,1408]{1,0:T(8,128)(2,1)}, bf16[512,1408]{1,0:T(8,128)(2,1)}, u32[]{:S(2)}, u32[]{:S(2)}) collective-permute-start(bf16[512,1408]{1,0:T(8,128)(2,1)} %bitcast.560), channel_id=1, source_target_pairs={{0,16},{8,24},{16,0},{24,8},{1,17},{9,25},{17,1},{25,9},{2,18},{10... | collective-permute-start | bytes 4325384 | tf_op jit(solution)/shard_map/ppermute | solution.py:140
  172.5 101.3 %all-to-all-start.2 = ((bf16[32,64,176]{2,1,0:T(8,128)(2,1)}), bf16[32,64,176]{2,1,0:T(8,128)(2,1)S(1)}, u32[]{:S(2)}, u32[]{:S(2)}) async-start(bf16[32,64,176]{2,1,0:T(8,128)(2,1)} %reshape.717), calls=%async_computation.2 | async-start | bytes 2097152 | tf_op jit(solution)/shard_map/all_to_all | solution.py:326
  186.8 134.9 %collective-permute-start.7 = (bf16[352,2048]{1,0:T(8,128)(2,1)}, bf16[352,2048]{1,0:T(8,128)(2,1)}, u32[]{:S(2)}, u32[]{:S(2)}) collective-permute-start(bf16[352,2048]{1,0:T(8,128)(2,1)} %bitcast.559), channel_id=1, source_target_pairs={{0,8},{8,0},{16,24},{24,16},{1,9},{9,1},{17,25},{25,17},{2,10},{10... | collective-permute-start | bytes 4325384 | tf_op jit(solution)/shard_map/ppermute | solution.py:140
  281.1 74.3 %collective-permute-start.11 = (bf16[512,1408]{1,0:T(8,128)(2,1)}, bf16[512,1408]{1,0:T(8,128)(2,1)}, u32[]{:S(2)}, u32[]{:S(2)}) collective-permute-start(bf16[512,1408]{1,0:T(8,128)(2,1)} %bitcast.557), channel_id=1, source_target_pairs={{0,8},{8,0},{16,24},{24,16},{1,9},{9,1},{17,25},{25,17},{2,10},{10... | collective-permute-start | bytes 4325384 | tf_op jit(solution)/shard_map/ppermute | solution.py:140
  283.9 113.0 %collective-permute-start.12 = (bf16[512,1408]{1,0:T(8,128)(2,1)}, bf16[512,1408]{1,0:T(8,128)(2,1)}, u32[]{:S(2)}, u32[]{:S(2)}) collective-permute-start(bf16[512,1408]{1,0:T(8,128)(2,1)} %bitcast.558), channel_id=1, source_target_pairs={{0,24},{8,16},{16,8},{24,0},{1,25},{9,17},{17,9},{25,1},{2,26},{10... | collective-permute-start | bytes 4325384 | tf_op jit(solution)/shard_map/ppermute | solution.py:140
  328.4 877.5 %reduce-scatter.2.cloned.1.call-start = ((), (), s32[]{:S(2)}) async-start(), calls=%async_computation.10 | async-start | bytes 17301504 | tf_op jit(solution)/shard_map/reduce_scatter | solution.py:482
  354.0 49.7 %collective-permute-start.8 = (bf16[128,2048]{1,0:T(8,128)(2,1)S(1)}, bf16[128,2048]{1,0:T(8,128)(2,1)S(1)}, u32[]{:S(2)}, u32[]{:S(2)}) collective-permute-start(bf16[128,2048]{1,0:T(8,128)(2,1)S(1)} %multiply_convert_fusion.22), channel_id=1, source_target_pairs={{0,2},{1,5},{2,0},{3,7},{4,6},{5,1},{6,4},{7,3},{8,10},{9,13},{10,... | collective-permute-start | bytes 1572872 | tf_op jit(solution)/shard_map/ppermute | solution.py:107
  400.5 42.7 %collective-permute-start.21 = (bf16[128,2048]{1,0:T(8,128)(2,1)S(1)}, bf16[128,2048]{1,0:T(8,128)(2,1)S(1)}, u32[]{:S(2)}, u32[]{:S(2)}) collective-permute-start(bf16[128,2048]{1,0:T(8,128)(2,1)S(1)} %multiply_convert_fusion.22), channel_id=1, source_target_pairs={{0,24},{8,16},{16,8},{24,0},{1,25},{9,17},{17,9},{25,1},{2,26},{10... | collective-permute-start | bytes 1572872 | tf_op jit(solution)/shard_map/ppermute | solution.py:140
  403.8 50.4 %collective-permute-start.9 = (bf16[256,2048]{1,0:T(8,128)(2,1)S(1)}, bf16[256,2048]{1,0:T(8,128)(2,1)S(1)}, u32[]{:S(2)}, u32[]{:S(2)}) collective-permute-start(bf16[256,2048]{1,0:T(8,128)(2,1)S(1)} %pad_maximum_fusion.26), channel_id=1, source_target_pairs={{0,4},{1,3},{2,6},{3,1},{4,0},{5,7},{6,2},{7,5},{8,12},{9,11},{10,... | collective-permute-start | bytes 3145736 | tf_op jit(solution)/shard_map/ppermute | solution.py:107
  454.4 39.2 %collective-permute-start.10 = (bf16[512,2048]{1,0:T(8,128)(2,1)S(1)}, bf16[512,2048]{1,0:T(8,128)(2,1)S(1)}, u32[]{:S(2)}, u32[]{:S(2)}) collective-permute-start(bf16[512,2048]{1,0:T(8,128)(2,1)S(1)} %pad_maximum_fusion.15), channel_id=1, source_target_pairs={{0,1},{1,0},{2,3},{3,2},{4,5},{5,4},{6,7},{7,6},{8,9},{9,8},{10,11... | collective-permute-start | bytes 6291464 | tf_op jit(solution)/shard_map/ppermute | solution.py:111
  668.7 81.4 %collective-permute-start.31 = (bf16[128,2048]{1,0:T(8,128)(2,1)}, bf16[128,2048]{1,0:T(8,128)(2,1)}, u32[]{:S(2)}, u32[]{:S(2)}) collective-permute-start(bf16[128,2048]{1,0:T(8,128)(2,1)} %slice_add_fusion.9), channel_id=1, source_target_pairs={{0,8},{8,0},{16,24},{24,16},{1,9},{9,1},{17,25},{25,17},{2,10},{10... | collective-permute-start | bytes 1572872 | tf_op jit(solution)/shard_map/ppermute | solution.py:140
  676.5 73.6 %collective-permute-start.33 = (bf16[128,2048]{1,0:T(8,128)(2,1)}, bf16[128,2048]{1,0:T(8,128)(2,1)}, u32[]{:S(2)}, u32[]{:S(2)}) collective-permute-start(bf16[128,2048]{1,0:T(8,128)(2,1)} %fusion.153), channel_id=1, source_target_pairs={{0,16},{8,24},{16,0},{24,8},{1,17},{9,25},{17,1},{25,9},{2,18},{10... | collective-permute-start | bytes 1572872 | tf_op jit(solution)/shard_map/ppermute | solution.py:140
  815.3 94.1 %collective-permute-start.44 = (bf16[512,1408]{1,0:T(8,128)(2,1)}, bf16[512,1408]{1,0:T(8,128)(2,1)S(1)}, u32[]{:S(2)}, u32[]{:S(2)}) collective-permute-start(bf16[512,1408]{1,0:T(8,128)(2,1)} %dynamic-slice_bitcast_fusion.7), channel_id=1, source_target_pairs={{0,16},{8,24},{16,0},{24,8},{1,17},{9,25},{17,1},{25,9},{2,18},{10... | collective-permute-start | bytes 4325384 | tf_op jit(solution)/shard_map/ppermute | solution.py:140
  815.3 94.1 %collective-permute-start.43 = (bf16[352,2048]{1,0:T(8,128)(2,1)}, bf16[352,2048]{1,0:T(8,128)(2,1)}, u32[]{:S(2)}, u32[]{:S(2)}) collective-permute-start(bf16[352,2048]{1,0:T(8,128)(2,1)} %select_convert_fusion), channel_id=1, source_target_pairs={{0,8},{8,0},{16,24},{24,16},{1,9},{9,1},{17,25},{25,17},{2,10},{10... | collective-permute-start | bytes 4325384 | tf_op jit(solution)/shard_map/ppermute | solution.py:140
  844.6 86.2 %collective-permute-start.57 = (bf16[128,2048]{1,0:T(8,128)(2,1)S(1)}, bf16[128,2048]{1,0:T(8,128)(2,1)}, u32[]{:S(2)}, u32[]{:S(2)}) collective-permute-start(bf16[128,2048]{1,0:T(8,128)(2,1)S(1)} %copy-done.31), channel_id=1, source_target_pairs={{0,2},{1,5},{2,0},{3,7},{4,6},{5,1},{6,4},{7,3},{8,10},{9,13},{10,... | collective-permute-start | bytes 1572872 | tf_op jit(solution)/shard_map/ppermute | solution.py:107
  852.4 183.9 %collective-permute-start.40 = (bf16[512,2048]{1,0:T(8,128)(2,1)}, bf16[512,2048]{1,0:T(8,128)(2,1)}, u32[]{:S(2)}, u32[]{:S(2)}) collective-permute-start(bf16[512,2048]{1,0:T(8,128)(2,1)} %slice.552), channel_id=1, source_target_pairs={{0,1},{1,0},{2,3},{3,2},{4,5},{5,4},{6,7},{7,6},{8,9},{9,8},{10,11... | collective-permute-start | bytes 6291464 | tf_op jit(solution)/shard_map/ppermute | solution.py:111
  928.7 53.2 %collective-permute-start.49 = (bf16[512,512]{1,0:T(8,128)(2,1)}, bf16[512,512]{1,0:T(8,128)(2,1)}, u32[]{:S(2)}, u32[]{:S(2)}) collective-permute-start(bf16[512,512]{1,0:T(8,128)(2,1)} %bitcast.586), channel_id=1, source_target_pairs={{0,16},{8,24},{16,0},{24,8},{1,17},{9,25},{17,1},{25,9},{2,18},{10... | collective-permute-start | bytes 1572872 | tf_op jit(solution)/shard_map/ppermute | solution.py:140
  930.8 51.1 %collective-permute-start.50 = (bf16[512,512]{1,0:T(8,128)(2,1)}, bf16[512,512]{1,0:T(8,128)(2,1)}, u32[]{:S(2)}, u32[]{:S(2)}) collective-permute-start(bf16[512,512]{1,0:T(8,128)(2,1)} %bitcast.588), channel_id=1, source_target_pairs={{0,24},{8,16},{16,8},{24,0},{1,25},{9,17},{17,9},{25,1},{2,26},{10... | collective-permute-start | bytes 1572872 | tf_op jit(solution)/shard_map/ppermute | solution.py:140
  941.4 88.1 %collective-permute-start.58 = (bf16[256,2048]{1,0:T(8,128)(2,1)}, bf16[256,2048]{1,0:T(8,128)(2,1)}, u32[]{:S(2)}, u32[]{:S(2)}) collective-permute-start(bf16[256,2048]{1,0:T(8,128)(2,1)} %pad_maximum_fusion.31), channel_id=1, source_target_pairs={{0,4},{1,3},{2,6},{3,1},{4,0},{5,7},{6,2},{7,5},{8,12},{9,11},{10,... | collective-permute-start | bytes 3145736 | tf_op jit(solution)/shard_map/ppermute | solution.py:107
  989.9 99.0 %collective-permute-start.64 = (bf16[512,1408]{1,0:T(8,128)(2,1)}, bf16[512,1408]{1,0:T(8,128)(2,1)}, u32[]{:S(2)}, u32[]{:S(2)}) collective-permute-start(bf16[512,1408]{1,0:T(8,128)(2,1)} %get-tuple-element.227), channel_id=1, source_target_pairs={{0,8},{8,0},{16,24},{24,16},{1,9},{9,1},{17,25},{25,17},{2,10},{10... | collective-permute-start | bytes 4325384 | tf_op jit(solution)/shard_map/ppermute | solution.py:140
  1001.5 87.5 %collective-permute-start.65 = (bf16[512,1408]{1,0:T(8,128)(2,1)}, bf16[512,1408]{1,0:T(8,128)(2,1)}, u32[]{:S(2)}, u32[]{:S(2)}) collective-permute-start(bf16[512,1408]{1,0:T(8,128)(2,1)} %get-tuple-element.226), channel_id=1, source_target_pairs={{0,24},{8,16},{16,8},{24,0},{1,25},{9,17},{17,9},{25,1},{2,26},{10... | collective-permute-start | bytes 4325384 | tf_op jit(solution)/shard_map/ppermute | solution.py:140
  1021.6 67.3 %all-to-all-start.6 = ((bf16[32,64,176]{2,1,0:T(8,128)(2,1)}), bf16[32,64,176]{2,1,0:T(8,128)(2,1)}, u32[]{:S(2)}, u32[]{:S(2)}) async-start(bf16[32,64,176]{2,1,0:T(8,128)(2,1)} %bitcast.532), calls=%async_computation.7 | async-start | bytes 2097152 | tf_op jit(solution)/shard_map/all_to_all | solution.py:501
  1032.4 100.3 %collective-permute-start.59 = (bf16[512,2048]{1,0:T(8,128)(2,1)}, bf16[512,2048]{1,0:T(8,128)(2,1)}, u32[]{:S(2)}, u32[]{:S(2)}) collective-permute-start(bf16[512,2048]{1,0:T(8,128)(2,1)} %pad_maximum_fusion.19), channel_id=1, source_target_pairs={{0,1},{1,0},{2,3},{3,2},{4,5},{5,4},{6,7},{7,6},{8,9},{9,8},{10,11... | collective-permute-start | bytes 6291464 | tf_op jit(solution)/shard_map/ppermute | solution.py:111
  1040.7 89.5 %collective-permute-start.41 = (bf16[256,2048]{1,0:T(8,128)(2,1)}, bf16[256,2048]{1,0:T(8,128)(2,1)}, u32[]{:S(2)}, u32[]{:S(2)}) collective-permute-start(bf16[256,2048]{1,0:T(8,128)(2,1)} %slice.799), channel_id=1, source_target_pairs={{0,4},{1,3},{2,6},{3,1},{4,0},{5,7},{6,2},{7,5},{8,12},{9,11},{10,... | collective-permute-start | bytes 3145736 | tf_op jit(solution)/shard_map/ppermute | solution.py:107
  1050.2 42.9 %collective-permute-start.53 = (bf16[512,576]{0,1:T(8,128)(2,1)}, bf16[512,576]{0,1:T(8,128)(2,1)}, u32[]{:S(2)}, u32[]{:S(2)}) collective-permute-start(bf16[512,576]{0,1:T(8,128)(2,1)} %pad_maximum_fusion.34), channel_id=1, source_target_pairs={{0,1},{1,0},{2,3},{3,2},{4,5},{5,4},{6,7},{7,6},{8,9},{9,8},{10,11... | collective-permute-start | bytes 1769480 | tf_op jit(solution)/shard_map/ppermute | solution.py:111
  1157.9 47.9 %collective-permute-start.63 = (f32[64,2048]{1,0:T(8,128)}, f32[64,2048]{1,0:T(8,128)}, u32[]{:S(2)}, u32[]{:S(2)}) collective-permute-start(f32[64,2048]{1,0:T(8,128)} %fusion.170), channel_id=1, source_target_pairs={{0,0},{1,4},{2,8},{3,12},{4,16},{5,20},{6,24},{7,28},{8,1},{9,5},{... | collective-permute-start | bytes 1572872 | tf_op jit(solution)/shard_map/ppermute | solution.py:510
  1165.6 39.1 %all-to-all-start.4 = ((f32[32,1,144]{2,1,0:T(1,128)}), f32[32,1,144]{2,1,0:T(1,128)S(1)}, u32[]{:S(2)}, u32[]{:S(2)}) async-start(f32[32,1,144]{2,1,0:T(1,128)} %all_to_all.63), calls=%async_computation.5 | async-start | bytes 65536 | tf_op jit(solution)/shard_map/all_to_all | solution.py:580
  (246 other events, 3560.0 us)
Sparse Core Ops, SparseCore 0:
  13.2 91.3 all-gather.8
  107.4 126.5 all-gather.4
  236.9 191.8 all-gather.6
  753.5 229.9 reduce-scatter.1

commit v5 on v4

--- a/solution.py
+++ b/solution.py
@@ -118,18 +118,23 @@
     return jnp.concatenate([current, core_swap(current, n_seq)], axis=0)
 
 
-def seq_scatter(values, n_seq):
+def seq_scatter(make_half, n_seq):
+    sent = core_swap(make_half(1).astype(BF16), n_seq)
+    kept = make_half(0)
     stages = []
+    for step in reversed(range(len(link_orders(n_seq)[0]))):
+        half = sent.shape[0] // 2
+        onward = (kept[half:].astype(F32) + sent[half:].astype(F32)).astype(BF16)
+        kept = kept[:half].astype(F32) + sent[:half].astype(F32)
+        stages.append(kept)
+        sent = seq_step(onward, n_seq, step)
+    stages.append(kept + sent.astype(F32))
+    return stages
+
+
+def half_of(values, part):
     half = values.shape[0] // 2
-    values = values.astype(BF16)
-    total = values[:half].astype(F32) + core_swap(values[half:], n_seq).astype(F32)
-    stages.append(total)
-    for step in reversed(range(len(link_orders(n_seq)[0]))):
-        half = total.shape[0] // 2
-        sent = seq_step(total[half:].astype(BF16), n_seq, step)
-        total = total[:half] + sent.astype(F32)
-        stages.append(total)
-    return stages
+    return values[part * half : (part + 1) * half]
 
 
 def hold(value, *until):
@@ -156,11 +161,6 @@
     for step in range(n_dp):
         result = lax.dynamic_update_index_in_dim(result, moved[step], dp_index ^ step, 0)
     return result
-
-
-def dp_gather(values, n_dp, dp_index):
-    moved = [values] + [dp_swap(values, n_dp, step) for step in range(1, n_dp)]
-    return in_order(moved, n_dp, dp_index)
 
 
 def dp_scatter(values, n_dp, dp_index):
@@ -253,18 +253,45 @@
     def absolute(values):
         return jnp.take(values, block_of, axis=0, mode="clip")
 
+    ff_width = expert_gate_up.shape[2] // 2
+    ff_part = ff_width // ff_parts
+    expert_rows = expert_gate_up.shape[0]
+    in_parts = expert_gate_up.reshape(expert_rows, per_device, 2, ff_parts, ff_part)
+    in_parts = jnp.transpose(in_parts, (3, 1, 0, 2, 4)).reshape(n_dp, expert_rows, 2 * ff_part)
+    down_kept = lax.dynamic_index_in_dim(expert_down, expert_bit, 1, keepdims=False)
+    down_sent = lax.dynamic_index_in_dim(expert_down, 1 - expert_bit, 1, keepdims=False)
+    is_low = expert_bit == 0
+
+    units = shared_down.shape[0]
+    shared_cols = shared_gate_up.reshape(down_rows, 2, n_dp, n_seq, units)
+    shared_cols = jnp.transpose(shared_cols, (0, 3, 2, 1, 4)).reshape(down_rows, n_seq, -1)
+
     up_rows = kv_up.reshape(kv_up.shape[0], n_seq, -1, kv_up.shape[0] * e_width // down_rows)
     up_rows = jnp.swapaxes(up_rows, 1, 2).reshape(down_rows, n_seq, -1)
-    joined = jnp.concatenate([q_weight.reshape(down_rows, n_seq, q_width), up_rows], axis=2)
-    joined_width = joined.shape[2]
+    joined_width = q_width + up_rows.shape[2]
+    joined = jnp.concatenate(
+        [q_weight.reshape(down_rows, n_seq, q_width), up_rows, shared_cols], axis=2
+    )
     joined = lax.all_to_all(joined, "seq", split_axis=1, concat_axis=0, tiled=True)
-    joined_here = joined
-    joined = joined.reshape(n_seq * down_rows, joined_width)
-    joined = dp_gather(joined, n_dp, dp_index).reshape(-1, joined_width)
+    joined = joined.reshape(n_seq * down_rows, -1)
+    shared_parts = joined[:, joined_width:].reshape(-1, n_dp, 2 * units)
+    shared_parts = jnp.swapaxes(shared_parts, 0, 1)
+    joined = joined[:, :joined_width]
+    joined = [joined] + [dp_swap(joined, n_dp, step) for step in range(1, n_dp)]
+    joined = hold(joined, in_parts, down_kept, down_sent)
+    joined = in_order(joined, n_dp, dp_index).reshape(-1, joined_width)
     weight_q = joined[:, :q_width]
     weight_up = joined[:, q_width:].reshape(KV_RANK, e_width)
 
     hidden_group = seq_gather(hidden, n_seq)
+    ready = joined
+    in_parts = jnp.concatenate([in_parts, shared_parts], axis=2)
+    even_steps, odd_steps = range(2, n_dp, 2), range(1, n_dp, 2)
+    in_even = dp_exchange(in_parts, n_dp, dp_index, even_steps, ready)
+    down_got = dp_swap(hold(down_sent, ready), n_dp, 1)
+    in_odd = dp_exchange(in_parts, n_dp, dp_index, odd_steps, in_even)
+    in_moved = in_even | in_odd
+    in_moved[0] = dp_block(in_parts, dp_index)
 
     labels = jnp.arange(experts, dtype=jnp.int32)
     hits = jnp.sum((expert_ids[:, :, None] == labels).astype(jnp.int32), axis=1)
@@ -301,31 +328,8 @@
     slot_code = routing[:, :, 0] * 16 + routing[:, :, 1]
     gate_of = (routing[:, :, 2] * 128 + routing[:, :, 3]).astype(F32) / GATE_UNIT
 
-    weight_out = lax.all_gather(hold(out_weight, joined_here), BOTH, axis=0, tiled=True)
-    cot_all = lax.all_gather(hold(cotangent, joined, hidden_group), BOTH, axis=0, tiled=True)
-
-    ff_width = expert_gate_up.shape[2] // 2
-    ff_part = ff_width // ff_parts
-    expert_rows = expert_gate_up.shape[0]
-    in_parts = expert_gate_up.reshape(expert_rows, per_device, 2, ff_parts, ff_part)
-    in_parts = jnp.transpose(in_parts, (3, 1, 0, 2, 4)).reshape(n_dp, expert_rows, 2 * ff_part)
-    even_steps, odd_steps = range(2, n_dp, 2), range(1, n_dp, 2)
-    in_even = dp_exchange(in_parts, n_dp, dp_index, even_steps, joined)
-    in_odd = dp_exchange(in_parts, n_dp, dp_index, odd_steps, in_even)
-    in_moved = in_even | in_odd
-    in_moved[0] = dp_block(in_parts, dp_index)
-    down_kept = lax.dynamic_index_in_dim(expert_down, expert_bit, 1, keepdims=False)
-    down_sent = lax.dynamic_index_in_dim(expert_down, 1 - expert_bit, 1, keepdims=False)
-    down_got = dp_swap(hold(down_sent, joined), n_dp, 1)
-    is_low = expert_bit == 0
-
-    units = shared_down.shape[0]
-    gate_up_parts = shared_gate_up.reshape(-1, 2, n_all, units)
-    gate_up_parts = jnp.transpose(gate_up_parts, (2, 0, 1, 3)).reshape(n_all, -1, 2 * units)
-    gate_up_parts = hold(gate_up_parts, joined_here)
-    weight_shared_in = lax.all_to_all(
-        gate_up_parts, BOTH, split_axis=0, concat_axis=0, tiled=True
-    ).reshape(-1, 2 * units)
+    weight_out = lax.all_gather(hold(out_weight, joined, hidden_group), BOTH, axis=0, tiled=True)
+    cot_all = lax.all_gather(hold(cotangent, joined, hidden_group, spread), BOTH, axis=0, tiled=True)
 
     def chunk_gather(values):
         far = hold(values, in_odd)
@@ -401,15 +405,26 @@
     shared_act_grad = contract(cot_rows, shared_down, 2, 1)
 
     ffn_chunks = chunk_gather(normed_ffn)
+    chunk_places, kept_rows = [], []
+    for step in range(n_dp):
+        codes = relative(dp_block(slot_code, dp_index ^ step)).reshape(group)
+        placed = lax.optimization_barrier((codes[:, None] == slots).astype(BF16))
+        if step == 1:
+            placed = hold(placed, slot_cot, shared_act_grad)
+        chunk_places.append(placed)
+        kept_rows.append(lead_dot(placed, ffn_chunks[step]).astype(BF16))
+
+    in_moved = hold([in_moved[step] for step in range(n_dp)], kept_rows[0])
+    weight_in = in_order([piece[:, : 2 * ff_part] for piece in in_moved], n_dp, dp_index)
+    weight_in = weight_in.reshape(-1, 2 * ff_part)
+    weight_shared_in = in_order([piece[:, 2 * ff_part :] for piece in in_moved], n_dp, dp_index)
+    weight_shared_in = weight_shared_in.reshape(-1, 2 * units)
     shared_in_back = weight_shared_in.T
     grad_shared_in = 0.0
-    kept_rows, kept_cots, kept_acts, kept_grads = [], [], [], []
+    kept_cots, kept_acts, kept_grads = [], [], []
     kept_shared, shared_acts, spreads = [], [], []
     for step in range(n_dp):
         ffn_rows = ffn_chunks[step]
-        codes = relative(dp_block(slot_code, dp_index ^ step)).reshape(group)
-        placed = lax.optimization_barrier((codes[:, None] == slots).astype(BF16))
-
         shared_in = matmul(ffn_rows, weight_shared_in)
         shared_gate, shared_up = shared_in[:, :units], shared_in[:, units:]
         act_grad = dp_block(shared_act_grad, dp_index ^ step)
@@ -420,11 +435,8 @@
         kept_shared.append(shared_in_grad)
         shared_acts.append(swiglu(shared_gate, shared_up).astype(BF16))
 
-        kept_rows.append(lead_dot(placed, ffn_rows).astype(BF16))
-        spreads.append((placed, shared_in_grad))
-
-    in_moved = hold([in_moved[step] for step in range(n_dp)], kept_rows[0])
-    weight_in = in_order(in_moved, n_dp, dp_index).reshape(-1, 2 * ff_part)
+        spreads.append((chunk_places[step], shared_in_grad))
+
     for step in range(n_dp):
         expert_in = matmul(kept_rows[step], weight_in)
         expert_gate, expert_up = expert_in[:, :ff_part], expert_in[:, ff_part:]
@@ -443,24 +455,31 @@
         placed, shared_in_grad, slot_grad = spreads[step]
         for age in range(1, min(len(planes), 3) + 1):
             placed = hold(placed, planes[-age][age - 1])
-        dn_part = matmul(
-            jnp.concatenate([placed, shared_in_grad], axis=1),
-            jnp.concatenate([slot_grad, shared_in_back], axis=0),
-        ).astype(BF16)
-        planes.append(seq_scatter(dn_part, n_seq))
+        left_side = jnp.concatenate([placed, shared_in_grad], axis=1)
+        right_side = jnp.concatenate([slot_grad, shared_in_back], axis=0)
+        planes.append(seq_scatter(lambda part: matmul(half_of(left_side, part), right_side), n_seq))
         if step:
             sums.append(dp_swap(planes[-1][-1].astype(BF16), n_dp, step).astype(F32))
         else:
             sums.append(planes[-1][-1])
     ffn_grad = sum(sums[1:], sums[0])
 
-    kept_rows, kept_cots, kept_acts, kept_grads, shared_acts, ffn_chunks = hold(
-        (kept_rows, kept_cots, kept_acts, kept_grads, shared_acts, ffn_chunks), dn_part
+    from_norm, gain_ffn_grad = rms_back(residual, gain_ffn, ffn_grad)
+    residual_grad = cotangent.astype(F32) + from_norm
+    residual_low = residual_grad.astype(BF16)
+    heads_grad = tail_dot(residual_low, weight_out).astype(BF16)
+    heads_grad_own = heads_grad
+    heads_grad = heads_grad.reshape(tokens, n_seq, heads * VD)
+    heads_grad = lax.all_to_all(heads_grad, "seq", split_axis=1, concat_axis=0, tiled=True)
+
+    out_acts, shared_acts = hold((kept_acts, shared_acts), planes[-1][0])
+    kept_rows, kept_cots, kept_acts, kept_grads, ffn_chunks = hold(
+        (kept_rows, kept_cots, kept_acts, kept_grads, ffn_chunks), heads_grad_own
     )
     grad_in = lead_dot(jnp.concatenate(kept_rows), jnp.concatenate(kept_grads)).astype(BF16)
     back_parts = grad_in.reshape(n_dp, expert_rows, 2 * ff_part)
     back_even = dp_exchange(back_parts, n_dp, dp_index, even_steps, ffn_grad)
-    expert_act = in_order(kept_acts, n_dp, dp_index)
+    expert_act = in_order(out_acts, n_dp, dp_index)
     grad_back = lead_dot(jnp.concatenate(kept_acts), jnp.concatenate(kept_cots))
     half = expert_down.shape[0]
     low_half, high_half = grad_back[:half], grad_back[half:]
@@ -486,16 +505,11 @@
         tiled=True,
     )
     output = (residual + out_sum.astype(F32)).astype(BF16)
-    grad_shared_down = lead_dot(shared_act.reshape(n_all * tokens, units), cot_all)
+    shared_late = hold(shared_act, heads_grad_own).reshape(n_all * tokens, units)
+    grad_shared_down = lead_dot(shared_late, cot_all)
     for step in range(n_dp):
         grad_shared_in = grad_shared_in + lead_dot(ffn_chunks[step], kept_shared[step])
 
-    from_norm, gain_ffn_grad = rms_back(residual, gain_ffn, ffn_grad)
-    residual_grad = cotangent.astype(F32) + from_norm
-    residual_low = residual_grad.astype(BF16)
-    heads_grad = tail_dot(residual_low, weight_out).astype(BF16)
-    heads_grad = heads_grad.reshape(tokens, n_seq, heads * VD)
-    heads_grad = lax.all_to_all(heads_grad, "seq", split_axis=1, concat_axis=0, tiled=True)
     residual_group = seq_gather(hold(residual_low, heads_grad), n_seq)
     grad_shared_in = hold(grad_shared_in.astype(BF16), heads_grad)
     shared_back = lax.all_to_all(
@@ -531,13 +545,23 @@
         [key_grad[..., :NOPE].astype(BF16), value_grad], axis=-1
     ).reshape(group, e_width)
 
-    expand_low = hold(expand_low, grad_got, back_even)
-    latent_part = tail_dot(expand_low, weight_up)
-    latent_sum = seq_scatter(jnp.concatenate([latent_part, rope_grad], axis=1), n_seq)[-1]
-    normed_sum = seq_scatter(tail_dot(query_low, weight_q), n_seq)[-1]
+    expand_low, rope_grad = hold((expand_low, rope_grad), shared_back)
+    latent_sum = seq_scatter(
+        lambda part: jnp.concatenate(
+            [tail_dot(half_of(expand_low, part), weight_up), half_of(rope_grad, part)], axis=1
+        ),
+        n_seq,
+    )[-1]
+    normed_low = [tail_dot(half_of(query_low, part), weight_q).astype(BF16) for part in (0, 1)]
+    normed_sum = seq_scatter(lambda part: normed_low[part], n_seq)[-1]
+    unit_rows = rows_group * rms_scale(rows_group)
+    gain_attn_grad = sum(
+        jnp.sum(normed_low[part].astype(F32) * half_of(unit_rows, part), axis=0) for part in (0, 1)
+    )
     grad_q = lead_dot(normed_group, query_low)
     grad_up = lead_dot(latent, expand_low).reshape(width, -1)
-    grad_joined = dp_scatter(jnp.concatenate([grad_q, grad_up], axis=1), n_dp, dp_index)
+    grad_joined = hold(jnp.concatenate([grad_q, grad_up], axis=1), back_even, grad_got)
+    grad_joined = dp_scatter(grad_joined, n_dp, dp_index)
     back_odd = dp_exchange(back_parts, n_dp, dp_index, odd_steps, grad_joined)
     grad_joined = grad_joined.reshape(n_seq, down_rows, joined_width)
     grad_joined = lax.all_to_all(grad_joined, "seq", split_axis=0, concat_axis=0, tiled=True)
@@ -565,10 +589,11 @@
     shared_back = shared_back.reshape(n_all, -1, 2, units).astype(F32)
     grad_shared_gate_up = jnp.transpose(shared_back, (1, 2, 0, 3)).reshape(shared_gate_up.shape)
 
-    normed_grad = normed_sum + tail_dot(down_low, weight_down)
-    rows_from_norm, gain_attn_grad = rms_back(rows, gain_attn, normed_grad)
+    down_grad = tail_dot(down_low, weight_down)
+    rows_from_norm, _ = rms_back(rows, gain_attn, normed_sum + down_grad)
     input_grad = residual_grad + rows_from_norm
 
+    gain_attn_grad = gain_attn_grad + jnp.sum(down_grad * rows * rms_scale(rows), axis=0)
     gain_grads = jnp.concatenate(
         [
             gain_attn_grad.reshape(n_all, -1),

time: 1230 us -> 1250 us (1.016)
  waiting for transfers between devices: 449 us -> 391 us
  starting transfers between devices: 154 us -> 200 us
  matrix products: 215 us -> 238 us
  local copies, waits for them, and re-layouts: 236 us -> 253 us
  blocking collectives: 13.4 us -> 0 us
    all_to_all x1, waiting for transfers between devices: 86.8 us -> 4.88 us  [body(): lax.all_to_all(joined, 'seq', split_axis=1, concat_axis=0, tiled=True)]
    all_to_all x1, waiting for transfers between devices: 38.2 us -> 72.6 us  [body(): lax.all_to_all(grad_shared_in.reshape(n_all, -1, 2 * units), BOTH, split_...]
    dot_general x49 -> x55, matrix products: 175 us -> 200 us  [contract(): lax.dot_general(left_side, right_side, (((left_dim,), (right_dim,)), ((),...]
    add x14 -> x3, other arithmetic: 25.6 us -> 2.08 us  [the longest x2 2.07 us: seq_scatter(): stages.append(kept + sent.astype(F32))]
    broadcast_in_dim x4 -> x20, local copies, waits for them, and re-layouts: 5.39 us -> 27.6 us  [in_order(): lax.dynamic_update_index_in_dim(result, moved[step], dp_index ^ step, 0)]
    ppermute x26, waiting for transfers between devices: 60.7 us -> 82.6 us  [seq_step(): lax.ppermute(values, 'seq', [(s, s ^ orders[s & 1][step]) for s in range(...]
    dynamic_update_slice x16 -> x20, local copies, waits for them, and re-layouts: 7.9 us -> 26.9 us  [in_order(): lax.dynamic_update_index_in_dim(result, moved[step], dp_index ^ step, 0)]
    convert_element_type x1 -> x12, other arithmetic: 2.9 us -> 21.5 us  [seq_scatter(): onward = (kept[half:].astype(F32) + sent[half:].astype(F32)).astype(BF16)]
  transfers between devices with their start and end apart: 76 -> 76, of which waited for: 24 -> 27; matrix products, arithmetic and copies ran while one was open for 39% -> 42% of each run, Pallas kernels for 1% -> 1%
where the time goes in v5:
time: 1250 us; the launch traced here: 1240 us
  waiting for transfers between devices  391 us (31%)
  local copies, waits for them, and re-layouts  253 us (20%)
  matrix products  238 us (19%)
  starting transfers between devices  200 us (16%)
  other arithmetic  126 us (10%)
  between operations  17.9 us (1%)
    ppermute x26, waiting for transfers between devices, dp_swap(): return lax.ppermute(values, 'dp', [(d, d ^ step) for d in range(n_dp)])  216 us
    dot_general x55, matrix products, contract(): lax.dot_general(left_side, right_side, (((left_dim,), (right_dim,)), ((),...  200 us
    ppermute x26, waiting for transfers between devices, seq_step(): lax.ppermute(values, 'seq', [(s, s ^ orders[s & 1][step]) for s in range(...  82.6 us
    all_to_all x1, waiting for transfers between devices, body(): lax.all_to_all(grad_shared_in.reshape(n_all, -1, 2 * units), BOTH, split_...  72.6 us
    ppermute x26, starting transfers between devices, dp_swap(): return lax.ppermute(values, 'dp', [(d, d ^ step) for d in range(n_dp)])  67.8 us
    unnamed x462, local copies, waits for them, and re-layouts  62 us
    ppermute x13, starting transfers between devices, core_swap(): return lax.ppermute(values, 'seq', [(s, s ^ 1) for s in range(n_seq)])  39.8 us
    ppermute x26, starting transfers between devices, seq_step(): lax.ppermute(values, 'seq', [(s, s ^ orders[s & 1][step]) for s in range(...  34.5 us
  transfers between devices with their start and end apart: 76, of which 27 were waited for; matrix products, arithmetic and copies ran while one was open for 42% of the time, Pallas kernels for 1%

profile of v5, /device:TPU:25, one launch (start us, length us, event | category | flops | bytes accessed | tf_op | source)
XLA Modules:
  0.0 1235.6 jit_solution(3906279023552375263)
XLA Ops:
  14.4 7.3 collective-permute-done
  62.0 14.8 %copy.304 = bf16[512,2,2816]{0,2,1:T(8,128)(2,1)} copy(bf16[512,2,2816]{2,1,0:T(2,128)(2,1)} %param.29) | data formatting | bytes 11534336 | tf_op args[11]
  89.7 11.6 collective-permute-done.5
  119.8 12.6 %collective-permute-start.6 = (bf16[512,1584]{0,1:T(8,128)(2,1)}, bf16[512,1584]{0,1:T(8,128)(2,1)S(1)}, u32[]{:S(2)}, u32[]{:S(2)}) collective-permute-start(bf16[512,1584]{0,1:T(8,128)(2,1)} %dynamic-slice_bitcast_fusion.2), channel_id=1, source_target_pairs={{0,16},{8,24},{16,0},{24,8},{1,17},{9,25},{17,1},{25,9},{2,18},{10... | collective-permute-start | bytes 4866056 | tf_op jit(solution)/shard_map/ppermute | solution.py:145
  141.8 76.8 %collective-permute-done.6 = bf16[512,1584]{0,1:T(8,128)(2,1)S(1)} collective-permute-done((bf16[512,1584]{0,1:T(8,128)(2,1)}, bf16[512,1584]{0,1:T(8,128)(2,1)S(1)}, u32[]{:S(2)}, u32[]{:S(2)}) %collective-permute-start.6) | collective-permute-done | bytes 1622048 | tf_op jit(solution)/shard_map/ppermute | solution.py:145
  247.9 7.7 fusion.298
  284.3 45.1 %collective-permute-done.12 = bf16[512,1584]{0,1:T(8,128)(2,1)} collective-permute-done((bf16[512,1584]{0,1:T(8,128)(2,1)}, bf16[512,1584]{0,1:T(8,128)(2,1)}, u32[]{:S(2)}, u32[]{:S(2)}) %collective-permute-start.12) | collective-permute-done | bytes 1622048 | tf_op jit(solution)/shard_map/ppermute | solution.py:145
  337.8 26.7 %collective-permute-done.13 = bf16[128,2048]{1,0:T(8,128)(2,1)S(1)} collective-permute-done((bf16[128,2048]{1,0:T(8,128)(2,1)S(1)}, bf16[128,2048]{1,0:T(8,128)(2,1)S(1)}, u32[]{:S(2)}, u32[]{:S(2)}) %collective-permute-start.13) | collective-permute-done | bytes 524320 | tf_op jit(solution)/shard_map/ppermute | solution.py:145
  366.1 15.3 %collective-permute-done.21 = bf16[128,2048]{1,0:T(8,128)(2,1)S(1)} collective-permute-done((bf16[128,2048]{1,0:T(8,128)(2,1)S(1)}, bf16[128,2048]{1,0:T(8,128)(2,1)S(1)}, u32[]{:S(2)}, u32[]{:S(2)}) %collective-permute-start.21) | collective-permute-done | bytes 524320 | tf_op jit(solution)/shard_map/ppermute | solution.py:145
  393.9 25.4 %collective-permute-start.10 = (bf16[512,2048]{1,0:T(8,128)(2,1)S(1)}, bf16[512,2048]{1,0:T(8,128)(2,1)S(1)}, u32[]{:S(2)}, u32[]{:S(2)}) collective-permute-start(bf16[512,2048]{1,0:T(8,128)(2,1)S(1)} %pad_maximum_fusion.11), channel_id=1, source_target_pairs={{0,1},{1,0},{2,3},{3,2},{4,5},{5,4},{6,7},{7,6},{8,9},{9,8},{10,11... | collective-permute-start | bytes 6291464 | tf_op jit(solution)/shard_map/ppermute | solution.py:111
  421.0 22.5 %collective-permute-done.19 = bf16[256,2048]{1,0:T(8,128)(2,1)S(1)} collective-permute-done((bf16[256,2048]{1,0:T(8,128)(2,1)S(1)}, bf16[256,2048]{1,0:T(8,128)(2,1)S(1)}, u32[]{:S(2)}, u32[]{:S(2)}) %collective-permute-start.19) | collective-permute-done | bytes 1048608 | tf_op jit(solution)/shard_map/ppermute | solution.py:107
  444.9 16.6 %collective-permute-done.23 = bf16[256,2048]{1,0:T(8,128)(2,1)S(1)} collective-permute-done((bf16[256,2048]{1,0:T(8,128)(2,1)S(1)}, bf16[256,2048]{1,0:T(8,128)(2,1)S(1)}, u32[]{:S(2)}, u32[]{:S(2)}) %collective-permute-start.23) | collective-permute-done | bytes 1048608 | tf_op jit(solution)/shard_map/ppermute | solution.py:107
  549.3 11.0 fusion.210
  689.1 6.4 collective-permute-start.31
  699.7 9.2 collective-permute-start.32
  736.8 9.1 multiply_convert_fusion
  749.5 16.6 %convolution_convert_fusion = bf16[4,1024,2048]{2,1,0:T(8,128)(2,1)} fusion(bf16[4,88,2048]{2,1,0:T(8,128)(2,1)} %broadcast_in_dim.238, bf16[4,384,2048]{2,1,0:T(8,128)(2,1)} %multiply_convert_fusion, bf16[4,1024,88]{1,2,0:T(8,128)(2,1)S(1)} %reshape.738, bf16[4,1024,384]{1,2,0:T(8,128)(2,1)} %compare_convert_fusion), kind=kOutput, calls=%fused_computation.16 | convolution fusion | flops 7950434304 | bytes 28377088 | tf_op jit(solution)/shard_map/gtk,gkd->gtd/dot_general | solution.py:493
  788.5 6.4 convolution_convert_fusion.16
  807.5 12.6 %convolution_convert_fusion.1 = bf16[2048,1408]{1,0:T(8,128)(2,1)S(1)} fusion(bf16[384,2048]{1,0:T(8,128)(2,1)} %copy-done.205, bf16[384,2048]{1,0:T(8,128)(2,1)} %copy-done.204, bf16[384,2048]{1,0:T(8,128)(2,1)} %copy-done.206, bf16[384,2048]{1,0:T(8,128)(2,1)} %convolution_convert_fusion.15, bf16[384,1408]{1,0:T(8,128)(2,1)S(1)} %copy-done.116, ...), kind=kOutput, calls=%fused_computation.33 | convolution fusion | flops 8903720960 | bytes 16384000 | tf_op jit(solution)/shard_map/dot_general | solution.py:26
  836.1 9.7 fusion.308
  853.6 6.5 all-to-all-start.3
  893.8 72.6 %all-to-all-done.3 = bf16[32,64,176]{2,1,0:T(8,128)(2,1)} async-done(((bf16[32,64,176]{2,1,0:T(8,128)(2,1)}), bf16[32,64,176]{2,1,0:T(8,128)(2,1)}, u32[]{:S(2)}, u32[]{:S(2)}) %all-to-all-start.3) | async-done | bytes 720928 | tf_op jit(solution)/shard_map/all_to_all | solution.py:515
  979.4 6.3 reshape.749
  1016.3 12.6 %collective-permute-done.49 = bf16[512,512]{1,0:T(8,128)(2,1)} collective-permute-done((bf16[512,512]{1,0:T(8,128)(2,1)}, bf16[512,512]{1,0:T(8,128)(2,1)}, u32[]{:S(2)}, u32[]{:S(2)}) %collective-permute-start.49) | collective-permute-done | bytes 524320 | tf_op jit(solution)/shard_map/ppermute | solution.py:145
  1037.9 13.7 %collective-permute-start.64 = (bf16[512,1408]{1,0:T(8,128)(2,1)}, bf16[512,1408]{1,0:T(8,128)(2,1)}, u32[]{:S(2)}, u32[]{:S(2)}) collective-permute-start(bf16[512,1408]{1,0:T(8,128)(2,1)} %get-tuple-element.251), channel_id=1, source_target_pairs={{0,8},{8,0},{16,24},{24,16},{1,9},{9,1},{17,25},{25,17},{2,10},{10... | collective-permute-start | bytes 4325384 | tf_op jit(solution)/shard_map/ppermute | solution.py:145
  1054.7 6.3 all-to-all-start.5
  1068.3 9.5 collective-permute-done.45
  1106.1 9.9 collective-permute-done.65.refs_3_
  1127.2 7.0 copy.377
  1145.4 9.6 assemble.1
  1181.5 26.7 %all-to-all-start.4 = ((f32[32,1,144]{2,1,0:T(1,128)}), f32[32,1,144]{2,1,0:T(1,128)S(1)}, u32[]{:S(2)}, u32[]{:S(2)}) async-start(f32[32,1,144]{2,1,0:T(1,128)} %all_to_all.58), calls=%async_computation.5 | async-start | bytes 65536 | tf_op jit(solution)/shard_map/all_to_all | solution.py:605
  1208.3 14.3 %all-to-all-done.4 = f32[32,1,144]{2,1,0:T(1,128)S(1)} async-done(((f32[32,1,144]{2,1,0:T(1,128)}), f32[32,1,144]{2,1,0:T(1,128)S(1)}, u32[]{:S(2)}, u32[]{:S(2)}) %all-to-all-start.4) | async-done | bytes 18464 | tf_op jit(solution)/shard_map/all_to_all | solution.py:605
  (931 shorter events, 659.5 us)
Async XLA Ops:
  7.2 101.9 %all-gather.9.cloned.1.call-start = ((), (), s32[]{:S(2)}) async-start(), calls=%async_computation.10 | async-start | bytes 3379200 | tf_op jit(solution)/shard_map/all_gather | solution.py:318
  38.1 238.8 %all-gather.5.cloned.1.call-start = ((), (), s32[]{:S(2)}) async-start(), calls=%async_computation.7 | async-start | bytes 8650752 | tf_op jit(solution)/shard_map/all_gather | solution.py:331
  47.3 58.5 %collective-permute-start.2 = (bf16[512,2048]{1,0:T(8,128)(2,1)}, bf16[512,2048]{1,0:T(8,128)(2,1)S(1)}, u32[]{:S(2)}, u32[]{:S(2)}) collective-permute-start(bf16[512,2048]{1,0:T(8,128)(2,1)} %pad_maximum_fusion.10), channel_id=1, source_target_pairs={{0,1},{1,0},{2,3},{3,2},{4,5},{5,4},{6,7},{7,6},{8,9},{9,8},{10,11... | collective-permute-start | bytes 6291464 | tf_op jit(solution)/shard_map/ppermute | solution.py:111
  57.8 43.5 %collective-permute-start.5 = (bf16[512,512]{1,0:T(8,128)(2,1)}, bf16[512,512]{1,0:T(8,128)(2,1)}, u32[]{:S(2)}, u32[]{:S(2)}) collective-permute-start(bf16[512,512]{1,0:T(8,128)(2,1)} %slice.629), channel_id=1, source_target_pairs={{0,24},{8,16},{16,8},{24,0},{1,25},{9,17},{17,9},{25,1},{2,26},{10... | collective-permute-start | bytes 1572872 | tf_op jit(solution)/shard_map/ppermute | solution.py:145
  108.8 440.5 %all-gather.7.cloned.1.call-start = ((), (), s32[]{:S(2)}) async-start(), calls=%async_computation.8 | async-start | bytes 17301504 | tf_op jit(solution)/shard_map/all_gather | solution.py:332
  119.8 98.8 %collective-permute-start.6 = (bf16[512,1584]{0,1:T(8,128)(2,1)}, bf16[512,1584]{0,1:T(8,128)(2,1)S(1)}, u32[]{:S(2)}, u32[]{:S(2)}) collective-permute-start(bf16[512,1584]{0,1:T(8,128)(2,1)} %dynamic-slice_bitcast_fusion.2), channel_id=1, source_target_pairs={{0,16},{8,24},{16,0},{24,8},{1,17},{9,25},{17,1},{25,9},{2,18},{10... | collective-permute-start | bytes 4866056 | tf_op jit(solution)/shard_map/ppermute | solution.py:145
  140.3 119.9 %collective-permute-start.7 = (bf16[352,2048]{1,0:T(8,128)(2,1)}, bf16[352,2048]{1,0:T(8,128)(2,1)}, u32[]{:S(2)}, u32[]{:S(2)}) collective-permute-start(bf16[352,2048]{1,0:T(8,128)(2,1)} %get-tuple-element.86), channel_id=1, source_target_pairs={{0,8},{8,0},{16,24},{24,16},{1,9},{9,1},{17,25},{25,17},{2,10},{10... | collective-permute-start | bytes 4325384 | tf_op jit(solution)/shard_map/ppermute | solution.py:145
  223.0 61.3 %collective-permute-start.11 = (bf16[512,1584]{0,1:T(8,128)(2,1)}, bf16[512,1584]{0,1:T(8,128)(2,1)}, u32[]{:S(2)}, u32[]{:S(2)}) collective-permute-start(bf16[512,1584]{0,1:T(8,128)(2,1)} %get-tuple-element.237), channel_id=1, source_target_pairs={{0,8},{8,0},{16,24},{24,16},{1,9},{9,1},{17,25},{25,17},{2,10},{10... | collective-permute-start | bytes 4866056 | tf_op jit(solution)/shard_map/ppermute | solution.py:145
  223.3 106.2 %collective-permute-start.12 = (bf16[512,1584]{0,1:T(8,128)(2,1)}, bf16[512,1584]{0,1:T(8,128)(2,1)}, u32[]{:S(2)}, u32[]{:S(2)}) collective-permute-start(bf16[512,1584]{0,1:T(8,128)(2,1)} %get-tuple-element.236), channel_id=1, source_target_pairs={{0,24},{8,16},{16,8},{24,0},{1,25},{9,17},{17,9},{25,1},{2,26},{10... | collective-permute-start | bytes 4866056 | tf_op jit(solution)/shard_map/ppermute | solution.py:145
  267.3 956.4 %reduce-scatter.2.cloned.1.call-start = ((), (), s32[]{:S(2)}) async-start(), calls=%async_computation.9 | async-start | bytes 17301504 | tf_op jit(solution)/shard_map/reduce_scatter | solution.py:501
  282.8 53.3 %collective-permute-start.8 = (bf16[128,2048]{1,0:T(8,128)(2,1)S(1)}, bf16[128,2048]{1,0:T(8,128)(2,1)S(1)}, u32[]{:S(2)}, u32[]{:S(2)}) collective-permute-start(bf16[128,2048]{1,0:T(8,128)(2,1)S(1)} %multiply_convert_fusion.23), channel_id=1, source_target_pairs={{0,2},{1,5},{2,0},{3,7},{4,6},{5,1},{6,4},{7,3},{8,10},{9,13},{10,... | collective-permute-start | bytes 1572872 | tf_op jit(solution)/shard_map/ppermute | solution.py:107
  330.3 51.0 %collective-permute-start.21 = (bf16[128,2048]{1,0:T(8,128)(2,1)S(1)}, bf16[128,2048]{1,0:T(8,128)(2,1)S(1)}, u32[]{:S(2)}, u32[]{:S(2)}) collective-permute-start(bf16[128,2048]{1,0:T(8,128)(2,1)S(1)} %multiply_convert_fusion.23), channel_id=1, source_target_pairs={{0,24},{8,16},{16,8},{24,0},{1,25},{9,17},{17,9},{25,1},{2,26},{10... | collective-permute-start | bytes 1572872 | tf_op jit(solution)/shard_map/ppermute | solution.py:145
  336.2 57.5 %collective-permute-start.9 = (bf16[256,2048]{1,0:T(8,128)(2,1)S(1)}, bf16[256,2048]{1,0:T(8,128)(2,1)S(1)}, u32[]{:S(2)}, u32[]{:S(2)}) collective-permute-start(bf16[256,2048]{1,0:T(8,128)(2,1)S(1)} %pad_maximum_fusion.34), channel_id=1, source_target_pairs={{0,4},{1,3},{2,6},{3,1},{4,0},{5,7},{6,2},{7,5},{8,12},{9,11},{10,... | collective-permute-start | bytes 3145736 | tf_op jit(solution)/shard_map/ppermute | solution.py:107
  385.3 58.2 %collective-permute-start.19 = (bf16[256,2048]{1,0:T(8,128)(2,1)S(1)}, bf16[256,2048]{1,0:T(8,128)(2,1)S(1)}, u32[]{:S(2)}, u32[]{:S(2)}) collective-permute-start(bf16[256,2048]{1,0:T(8,128)(2,1)S(1)} %pad_maximum_fusion.36), channel_id=1, source_target_pairs={{0,4},{1,3},{2,6},{3,1},{4,0},{5,7},{6,2},{7,5},{8,12},{9,11},{10,... | collective-permute-start | bytes 3145736 | tf_op jit(solution)/shard_map/ppermute | solution.py:107
  389.9 71.6 %collective-permute-start.23 = (bf16[256,2048]{1,0:T(8,128)(2,1)S(1)}, bf16[256,2048]{1,0:T(8,128)(2,1)S(1)}, u32[]{:S(2)}, u32[]{:S(2)}) collective-permute-start(bf16[256,2048]{1,0:T(8,128)(2,1)S(1)} %pad_maximum_fusion.37), channel_id=1, source_target_pairs={{0,4},{1,3},{2,6},{3,1},{4,0},{5,7},{6,2},{7,5},{8,12},{9,11},{10,... | collective-permute-start | bytes 3145736 | tf_op jit(solution)/shard_map/ppermute | solution.py:107
  393.9 71.3 %collective-permute-start.10 = (bf16[512,2048]{1,0:T(8,128)(2,1)S(1)}, bf16[512,2048]{1,0:T(8,128)(2,1)S(1)}, u32[]{:S(2)}, u32[]{:S(2)}) collective-permute-start(bf16[512,2048]{1,0:T(8,128)(2,1)S(1)} %pad_maximum_fusion.11), channel_id=1, source_target_pairs={{0,1},{1,0},{2,3},{3,2},{4,5},{5,4},{6,7},{7,6},{8,9},{9,8},{10,11... | collective-permute-start | bytes 6291464 | tf_op jit(solution)/shard_map/ppermute | solution.py:111
  421.0 99.3 %collective-permute-start.16 = (bf16[512,2048]{1,0:T(8,128)(2,1)}, bf16[512,2048]{1,0:T(8,128)(2,1)}, u32[]{:S(2)}, u32[]{:S(2)}) collective-permute-start(bf16[512,2048]{1,0:T(8,128)(2,1)} %pad_maximum_fusion.12), channel_id=1, source_target_pairs={{0,1},{1,0},{2,3},{3,2},{4,5},{5,4},{6,7},{7,6},{8,9},{9,8},{10,11... | collective-permute-start | bytes 6291464 | tf_op jit(solution)/shard_map/ppermute | solution.py:111
  444.9 77.3 %collective-permute-start.20 = (bf16[512,2048]{1,0:T(8,128)(2,1)}, bf16[512,2048]{1,0:T(8,128)(2,1)}, u32[]{:S(2)}, u32[]{:S(2)}) collective-permute-start(bf16[512,2048]{1,0:T(8,128)(2,1)} %pad_maximum_fusion.13), channel_id=1, source_target_pairs={{0,1},{1,0},{2,3},{3,2},{4,5},{5,4},{6,7},{7,6},{8,9},{9,8},{10,11... | collective-permute-start | bytes 6291464 | tf_op jit(solution)/shard_map/ppermute | solution.py:111
  463.0 63.5 %collective-permute-start.24 = (bf16[512,2048]{1,0:T(8,128)(2,1)}, bf16[512,2048]{1,0:T(8,128)(2,1)}, u32[]{:S(2)}, u32[]{:S(2)}) collective-permute-start(bf16[512,2048]{1,0:T(8,128)(2,1)} %pad_maximum_fusion.14), channel_id=1, source_target_pairs={{0,1},{1,0},{2,3},{3,2},{4,5},{5,4},{6,7},{7,6},{8,9},{9,8},{10,11... | collective-permute-start | bytes 6291464 | tf_op jit(solution)/shard_map/ppermute | solution.py:111
  699.7 66.3 %collective-permute-start.32 = (bf16[128,2048]{1,0:T(8,128)(2,1)}, bf16[128,2048]{1,0:T(8,128)(2,1)}, u32[]{:S(2)}, u32[]{:S(2)}) collective-permute-start(bf16[128,2048]{1,0:T(8,128)(2,1)} %convert_add_fusion.1), channel_id=1, source_target_pairs={{0,8},{8,0},{16,24},{24,16},{1,9},{9,1},{17,25},{25,17},{2,10},{10... | collective-permute-start | bytes 1572872 | tf_op jit(solution)/shard_map/ppermute | solution.py:145
  709.0 57.1 %collective-permute-start.34 = (bf16[128,2048]{1,0:T(8,128)(2,1)}, bf16[128,2048]{1,0:T(8,128)(2,1)}, u32[]{:S(2)}, u32[]{:S(2)}) collective-permute-start(bf16[128,2048]{1,0:T(8,128)(2,1)} %add_convert_fusion.2), channel_id=1, source_target_pairs={{0,16},{8,24},{16,0},{24,8},{1,17},{9,25},{17,1},{25,9},{2,18},{10... | collective-permute-start | bytes 1572872 | tf_op jit(solution)/shard_map/ppermute | solution.py:145
  711.8 54.3 %collective-permute-start.37 = (bf16[128,2048]{1,0:T(8,128)(2,1)}, bf16[128,2048]{1,0:T(8,128)(2,1)}, u32[]{:S(2)}, u32[]{:S(2)}) collective-permute-start(bf16[128,2048]{1,0:T(8,128)(2,1)} %fusion.144), channel_id=1, source_target_pairs={{0,24},{8,16},{16,8},{24,0},{1,25},{9,17},{17,9},{25,1},{2,26},{10... | collective-permute-start | bytes 1572872 | tf_op jit(solution)/shard_map/ppermute | solution.py:145
  803.6 175.8 %collective-permute-start.47 = (bf16[352,2048]{1,0:T(8,128)(2,1)}, bf16[352,2048]{1,0:T(8,128)(2,1)}, u32[]{:S(2)}, u32[]{:S(2)}) collective-permute-start(bf16[352,2048]{1,0:T(8,128)(2,1)} %select_convert_fusion), channel_id=1, source_target_pairs={{0,8},{8,0},{16,24},{24,16},{1,9},{9,1},{17,25},{25,17},{2,10},{10... | collective-permute-start | bytes 4325384 | tf_op jit(solution)/shard_map/ppermute | solution.py:145
  823.9 155.5 %collective-permute-start.46 = (bf16[512,1408]{1,0:T(8,128)(2,1)}, bf16[512,1408]{1,0:T(8,128)(2,1)S(1)}, u32[]{:S(2)}, u32[]{:S(2)}) collective-permute-start(bf16[512,1408]{1,0:T(8,128)(2,1)} %dynamic-slice_bitcast_fusion.10), channel_id=1, source_target_pairs={{0,16},{8,24},{16,0},{24,8},{1,17},{9,25},{17,1},{25,9},{2,18},{10... | collective-permute-start | bytes 4325384 | tf_op jit(solution)/shard_map/ppermute | solution.py:145
  853.6 112.8 %all-to-all-start.3 = ((bf16[32,64,176]{2,1,0:T(8,128)(2,1)}), bf16[32,64,176]{2,1,0:T(8,128)(2,1)}, u32[]{:S(2)}, u32[]{:S(2)}) async-start(bf16[32,64,176]{2,1,0:T(8,128)(2,1)} %bitcast.115), calls=%async_computation.4 | async-start | bytes 2097152 | tf_op jit(solution)/shard_map/all_to_all | solution.py:515
  881.5 181.0 %collective-permute-start.40 = (bf16[512,2048]{1,0:T(8,128)(2,1)}, bf16[512,2048]{1,0:T(8,128)(2,1)}, u32[]{:S(2)}, u32[]{:S(2)}) collective-permute-start(bf16[512,2048]{1,0:T(8,128)(2,1)} %get-tuple-element.334), channel_id=1, source_target_pairs={{0,1},{1,0},{2,3},{3,2},{4,5},{5,4},{6,7},{7,6},{8,9},{9,8},{10,11... | collective-permute-start | bytes 6291464 | tf_op jit(solution)/shard_map/ppermute | solution.py:111
  1016.3 73.2 %collective-permute-start.58 = (bf16[256,2048]{1,0:T(8,128)(2,1)}, bf16[256,2048]{1,0:T(8,128)(2,1)}, u32[]{:S(2)}, u32[]{:S(2)}) collective-permute-start(bf16[256,2048]{1,0:T(8,128)(2,1)} %pad_maximum_fusion.39), channel_id=1, source_target_pairs={{0,4},{1,3},{2,6},{3,1},{4,0},{5,7},{6,2},{7,5},{8,12},{9,11},{10,... | collective-permute-start | bytes 3145736 | tf_op jit(solution)/shard_map/ppermute | solution.py:107
  1037.9 68.1 %collective-permute-start.64 = (bf16[512,1408]{1,0:T(8,128)(2,1)}, bf16[512,1408]{1,0:T(8,128)(2,1)}, u32[]{:S(2)}, u32[]{:S(2)}) collective-permute-start(bf16[512,1408]{1,0:T(8,128)(2,1)} %get-tuple-element.251), channel_id=1, source_target_pairs={{0,8},{8,0},{16,24},{24,16},{1,9},{9,1},{17,25},{25,17},{2,10},{10... | collective-permute-start | bytes 4325384 | tf_op jit(solution)/shard_map/ppermute | solution.py:145
  1051.6 64.3 %collective-permute-start.65 = (bf16[512,1408]{1,0:T(8,128)(2,1)}, bf16[512,1408]{1,0:T(8,128)(2,1)}, u32[]{:S(2)}, u32[]{:S(2)}) collective-permute-start(bf16[512,1408]{1,0:T(8,128)(2,1)} %get-tuple-element.250), channel_id=1, source_target_pairs={{0,24},{8,16},{16,8},{24,0},{1,25},{9,17},{17,9},{25,1},{2,26},{10... | collective-permute-start | bytes 4325384 | tf_op jit(solution)/shard_map/ppermute | solution.py:145
  1092.4 64.3 %collective-permute-start.59 = (bf16[512,2048]{1,0:T(8,128)(2,1)}, bf16[512,2048]{1,0:T(8,128)(2,1)}, u32[]{:S(2)}, u32[]{:S(2)}) collective-permute-start(bf16[512,2048]{1,0:T(8,128)(2,1)} %pad_maximum_fusion.15), channel_id=1, source_target_pairs={{0,1},{1,0},{2,3},{3,2},{4,5},{5,4},{6,7},{7,6},{8,9},{9,8},{10,11... | collective-permute-start | bytes 6291464 | tf_op jit(solution)/shard_map/ppermute | solution.py:111
  1105.7 59.4 %collective-permute-start.42 = (bf16[128,2048]{1,0:T(8,128)(2,1)}, bf16[128,2048]{1,0:T(8,128)(2,1)}, u32[]{:S(2)}, u32[]{:S(2)}) collective-permute-start(bf16[128,2048]{1,0:T(8,128)(2,1)} %fusion.135), channel_id=1, source_target_pairs={{0,2},{1,5},{2,0},{3,7},{4,6},{5,1},{6,4},{7,3},{8,10},{9,13},{10,... | collective-permute-start | bytes 1572872 | tf_op jit(solution)/shard_map/ppermute | solution.py:107
  1178.9 44.9 %collective-permute-start.63 = (f32[64,2048]{1,0:T(8,128)}, f32[64,2048]{1,0:T(8,128)}, u32[]{:S(2)}, u32[]{:S(2)}) collective-permute-start(f32[64,2048]{1,0:T(8,128)} %fusion.172), channel_id=1, source_target_pairs={{0,0},{1,4},{2,8},{3,12},{4,16},{5,20},{6,24},{7,28},{8,1},{9,5},{... | collective-permute-start | bytes 1572872 | tf_op jit(solution)/shard_map/ppermute | solution.py:524
  (262 other events, 4043.8 us)
Sparse Core Ops, SparseCore 0:
  13.3 73.8 all-gather.8
  108.9 164.7 all-gather.4
  276.5 198.8 all-gather.6
  768.8 231.2 reduce-scatter.1

commit v6 on v5

--- a/solution.py
+++ b/solution.py
@@ -289,9 +289,6 @@
     even_steps, odd_steps = range(2, n_dp, 2), range(1, n_dp, 2)
     in_even = dp_exchange(in_parts, n_dp, dp_index, even_steps, ready)
     down_got = dp_swap(hold(down_sent, ready), n_dp, 1)
-    in_odd = dp_exchange(in_parts, n_dp, dp_index, odd_steps, in_even)
-    in_moved = in_even | in_odd
-    in_moved[0] = dp_block(in_parts, dp_index)
 
     labels = jnp.arange(experts, dtype=jnp.int32)
     hits = jnp.sum((expert_ids[:, :, None] == labels).astype(jnp.int32), axis=1)
@@ -331,11 +328,6 @@
     weight_out = lax.all_gather(hold(out_weight, joined, hidden_group), BOTH, axis=0, tiled=True)
     cot_all = lax.all_gather(hold(cotangent, joined, hidden_group, spread), BOTH, axis=0, tiled=True)
 
-    def chunk_gather(values):
-        far = hold(values, in_odd)
-        sent = [values] + [dp_swap(far, n_dp, step) for step in range(1, n_dp)]
-        return [seq_gather(piece, n_seq) for piece in sent]
-
     rows_group = hidden_group.astype(F32)
     normed_group = (rows_group * rms_scale(rows_group) * gain_attn).astype(BF16)
     in_part = jnp.arange(tokens, dtype=jnp.int32) % part
@@ -376,6 +368,9 @@
     shares = probs.astype(BF16)
     attended = jnp.einsum("bhqk,bkhd->bqhd", shares, values, preferred_element_type=F32)
     attended = to_rows(attended.astype(BF16)).reshape(group, heads * VD)
+    in_odd = dp_exchange(in_parts, n_dp, dp_index, odd_steps, (in_even, attended))
+    in_moved = in_even | in_odd
+    in_moved[0] = dp_block(in_parts, dp_index)
     attended = hold(attended, in_even, down_got)
     heads_out = absolute(attended.reshape(n_seq, tokens, heads * VD))
     heads_out = lax.all_to_all(heads_out, "seq", split_axis=0, concat_axis=2, tiled=True)
@@ -402,9 +397,11 @@
     weight_back = jnp.concatenate(
         [jnp.where(is_low, down_kept, down_got), jnp.where(is_low, down_got, down_kept)], axis=0
     )
-    shared_act_grad = contract(cot_rows, shared_down, 2, 1)
-
-    ffn_chunks = chunk_gather(normed_ffn)
+    shared_act_grad = jnp.stack([tail_dot(cot_rows[g], shared_down) for g in range(n_dp)])
+
+    far = hold(normed_ffn, in_odd)
+    ffn_chunks = [normed_ffn] + [dp_swap(far, n_dp, step) for step in range(1, n_dp)]
+    ffn_chunks = [seq_gather(chunk, n_seq) for chunk in ffn_chunks]
     chunk_places, kept_rows = [], []
     for step in range(n_dp):
         codes = relative(dp_block(slot_code, dp_index ^ step)).reshape(group)
@@ -414,11 +411,10 @@
         chunk_places.append(placed)
         kept_rows.append(lead_dot(placed, ffn_chunks[step]).astype(BF16))
 
-    in_moved = hold([in_moved[step] for step in range(n_dp)], kept_rows[0])
-    weight_in = in_order([piece[:, : 2 * ff_part] for piece in in_moved], n_dp, dp_index)
-    weight_in = weight_in.reshape(-1, 2 * ff_part)
-    weight_shared_in = in_order([piece[:, 2 * ff_part :] for piece in in_moved], n_dp, dp_index)
-    weight_shared_in = weight_shared_in.reshape(-1, 2 * units)
+    in_moved = hold([in_moved[step] for step in range(n_dp)], ffn_chunks[0])
+    weight_in = in_order(in_moved, n_dp, dp_index).reshape(width, -1)
+    weight_shared_in = weight_in[:, 2 * ff_part :]
+    weight_in = weight_in[:, : 2 * ff_part]
     shared_in_back = weight_shared_in.T
     grad_shared_in = 0.0
     kept_cots, kept_acts, kept_grads = [], [], []
@@ -468,13 +464,12 @@
     residual_grad = cotangent.astype(F32) + from_norm
     residual_low = residual_grad.astype(BF16)
     heads_grad = tail_dot(residual_low, weight_out).astype(BF16)
-    heads_grad_own = heads_grad
     heads_grad = heads_grad.reshape(tokens, n_seq, heads * VD)
     heads_grad = lax.all_to_all(heads_grad, "seq", split_axis=1, concat_axis=0, tiled=True)
 
     out_acts, shared_acts = hold((kept_acts, shared_acts), planes[-1][0])
     kept_rows, kept_cots, kept_acts, kept_grads, ffn_chunks = hold(
-        (kept_rows, kept_cots, kept_acts, kept_grads, ffn_chunks), heads_grad_own
+        (kept_rows, kept_cots, kept_acts, kept_grads, ffn_chunks), heads_grad
     )
     grad_in = lead_dot(jnp.concatenate(kept_rows), jnp.concatenate(kept_grads)).astype(BF16)
     back_parts = grad_in.reshape(n_dp, expert_rows, 2 * ff_part)
@@ -505,7 +500,7 @@
         tiled=True,
     )
     output = (residual + out_sum.astype(F32)).astype(BF16)
-    shared_late = hold(shared_act, heads_grad_own).reshape(n_all * tokens, units)
+    shared_late = hold(shared_act, heads_grad).reshape(n_all * tokens, units)
     grad_shared_down = lead_dot(shared_late, cot_all)
     for step in range(n_dp):
         grad_shared_in = grad_shared_in + lead_dot(ffn_chunks[step], kept_shared[step])
@@ -545,7 +540,6 @@
         [key_grad[..., :NOPE].astype(BF16), value_grad], axis=-1
     ).reshape(group, e_width)
 
-    expand_low, rope_grad = hold((expand_low, rope_grad), shared_back)
     latent_sum = seq_scatter(
         lambda part: jnp.concatenate(
             [tail_dot(half_of(expand_low, part), weight_up), half_of(rope_grad, part)], axis=1
@@ -564,6 +558,7 @@
     grad_joined = dp_scatter(grad_joined, n_dp, dp_index)
     back_odd = dp_exchange(back_parts, n_dp, dp_index, odd_steps, grad_joined)
     grad_joined = grad_joined.reshape(n_seq, down_rows, joined_width)
+    grad_joined = hold(grad_joined, shared_back)
     grad_joined = lax.all_to_all(grad_joined, "seq", split_axis=0, concat_axis=0, tiled=True)
     grad_q = jnp.swapaxes(grad_joined[..., :q_width], 0, 1).reshape(q_weight.shape)
     grad_up = grad_joined[..., q_width:].reshape(n_seq, kv_up.shape[0], e_width)

time: 1250 us -> 1540 us (1.23)
  local copies, waits for them, and re-layouts: 253 us -> 505 us
  waiting for transfers between devices: 391 us -> 422 us
    dynamic_update_slice x20 -> x16, local copies, waits for them, and re-layouts: 26.9 us -> 243 us  [in_order(): lax.dynamic_update_index_in_dim(result, moved[step], dp_index ^ step, 0)]
    ppermute x26, waiting for transfers between devices: 216 us -> 308 us  [dp_swap(): return lax.ppermute(values, 'dp', [(d, d ^ step) for d in range(n_dp)])]
    all_to_all x1, waiting for transfers between devices: 72.6 us -> 0.01 us  [body(): lax.all_to_all(grad_shared_in.reshape(n_all, -1, 2 * units), BOTH, split_...]
    broadcast_in_dim x20 -> x8, local copies, waits for them, and re-layouts: 27.6 us -> 49 us  [in_order(): lax.dynamic_update_index_in_dim(result, moved[step], dp_index ^ step, 0)]
    all_to_all x1, starting transfers between devices: 26.7 us -> 9.92 us  [body(): lax.all_to_all(gain_grads, BOTH, split_axis=0, concat_axis=0, tiled=True)]
    dot_general x55 -> x58, matrix products: 200 us -> 201 us  [contract(): lax.dot_general(left_side, right_side, (((left_dim,), (right_dim,)), ((),...]
    unnamed x462 -> x434, local copies, waits for them, and re-layouts: 62 us -> 62.3 us
  transfers between devices with their start and end apart: 76 -> 76, of which waited for: 27 -> 31; matrix products, arithmetic and copies ran while one was open for 42% -> 51% of each run, Pallas kernels for 1% -> 1%
where the time goes in v6:
time: 1540 us; the launch traced here: 1510 us
  local copies, waits for them, and re-layouts  505 us (33%)
  waiting for transfers between devices  422 us (27%)
  matrix products  240 us (16%)
  starting transfers between devices  190 us (12%)
  other arithmetic  128 us (8%)
  between operations  17.4 us (1%)
    ppermute x26, waiting for transfers between devices, dp_swap(): return lax.ppermute(values, 'dp', [(d, d ^ step) for d in range(n_dp)])  308 us
    dynamic_update_slice x16, local copies, waits for them, and re-layouts, in_order(): lax.dynamic_update_index_in_dim(result, moved[step], dp_index ^ step, 0)  243 us
    dot_general x58, matrix products, contract(): lax.dot_general(left_side, right_side, (((left_dim,), (right_dim,)), ((),...  201 us
    ppermute x26, starting transfers between devices, dp_swap(): return lax.ppermute(values, 'dp', [(d, d ^ step) for d in range(n_dp)])  74.7 us
    ppermute x26, waiting for transfers between devices, seq_step(): lax.ppermute(values, 'seq', [(s, s ^ orders[s & 1][step]) for s in range(...  71.4 us
    unnamed x434, local copies, waits for them, and re-layouts  62.3 us
    broadcast_in_dim x8, local copies, waits for them, and re-layouts, in_order(): lax.dynamic_update_index_in_dim(result, moved[step], dp_index ^ step, 0)  49 us
    ppermute x13, starting transfers between devices, core_swap(): return lax.ppermute(values, 'seq', [(s, s ^ 1) for s in range(n_seq)])  44.1 us
  transfers between devices with their start and end apart: 76, of which 31 were waited for; matrix products, arithmetic and copies ran while one was open for 51% of the time, Pallas kernels for 1%

profile of v6, /device:TPU:25, one launch (start us, length us, event | category | flops | bytes accessed | tf_op | source)
XLA Modules:
  0.0 1511.1 jit_solution(4912012474751116927)
XLA Ops:
  62.3 14.8 copy.292
  89.0 10.5 collective-permute-done.5
  129.5 13.0 collective-permute-start.6
  178.8 43.6 %collective-permute-done.7 = bf16[352,2048]{1,0:T(8,128)(2,1)} collective-permute-done((bf16[352,2048]{1,0:T(8,128)(2,1)S(1)}, bf16[352,2048]{1,0:T(8,128)(2,1)}, u32[]{:S(2)}, u32[]{:S(2)}) %collective-permute-start.7) | collective-permute-done | bytes 1441824 | tf_op jit(solution)/shard_map/ppermute | solution.py:145
  222.4 25.3 %collective-permute-done.6 = bf16[512,1584]{0,1:T(8,128)(2,1)} collective-permute-done((bf16[512,1584]{0,1:T(8,128)(2,1)}, bf16[512,1584]{0,1:T(8,128)(2,1)}, u32[]{:S(2)}, u32[]{:S(2)}) %collective-permute-start.6) | collective-permute-done | bytes 1622048 | tf_op jit(solution)/shard_map/ppermute | solution.py:145
  276.3 61.2 %collective-permute-done.11 = bf16[512,1584]{0,1:T(8,128)(2,1)} collective-permute-done((bf16[512,1584]{0,1:T(8,128)(2,1)}, bf16[512,1584]{0,1:T(8,128)(2,1)}, u32[]{:S(2)}, u32[]{:S(2)}) %collective-permute-start.11) | collective-permute-done | bytes 1622048 | tf_op jit(solution)/shard_map/ppermute | solution.py:145
  337.5 26.2 %collective-permute-done.12 = bf16[512,1584]{0,1:T(8,128)(2,1)} collective-permute-done((bf16[512,1584]{0,1:T(8,128)(2,1)}, bf16[512,1584]{0,1:T(8,128)(2,1)}, u32[]{:S(2)}, u32[]{:S(2)}) %collective-permute-start.12) | collective-permute-done | bytes 1622048 | tf_op jit(solution)/shard_map/ppermute | solution.py:145
  372.1 31.4 %collective-permute-done.13 = bf16[128,2048]{1,0:T(8,128)(2,1)S(1)} collective-permute-done((bf16[128,2048]{1,0:T(8,128)(2,1)S(1)}, bf16[128,2048]{1,0:T(8,128)(2,1)S(1)}, u32[]{:S(2)}, u32[]{:S(2)}) %collective-permute-start.13) | collective-permute-done | bytes 524320 | tf_op jit(solution)/shard_map/ppermute | solution.py:145
  406.4 11.3 collective-permute-done.17
  417.7 14.6 collective-permute-done.21
  453.7 9.5 collective-permute-done.19
  482.2 14.5 copy.302
  496.7 9.4 copy.303
  506.1 9.4 copy.304
  528.2 57.6 %dynamic_update_slice.56 = bf16[4,512,1584]{1,0,2:T(4,128)(2,1)} dynamic-update-slice(bf16[4,512,1584]{1,0,2:T(4,128)(2,1)} %broadcast_in_dim.201, bf16[1,512,1584]{1,0,2:T(2,128)(2,1)} %copy.302, s32[]{:T(128)S(6)} %select_n.199, s32[]{:T(128)} %constant.280.clone.1, s32[]{:T(128)} %constant.280.clone.1) | dynamic-update-slice | bytes 3244036 | tf_op jit(solution)/shard_map/jit(dynamic_update_index_in_dim)/dynamic_update_slice | solution.py:162
  585.8 57.6 %dynamic_update_slice.57 = bf16[4,512,1584]{1,0,2:T(4,128)(2,1)} dynamic-update-slice(bf16[4,512,1584]{1,0,2:T(4,128)(2,1)} %dynamic_update_slice.56, bf16[1,512,1584]{1,0,2:T(2,128)(2,1)} %copy.303, s32[]{:T(128)S(6)} %select_n.200, s32[]{:T(128)} %constant.280.clone.1, s32[]{:T(128)} %constant.280.clone.1) | dynamic-update-slice | bytes 3244036 | tf_op jit(solution)/shard_map/jit(dynamic_update_index_in_dim)/dynamic_update_slice | solution.py:162
  643.4 57.6 %dynamic_update_slice.58 = bf16[4,512,1584]{1,0,2:T(4,128)(2,1)} dynamic-update-slice(bf16[4,512,1584]{1,0,2:T(4,128)(2,1)} %dynamic_update_slice.57, bf16[1,512,1584]{1,0,2:T(2,128)(2,1)} %copy.304, s32[]{:T(128)S(6)} %select_n.201, s32[]{:T(128)} %constant.280.clone.1, s32[]{:T(128)} %constant.280.clone.1) | dynamic-update-slice | bytes 3244036 | tf_op jit(solution)/shard_map/jit(dynamic_update_index_in_dim)/dynamic_update_slice | solution.py:162
  701.0 57.8 %dynamic_update_slice.59 = bf16[4,512,1584]{1,0,2:T(4,128)(2,1)} dynamic-update-slice(bf16[4,512,1584]{1,0,2:T(4,128)(2,1)} %dynamic_update_slice.58, bf16[1,512,1584]{1,0,2:T(2,128)(2,1)S(1)} %copy.305, s32[]{:T(128)S(6)} %select_n.202, s32[]{:T(128)} %constant.280.clone.1, s32[]{:T(128)} %constant.280.clone.1) | dynamic-update-slice | bytes 3244036 | tf_op jit(solution)/shard_map/jit(dynamic_update_index_in_dim)/dynamic_update_slice | solution.py:162
  956.4 25.7 %collective-permute-start.32 = (bf16[128,2048]{1,0:T(8,128)(2,1)}, bf16[128,2048]{1,0:T(8,128)(2,1)}, u32[]{:S(2)}, u32[]{:S(2)}) collective-permute-start(bf16[128,2048]{1,0:T(8,128)(2,1)} %convert_add_fusion.1), channel_id=1, source_target_pairs={{0,8},{8,0},{16,24},{24,16},{1,9},{9,1},{17,25},{25,17},{2,10},{10... | collective-permute-start | bytes 1572872 | tf_op jit(solution)/shard_map/ppermute | solution.py:145
  1020.6 16.5 %convolution_convert_fusion = bf16[4,1024,2048]{2,1,0:T(8,128)(2,1)} fusion(bf16[4,88,2048]{2,1,0:T(8,128)(2,1)} %broadcast_in_dim.217, bf16[4,384,2048]{2,1,0:T(8,128)(2,1)} %multiply_convert_fusion, bf16[4,1024,88]{1,2,0:T(8,128)(2,1)S(1)} %reshape.733, bf16[4,1024,384]{1,2,0:T(8,128)(2,1)} %compare_convert_fusion), kind=kOutput, calls=%fused_computation.16 | convolution fusion | flops 7950434304 | bytes 28377088 | tf_op jit(solution)/shard_map/gtk,gkd->gtd/dot_general | solution.py:488
  1073.7 12.0 all-to-all-done.2
  1097.6 12.5 convolution_convert_fusion.1
  1173.0 9.7 fusion.339
  1195.9 10.2 collective-permute-done.44
  1263.3 15.0 collective-permute-start.53
  1278.3 13.9 collective-permute-done.49
  1298.6 11.5 collective-permute-start.64
  1333.6 37.2 %collective-permute-done.54 = bf16[64,576]{1,0:T(8,128)(2,1)S(1)} collective-permute-done((bf16[64,576]{1,0:T(8,128)(2,1)S(1)}, bf16[64,576]{1,0:T(8,128)(2,1)S(1)}, u32[]{:S(2)}, u32[]{:S(2)}) %collective-permute-start.54) | collective-permute-done | bytes 73760 | tf_op jit(solution)/shard_map/ppermute | solution.py:145
  1416.1 9.6 assemble.1
  1437.9 13.3 collective-permute-done.61
  1460.5 9.9 all-to-all-start.3
  1470.4 27.8 %all-to-all-done.3 = f32[32,1,144]{2,1,0:T(1,128)S(1)} async-done(((f32[32,1,144]{2,1,0:T(1,128)}), f32[32,1,144]{2,1,0:T(1,128)S(1)}, u32[]{:S(2)}, u32[]{:S(2)}) %all-to-all-start.3) | async-done | bytes 18464 | tf_op jit(solution)/shard_map/all_to_all | solution.py:600
  (890 shorter events, 743.8 us)
Async XLA Ops:
  7.2 103.8 %all-gather.9.cloned.1.call-start = ((), (), s32[]{:S(2)}) async-start(), calls=%async_computation.10 | async-start | bytes 3379200 | tf_op jit(solution)/shard_map/all_gather | solution.py:315
  40.6 228.3 %all-gather.5.cloned.1.call-start = ((), (), s32[]{:S(2)}) async-start(), calls=%async_computation.7 | async-start | bytes 8650752 | tf_op jit(solution)/shard_map/all_gather | solution.py:328
  51.1 56.5 %collective-permute-start.2 = (bf16[512,2048]{1,0:T(8,128)(2,1)}, bf16[512,2048]{1,0:T(8,128)(2,1)}, u32[]{:S(2)}, u32[]{:S(2)}) collective-permute-start(bf16[512,2048]{1,0:T(8,128)(2,1)} %pad_maximum_fusion.10), channel_id=1, source_target_pairs={{0,1},{1,0},{2,3},{3,2},{4,5},{5,4},{6,7},{7,6},{8,9},{9,8},{10,11... | collective-permute-start | bytes 6291464 | tf_op jit(solution)/shard_map/ppermute | solution.py:111
  110.7 691.9 %all-gather.7.cloned.1.call-start = ((), (), s32[]{:S(2)}) async-start(), calls=%async_computation.8 | async-start | bytes 17301504 | tf_op jit(solution)/shard_map/all_gather | solution.py:329
  129.5 118.2 %collective-permute-start.6 = (bf16[512,1584]{0,1:T(8,128)(2,1)}, bf16[512,1584]{0,1:T(8,128)(2,1)}, u32[]{:S(2)}, u32[]{:S(2)}) collective-permute-start(bf16[512,1584]{0,1:T(8,128)(2,1)} %dynamic-slice_bitcast_fusion.2), channel_id=1, source_target_pairs={{0,16},{8,24},{16,0},{24,8},{1,17},{9,25},{17,1},{25,9},{2,18},{10... | collective-permute-start | bytes 4866056 | tf_op jit(solution)/shard_map/ppermute | solution.py:145
  142.5 79.9 %collective-permute-start.7 = (bf16[352,2048]{1,0:T(8,128)(2,1)S(1)}, bf16[352,2048]{1,0:T(8,128)(2,1)}, u32[]{:S(2)}, u32[]{:S(2)}) collective-permute-start(bf16[352,2048]{1,0:T(8,128)(2,1)S(1)} %copy-done.96), channel_id=1, source_target_pairs={{0,8},{8,0},{16,24},{24,16},{1,9},{9,1},{17,25},{25,17},{2,10},{10... | collective-permute-start | bytes 4325384 | tf_op jit(solution)/shard_map/ppermute | solution.py:145
  253.7 1245.6 %reduce-scatter.2.cloned.1.call-start = ((), (), s32[]{:S(2)}) async-start(), calls=%async_computation.9 | async-start | bytes 17301504 | tf_op jit(solution)/shard_map/reduce_scatter | solution.py:496
  257.7 79.9 %collective-permute-start.11 = (bf16[512,1584]{0,1:T(8,128)(2,1)}, bf16[512,1584]{0,1:T(8,128)(2,1)}, u32[]{:S(2)}, u32[]{:S(2)}) collective-permute-start(bf16[512,1584]{0,1:T(8,128)(2,1)} %get-tuple-element.235), channel_id=1, source_target_pairs={{0,8},{8,0},{16,24},{24,16},{1,9},{9,1},{17,25},{25,17},{2,10},{10... | collective-permute-start | bytes 4866056 | tf_op jit(solution)/shard_map/ppermute | solution.py:145
  257.7 106.0 %collective-permute-start.12 = (bf16[512,1584]{0,1:T(8,128)(2,1)}, bf16[512,1584]{0,1:T(8,128)(2,1)}, u32[]{:S(2)}, u32[]{:S(2)}) collective-permute-start(bf16[512,1584]{0,1:T(8,128)(2,1)} %get-tuple-element.234), channel_id=1, source_target_pairs={{0,24},{8,16},{16,8},{24,0},{1,25},{9,17},{17,9},{25,1},{2,26},{10... | collective-permute-start | bytes 4866056 | tf_op jit(solution)/shard_map/ppermute | solution.py:145
  274.8 96.0 %collective-permute-start.8 = (bf16[128,2048]{1,0:T(8,128)(2,1)S(1)}, bf16[128,2048]{1,0:T(8,128)(2,1)S(1)}, u32[]{:S(2)}, u32[]{:S(2)}) collective-permute-start(bf16[128,2048]{1,0:T(8,128)(2,1)S(1)} %multiply_convert_fusion.23), channel_id=1, source_target_pairs={{0,2},{1,5},{2,0},{3,7},{4,6},{5,1},{6,4},{7,3},{8,10},{9,13},{10,... | collective-permute-start | bytes 1572872 | tf_op jit(solution)/shard_map/ppermute | solution.py:107
  365.8 66.5 %collective-permute-start.21 = (bf16[128,2048]{1,0:T(8,128)(2,1)S(1)}, bf16[128,2048]{1,0:T(8,128)(2,1)S(1)}, u32[]{:S(2)}, u32[]{:S(2)}) collective-permute-start(bf16[128,2048]{1,0:T(8,128)(2,1)S(1)} %multiply_convert_fusion.23), channel_id=1, source_target_pairs={{0,24},{8,16},{16,8},{24,0},{1,25},{9,17},{17,9},{25,1},{2,26},{10... | collective-permute-start | bytes 1572872 | tf_op jit(solution)/shard_map/ppermute | solution.py:145
  370.9 70.9 %collective-permute-start.9 = (bf16[256,2048]{1,0:T(8,128)(2,1)S(1)}, bf16[256,2048]{1,0:T(8,128)(2,1)S(1)}, u32[]{:S(2)}, u32[]{:S(2)}) collective-permute-start(bf16[256,2048]{1,0:T(8,128)(2,1)S(1)} %pad_maximum_fusion.36), channel_id=1, source_target_pairs={{0,4},{1,3},{2,6},{3,1},{4,0},{5,7},{6,2},{7,5},{8,12},{9,11},{10,... | collective-permute-start | bytes 3145736 | tf_op jit(solution)/shard_map/ppermute | solution.py:107
  453.6 320.3 %collective-permute-start.16 = (bf16[512,2048]{1,0:T(8,128)(2,1)}, bf16[512,2048]{1,0:T(8,128)(2,1)}, u32[]{:S(2)}, u32[]{:S(2)}) collective-permute-start(bf16[512,2048]{1,0:T(8,128)(2,1)} %pad_maximum_fusion.12), channel_id=1, source_target_pairs={{0,1},{1,0},{2,3},{3,2},{4,5},{5,4},{6,7},{7,6},{8,9},{9,8},{10,11... | collective-permute-start | bytes 6291464 | tf_op jit(solution)/shard_map/ppermute | solution.py:111
  464.7 311.2 %collective-permute-start.20 = (bf16[512,2048]{1,0:T(8,128)(2,1)}, bf16[512,2048]{1,0:T(8,128)(2,1)}, u32[]{:S(2)}, u32[]{:S(2)}) collective-permute-start(bf16[512,2048]{1,0:T(8,128)(2,1)} %pad_maximum_fusion.13), channel_id=1, source_target_pairs={{0,1},{1,0},{2,3},{3,2},{4,5},{5,4},{6,7},{7,6},{8,9},{9,8},{10,11... | collective-permute-start | bytes 6291464 | tf_op jit(solution)/shard_map/ppermute | solution.py:111
  475.8 304.4 %collective-permute-start.24 = (bf16[512,2048]{1,0:T(8,128)(2,1)}, bf16[512,2048]{1,0:T(8,128)(2,1)}, u32[]{:S(2)}, u32[]{:S(2)}) collective-permute-start(bf16[512,2048]{1,0:T(8,128)(2,1)} %pad_maximum_fusion.14), channel_id=1, source_target_pairs={{0,1},{1,0},{2,3},{3,2},{4,5},{5,4},{6,7},{7,6},{8,9},{9,8},{10,11... | collective-permute-start | bytes 6291464 | tf_op jit(solution)/shard_map/ppermute | solution.py:111
  956.4 80.7 %collective-permute-start.32 = (bf16[128,2048]{1,0:T(8,128)(2,1)}, bf16[128,2048]{1,0:T(8,128)(2,1)}, u32[]{:S(2)}, u32[]{:S(2)}) collective-permute-start(bf16[128,2048]{1,0:T(8,128)(2,1)} %convert_add_fusion.1), channel_id=1, source_target_pairs={{0,8},{8,0},{16,24},{24,16},{1,9},{9,1},{17,25},{25,17},{2,10},{10... | collective-permute-start | bytes 1572872 | tf_op jit(solution)/shard_map/ppermute | solution.py:145
  982.1 55.0 %collective-permute-start.34 = (bf16[128,2048]{1,0:T(8,128)(2,1)}, bf16[128,2048]{1,0:T(8,128)(2,1)}, u32[]{:S(2)}, u32[]{:S(2)}) collective-permute-start(bf16[128,2048]{1,0:T(8,128)(2,1)} %add_convert_fusion.2), channel_id=1, source_target_pairs={{0,16},{8,24},{16,0},{24,8},{1,17},{9,25},{17,1},{25,9},{2,18},{10... | collective-permute-start | bytes 1572872 | tf_op jit(solution)/shard_map/ppermute | solution.py:145
  1096.6 119.5 %collective-permute-start.47 = (bf16[352,2048]{1,0:T(8,128)(2,1)}, bf16[352,2048]{1,0:T(8,128)(2,1)}, u32[]{:S(2)}, u32[]{:S(2)}) collective-permute-start(bf16[352,2048]{1,0:T(8,128)(2,1)} %select_convert_fusion), channel_id=1, source_target_pairs={{0,8},{8,0},{16,24},{24,16},{1,9},{9,1},{17,25},{25,17},{2,10},{10... | collective-permute-start | bytes 4325384 | tf_op jit(solution)/shard_map/ppermute | solution.py:145
  1113.9 110.9 %collective-permute-start.46 = (bf16[512,1408]{1,0:T(8,128)(2,1)}, bf16[512,1408]{1,0:T(8,128)(2,1)S(1)}, u32[]{:S(2)}, u32[]{:S(2)}) collective-permute-start(bf16[512,1408]{1,0:T(8,128)(2,1)} %dynamic-slice_bitcast_fusion.10), channel_id=1, source_target_pairs={{0,16},{8,24},{16,0},{24,8},{1,17},{9,25},{17,1},{25,9},{2,18},{10... | collective-permute-start | bytes 4325384 | tf_op jit(solution)/shard_map/ppermute | solution.py:145
  1149.5 160.7 %all-to-all-start.4 = ((bf16[32,64,176]{2,1,0:T(8,128)(2,1)}), bf16[32,64,176]{2,1,0:T(8,128)(2,1)}, u32[]{:S(2)}, u32[]{:S(2)}) async-start(bf16[32,64,176]{2,1,0:T(8,128)(2,1)} %bitcast.521), calls=%async_computation.5 | async-start | bytes 2097152 | tf_op jit(solution)/shard_map/all_to_all | solution.py:510
  1156.6 85.7 %collective-permute-start.57 = (bf16[128,2048]{1,0:T(8,128)(2,1)S(1)}, bf16[128,2048]{1,0:T(8,128)(2,1)}, u32[]{:S(2)}, u32[]{:S(2)}) collective-permute-start(bf16[128,2048]{1,0:T(8,128)(2,1)S(1)} %fusion.326), channel_id=1, source_target_pairs={{0,2},{1,5},{2,0},{3,7},{4,6},{5,1},{6,4},{7,3},{8,10},{9,13},{10,... | collective-permute-start | bytes 1572872 | tf_op jit(solution)/shard_map/ppermute | solution.py:107
  1172.2 150.7 %collective-permute-start.40 = (bf16[512,2048]{1,0:T(8,128)(2,1)}, bf16[512,2048]{1,0:T(8,128)(2,1)}, u32[]{:S(2)}, u32[]{:S(2)}) collective-permute-start(bf16[512,2048]{1,0:T(8,128)(2,1)} %get-tuple-element.334), channel_id=1, source_target_pairs={{0,1},{1,0},{2,3},{3,2},{4,5},{5,4},{6,7},{7,6},{8,9},{9,8},{10,11... | collective-permute-start | bytes 6291464 | tf_op jit(solution)/shard_map/ppermute | solution.py:111
  1238.0 54.2 %collective-permute-start.49 = (bf16[512,512]{1,0:T(8,128)(2,1)}, bf16[512,512]{1,0:T(8,128)(2,1)}, u32[]{:S(2)}, u32[]{:S(2)}) collective-permute-start(bf16[512,512]{1,0:T(8,128)(2,1)} %get-tuple-element.271), channel_id=1, source_target_pairs={{0,16},{8,24},{16,0},{24,8},{1,17},{9,25},{17,1},{25,9},{2,18},{10... | collective-permute-start | bytes 1572872 | tf_op jit(solution)/shard_map/ppermute | solution.py:145
  1238.0 54.2 %collective-permute-start.50 = (bf16[512,512]{1,0:T(8,128)(2,1)}, bf16[512,512]{1,0:T(8,128)(2,1)}, u32[]{:S(2)}, u32[]{:S(2)}) collective-permute-start(bf16[512,512]{1,0:T(8,128)(2,1)} %get-tuple-element.272), channel_id=1, source_target_pairs={{0,24},{8,16},{16,8},{24,0},{1,25},{9,17},{17,9},{25,1},{2,26},{10... | collective-permute-start | bytes 1572872 | tf_op jit(solution)/shard_map/ppermute | solution.py:145
  1255.6 73.6 %collective-permute-start.58 = (bf16[256,2048]{1,0:T(8,128)(2,1)}, bf16[256,2048]{1,0:T(8,128)(2,1)}, u32[]{:S(2)}, u32[]{:S(2)}) collective-permute-start(bf16[256,2048]{1,0:T(8,128)(2,1)} %pad_maximum_fusion.40), channel_id=1, source_target_pairs={{0,4},{1,3},{2,6},{3,1},{4,0},{5,7},{6,2},{7,5},{8,12},{9,11},{10,... | collective-permute-start | bytes 3145736 | tf_op jit(solution)/shard_map/ppermute | solution.py:107
  1263.3 56.0 %collective-permute-start.53 = (bf16[512,576]{0,1:T(8,128)(2,1)}, bf16[512,576]{0,1:T(8,128)(2,1)}, u32[]{:S(2)}, u32[]{:S(2)}) collective-permute-start(bf16[512,576]{0,1:T(8,128)(2,1)} %pad_maximum_fusion.45), channel_id=1, source_target_pairs={{0,1},{1,0},{2,3},{3,2},{4,5},{5,4},{6,7},{7,6},{8,9},{9,8},{10,11... | collective-permute-start | bytes 1769480 | tf_op jit(solution)/shard_map/ppermute | solution.py:111
  1298.6 95.2 %collective-permute-start.64 = (bf16[512,1408]{1,0:T(8,128)(2,1)}, bf16[512,1408]{1,0:T(8,128)(2,1)}, u32[]{:S(2)}, u32[]{:S(2)}) collective-permute-start(bf16[512,1408]{1,0:T(8,128)(2,1)} %get-tuple-element.249), channel_id=1, source_target_pairs={{0,8},{8,0},{16,24},{24,16},{1,9},{9,1},{17,25},{25,17},{2,10},{10... | collective-permute-start | bytes 4325384 | tf_op jit(solution)/shard_map/ppermute | solution.py:145
  1310.1 83.6 %collective-permute-start.65 = (bf16[512,1408]{1,0:T(8,128)(2,1)}, bf16[512,1408]{1,0:T(8,128)(2,1)}, u32[]{:S(2)}, u32[]{:S(2)}) collective-permute-start(bf16[512,1408]{1,0:T(8,128)(2,1)} %get-tuple-element.248), channel_id=1, source_target_pairs={{0,24},{8,16},{16,8},{24,0},{1,25},{9,17},{17,9},{25,1},{2,26},{10... | collective-permute-start | bytes 4325384 | tf_op jit(solution)/shard_map/ppermute | solution.py:145
  1310.3 74.0 %all-to-all-start.5 = ((f32[8,64,512]{2,1,0:T(8,128)}), f32[8,64,512]{2,1,0:T(8,128)}, u32[]{:S(2)}, u32[]{:S(2)}) async-start(f32[8,64,512]{2,1,0:T(8,128)} %bitcast.123), calls=%async_computation.6 | async-start | bytes 2097152 | tf_op jit(solution)/shard_map/all_to_all | solution.py:562
  1322.9 53.5 %collective-permute-start.55 = (bf16[64,576]{1,0:T(8,128)(2,1)S(1)}, bf16[64,576]{1,0:T(8,128)(2,1)S(1)}, u32[]{:S(2)}, u32[]{:S(2)}) collective-permute-start(bf16[64,576]{1,0:T(8,128)(2,1)S(1)} %get-tuple-element.306), channel_id=1, source_target_pairs={{0,16},{8,24},{16,0},{24,8},{1,17},{9,25},{17,1},{25,9},{2,18},{10... | collective-permute-start | bytes 221192 | tf_op jit(solution)/shard_map/ppermute | solution.py:145
  1329.2 62.3 %collective-permute-start.41 = (bf16[256,2048]{1,0:T(8,128)(2,1)}, bf16[256,2048]{1,0:T(8,128)(2,1)}, u32[]{:S(2)}, u32[]{:S(2)}) collective-permute-start(bf16[256,2048]{1,0:T(8,128)(2,1)} %get-tuple-element.250), channel_id=1, source_target_pairs={{0,4},{1,3},{2,6},{3,1},{4,0},{5,7},{6,2},{7,5},{8,12},{9,11},{10,... | collective-permute-start | bytes 3145736 | tf_op jit(solution)/shard_map/ppermute | solution.py:107
  1370.8 54.9 %collective-permute-start.59 = (bf16[512,2048]{1,0:T(8,128)(2,1)}, bf16[512,2048]{1,0:T(8,128)(2,1)}, u32[]{:S(2)}, u32[]{:S(2)}) collective-permute-start(bf16[512,2048]{1,0:T(8,128)(2,1)} %pad_maximum_fusion.15), channel_id=1, source_target_pairs={{0,1},{1,0},{2,3},{3,2},{4,5},{5,4},{6,7},{7,6},{8,9},{9,8},{10,11... | collective-permute-start | bytes 6291464 | tf_op jit(solution)/shard_map/ppermute | solution.py:111
  (247 other events, 3523.0 us)
Sparse Core Ops, SparseCore 0:
  13.3 69.4 all-gather.8
  110.9 138.3 all-gather.4
  252.2 209.6 all-gather.6
  1039.8 248.0 reduce-scatter.1

commit v7 on v6

--- a/solution.py
+++ b/solution.py
@@ -111,9 +111,9 @@
     return lax.ppermute(values, "seq", [(s, s ^ 1) for s in range(n_seq)])
 
 
-def seq_gather(values, n_seq):
-    current = values
-    for step in range(len(link_orders(n_seq)[0])):
+def seq_gather(values, n_seq, first=None):
+    current = values if first is None else first
+    for step in range(0 if first is None else 1, len(link_orders(n_seq)[0])):
         current = jnp.concatenate([current, seq_step(current, n_seq, step)], axis=0)
     return jnp.concatenate([current, core_swap(current, n_seq)], axis=0)
 
@@ -204,6 +204,39 @@
         ),
         compiler_params=pltpu.CompilerParams(vmem_limit_bytes=48 * 2**20),
         name="assemble",
+    )(jnp.reshape(dp_index, (1,)).astype(jnp.int32), *pieces)
+
+
+def lay_out_kernel(index_ref, *refs):
+    count = (len(refs) - 2)
+    pieces, out_ref, sems = refs[:count], refs[count], refs[count + 1]
+    rows = pieces[0].shape[0]
+    copies = [
+        pltpu.make_async_copy(
+            pieces[step], out_ref.at[pl.ds((index_ref[0] ^ step) * rows, rows)], sems.at[step]
+        )
+        for step in range(count)
+    ]
+    for copy in copies:
+        copy.start()
+    for copy in copies:
+        copy.wait()
+
+
+def lay_out(pieces, dp_index):
+    rows, cols = pieces[0].shape
+    count = len(pieces)
+    return pl.pallas_call(
+        lay_out_kernel,
+        out_shape=jax.ShapeDtypeStruct((count * rows, cols), pieces[0].dtype),
+        grid_spec=pltpu.PrefetchScalarGridSpec(
+            num_scalar_prefetch=1,
+            grid=(1,),
+            in_specs=[pl.BlockSpec(memory_space=pl.ANY)] * count,
+            out_specs=pl.BlockSpec(memory_space=pl.ANY),
+            scratch_shapes=[pltpu.SemaphoreType.DMA((count,))],
+        ),
+        name="lay_out",
     )(jnp.reshape(dp_index, (1,)).astype(jnp.int32), *pieces)
 
 
@@ -266,6 +299,11 @@
     shared_cols = shared_gate_up.reshape(down_rows, 2, n_dp, n_seq, units)
     shared_cols = jnp.transpose(shared_cols, (0, 3, 2, 1, 4)).reshape(down_rows, n_seq, -1)
 
+    out_far = [out_weight] + [dp_swap(out_weight, n_dp, step) for step in range(1, n_dp)]
+    out_rows = jnp.concatenate(out_far, axis=0)
+    late_cot = hold(cotangent, out_far)
+    cot_far = [late_cot] + [dp_swap(late_cot, n_dp, step) for step in range(1, n_dp)]
+
     up_rows = kv_up.reshape(kv_up.shape[0], n_seq, -1, kv_up.shape[0] * e_width // down_rows)
     up_rows = jnp.swapaxes(up_rows, 1, 2).reshape(down_rows, n_seq, -1)
     joined_width = q_width + up_rows.shape[2]
@@ -278,12 +316,13 @@
     shared_parts = jnp.swapaxes(shared_parts, 0, 1)
     joined = joined[:, :joined_width]
     joined = [joined] + [dp_swap(joined, n_dp, step) for step in range(1, n_dp)]
-    joined = hold(joined, in_parts, down_kept, down_sent)
+    joined = hold(joined, in_parts, down_kept, down_sent, cot_far)
     joined = in_order(joined, n_dp, dp_index).reshape(-1, joined_width)
     weight_q = joined[:, :q_width]
     weight_up = joined[:, q_width:].reshape(KV_RANK, e_width)
 
     hidden_group = seq_gather(hidden, n_seq)
+    out_rows = seq_gather(hold(out_rows, joined), n_seq).reshape(n_seq, n_dp * down_rows, width)
     ready = joined
     in_parts = jnp.concatenate([in_parts, shared_parts], axis=2)
     even_steps, odd_steps = range(2, n_dp, 2), range(1, n_dp, 2)
@@ -325,8 +364,10 @@
     slot_code = routing[:, :, 0] * 16 + routing[:, :, 1]
     gate_of = (routing[:, :, 2] * 128 + routing[:, :, 3]).astype(F32) / GATE_UNIT
 
-    weight_out = lax.all_gather(hold(out_weight, joined, hidden_group), BOTH, axis=0, tiled=True)
-    cot_all = lax.all_gather(hold(cotangent, joined, hidden_group, spread), BOTH, axis=0, tiled=True)
+    out_rows = absolute(out_rows).reshape(n_seq, n_dp, down_rows, width)
+    dp_order = jnp.arange(n_dp, dtype=jnp.int32) ^ dp_index
+    weight_out = jnp.swapaxes(jnp.take(out_rows, dp_order, axis=1, mode="clip"), 0, 1)
+    weight_out = weight_out.reshape(H * VD, width)
 
     rows_group = hidden_group.astype(F32)
     normed_group = (rows_group * rms_scale(rows_group) * gain_attn).astype(BF16)
@@ -346,6 +387,7 @@
     latent_in = matmul(normed_group, weight_down)
     latent_raw = latent_in[:, :KV_RANK]
     latent = (latent_raw * rms_scale(latent_raw) * gain_kv).astype(BF16)
+    cot_chunks = [seq_gather(chunk, n_seq) for chunk in hold(cot_far[:2], latent)]
     expanded = matmul(latent, weight_up).reshape(group, heads, NOPE + VD)
     rope_query = rotate(query_raw[..., NOPE:], cosine[:, None], sine[:, None])
     rope_key = rotate(latent_in[:, KV_RANK:], cosine, sine)
@@ -374,57 +416,48 @@
     attended = hold(attended, in_even, down_got)
     heads_out = absolute(attended.reshape(n_seq, tokens, heads * VD))
     heads_out = lax.all_to_all(heads_out, "seq", split_axis=0, concat_axis=2, tiled=True)
-    heads_out = heads_out.reshape(tokens, H * VD)
+    heads_out = hold(heads_out.reshape(tokens, H * VD), cot_chunks)
 
     rows = hidden.astype(F32)
     residual = rows + matmul(heads_out, weight_out)
     normed_ffn = (residual * rms_scale(residual) * gain_ffn).astype(BF16)
 
     slots = jnp.arange(1, capacity + 1, dtype=jnp.int32)
-    all_codes = slot_code.reshape(n_dp, group)
-    all_here = all_codes[:, :, None] == slots
-    slot_gate = jnp.where(all_here, gate_of.reshape(n_dp, group)[:, :, None], 0.0)
-    slot_gate = jnp.sum(slot_gate, axis=1)[:, :, None]
-    all_placed = lax.optimization_barrier(all_here.astype(BF16))
-    cot_rows = cot_all.reshape(n_dp, group, width)
-    slot_cot = jnp.stack(
-        [
-            (lead_dot(all_placed[g], cot_rows[g]) * slot_gate[g]).astype(BF16)
-            for g in range(n_dp)
-        ]
-    )
     down_kept, down_got = hold((down_kept, down_got), normed_ffn)
     weight_back = jnp.concatenate(
         [jnp.where(is_low, down_kept, down_got), jnp.where(is_low, down_got, down_kept)], axis=0
     )
-    shared_act_grad = jnp.stack([tail_dot(cot_rows[g], shared_down) for g in range(n_dp)])
 
     far = hold(normed_ffn, in_odd)
-    ffn_chunks = [normed_ffn] + [dp_swap(far, n_dp, step) for step in range(1, n_dp)]
-    ffn_chunks = [seq_gather(chunk, n_seq) for chunk in ffn_chunks]
-    chunk_places, kept_rows = [], []
+    cot_chunks += [seq_gather(chunk, n_seq) for chunk in hold(cot_far[2:], far)]
+    near = jnp.concatenate([normed_ffn, seq_step(normed_ffn, n_seq, 0)], axis=0)
+    ffn_chunks = [seq_gather(normed_ffn, n_seq, near)]
+    for step in range(1, n_dp):
+        ffn_chunks.append(seq_gather(dp_swap(far, n_dp, step), n_seq))
+    in_moved = hold([in_moved[step] for step in range(n_dp)], near)
+    weight_in = lay_out(in_moved, dp_index)
+    weight_shared_in = weight_in[:, 2 * ff_part :]
+    weight_in = weight_in[:, : 2 * ff_part]
+    chunk_places, chunk_gates, kept_rows, kept_cots = [], [], [], []
     for step in range(n_dp):
         codes = relative(dp_block(slot_code, dp_index ^ step)).reshape(group)
-        placed = lax.optimization_barrier((codes[:, None] == slots).astype(BF16))
-        if step == 1:
-            placed = hold(placed, slot_cot, shared_act_grad)
+        gates_here = relative(dp_block(gate_of, dp_index ^ step)).reshape(group)
+        here = codes[:, None] == slots
+        placed = lax.optimization_barrier(here.astype(BF16))
+        slot_gate = jnp.sum(jnp.where(here, gates_here[:, None], 0.0), axis=0)[:, None]
         chunk_places.append(placed)
+        chunk_gates.append(slot_gate)
+        kept_cots.append((lead_dot(placed, cot_chunks[step]) * slot_gate).astype(BF16))
         kept_rows.append(lead_dot(placed, ffn_chunks[step]).astype(BF16))
-
-    in_moved = hold([in_moved[step] for step in range(n_dp)], ffn_chunks[0])
-    weight_in = in_order(in_moved, n_dp, dp_index).reshape(width, -1)
-    weight_shared_in = weight_in[:, 2 * ff_part :]
-    weight_in = weight_in[:, : 2 * ff_part]
     shared_in_back = weight_shared_in.T
     grad_shared_in = 0.0
-    kept_cots, kept_acts, kept_grads = [], [], []
+    kept_acts, kept_grads = [], []
     kept_shared, shared_acts, spreads = [], [], []
     for step in range(n_dp):
         ffn_rows = ffn_chunks[step]
         shared_in = matmul(ffn_rows, weight_shared_in)
         shared_gate, shared_up = shared_in[:, :units], shared_in[:, units:]
-        act_grad = dp_block(shared_act_grad, dp_index ^ step)
-        act_grad = relative(act_grad.reshape(n_seq, tokens, units)).reshape(group, units)
+        act_grad = tail_dot(cot_chunks[step], shared_down)
         shared_in_grad = jnp.concatenate(
             swiglu_back(shared_gate, shared_up, act_grad), axis=1
         ).astype(BF16)
@@ -436,13 +469,11 @@
     for step in range(n_dp):
         expert_in = matmul(kept_rows[step], weight_in)
         expert_gate, expert_up = expert_in[:, :ff_part], expert_in[:, ff_part:]
-        chunk_cot = dp_block(slot_cot, dp_index ^ step)
         expert_in_grad = jnp.concatenate(
-            swiglu_back(expert_gate, expert_up, tail_dot(chunk_cot, weight_back)), axis=1
+            swiglu_back(expert_gate, expert_up, tail_dot(kept_cots[step], weight_back)), axis=1
         ).astype(BF16)
         slot_grad = tail_dot(expert_in_grad, weight_in).astype(BF16)
         spreads[step] += (slot_grad,)
-        kept_cots.append(chunk_cot)
         kept_acts.append(swiglu(expert_gate, expert_up).astype(BF16))
         kept_grads.append(expert_in_grad)
 
@@ -467,43 +498,42 @@
     heads_grad = heads_grad.reshape(tokens, n_seq, heads * VD)
     heads_grad = lax.all_to_all(heads_grad, "seq", split_axis=1, concat_axis=0, tiled=True)
 
-    out_acts, shared_acts = hold((kept_acts, shared_acts), planes[-1][0])
-    kept_rows, kept_cots, kept_acts, kept_grads, ffn_chunks = hold(
-        (kept_rows, kept_cots, kept_acts, kept_grads, ffn_chunks), heads_grad
+    late_acts, late_cots, late_rows = hold((shared_acts, cot_chunks, ffn_chunks), planes[-1][0])
+    grad_shared_down = 0.0
+    for step in range(n_dp):
+        grad_shared_down = grad_shared_down + lead_dot(late_acts[step], late_cots[step])
+        grad_shared_in = grad_shared_in + lead_dot(late_rows[step], kept_shared[step])
+    out_acts, shared_acts = hold(
+        (kept_acts, shared_acts), planes[-1][0], grad_shared_down, grad_shared_in
+    )
+    out_halves = []
+    for step in range(n_dp):
+        expert_out = (matmul(out_acts[step], weight_back) * chunk_gates[step]).astype(BF16)
+        left_side = jnp.concatenate([chunk_places[step], shared_acts[step]], axis=1)
+        right_side = jnp.concatenate([expert_out, shared_down], axis=0)
+        out_halves.append(
+            [matmul(half_of(left_side, part), right_side).astype(BF16) for part in (0, 1)]
+        )
+    kept_rows, kept_cots, kept_acts, kept_grads = hold(
+        (kept_rows, kept_cots, kept_acts, kept_grads), heads_grad
     )
     grad_in = lead_dot(jnp.concatenate(kept_rows), jnp.concatenate(kept_grads)).astype(BF16)
     back_parts = grad_in.reshape(n_dp, expert_rows, 2 * ff_part)
     back_even = dp_exchange(back_parts, n_dp, dp_index, even_steps, ffn_grad)
-    expert_act = in_order(out_acts, n_dp, dp_index)
     grad_back = lead_dot(jnp.concatenate(kept_acts), jnp.concatenate(kept_cots))
     half = expert_down.shape[0]
     low_half, high_half = grad_back[:half], grad_back[half:]
     grad_kept = jnp.where(is_low, low_half, high_half)
     grad_sent = jnp.where(is_low, high_half, low_half).astype(BF16)
     grad_got = dp_swap(hold(grad_sent, ffn_grad), n_dp, 1)
-    shared_act = in_order(
-        [absolute(act.reshape(n_seq, tokens, units)) for act in shared_acts], n_dp, dp_index
-    ).reshape(n_dp, group, units)
-    expert_out = (contract(expert_act, weight_back, 2, 0) * slot_gate).astype(BF16)
-    out_part = jnp.einsum(
-        "gtk,gkd->gtd",
-        jnp.concatenate([all_placed, shared_act], axis=2),
-        jnp.concatenate(
-            [expert_out, jnp.broadcast_to(shared_down, (n_dp, units, width))], axis=1
-        ),
-        preferred_element_type=F32,
-    ).astype(BF16)
-    out_sum = lax.psum_scatter(
-        hold(out_part.reshape(n_all * tokens, width), ffn_grad),
-        BOTH,
-        scatter_dimension=0,
-        tiled=True,
-    )
-    output = (residual + out_sum.astype(F32)).astype(BF16)
-    shared_late = hold(shared_act, heads_grad).reshape(n_all * tokens, units)
-    grad_shared_down = lead_dot(shared_late, cot_all)
-    for step in range(n_dp):
-        grad_shared_in = grad_shared_in + lead_dot(ffn_chunks[step], kept_shared[step])
+    out_halves = hold(out_halves, ffn_grad)
+    output = residual
+    for step in list(range(1, n_dp)) + [0]:
+        plane_sum = seq_scatter(lambda part: out_halves[step][part], n_seq)[-1]
+        if step:
+            plane_sum = dp_swap(plane_sum.astype(BF16), n_dp, step).astype(F32)
+        output = output + plane_sum
+    output = output.astype(BF16)
 
     residual_group = seq_gather(hold(residual_low, heads_grad), n_seq)
     grad_shared_in = hold(grad_shared_in.astype(BF16), heads_grad)

time: 1540 us -> 1420 us (0.922); the launches traced: 1510 us -> 1410 us
  local copies, waits for them, and re-layouts: 505 us -> 262 us
  Pallas kernels: 9.61 us -> 217 us
  waiting for transfers between devices: 422 us -> 309 us
  other arithmetic: 128 us -> 189 us
  starting transfers between devices: 190 us -> 171 us
    dynamic_update_slice x16 -> x4, local copies, waits for them, and re-layouts: 243 us -> 4.33 us  [in_order(): lax.dynamic_update_index_in_dim(result, moved[step], dp_index ^ step, 0)]
    pallas_call x0 -> x1, Pallas kernels: none -> 208 us  [lay_out(): pl.pallas_call(lay_out_kernel, out_shape=jax.ShapeDtypeStruct((count * ro...]
    ppermute x26 -> x35, waiting for transfers between devices: 308 us -> 154 us  [dp_swap(): return lax.ppermute(values, 'dp', [(d, d ^ step) for d in range(n_dp)])]
    broadcast_in_dim x9 -> x1, local copies, waits for them, and re-layouts: 50.2 us -> 0.69 us  [absolute(): return jnp.take(values, block_of, axis=0, mode='clip')]
    ppermute x26 -> x44, waiting for transfers between devices: 71.4 us -> 114 us  [seq_step(): lax.ppermute(values, 'seq', [(s, s ^ orders[s & 1][step]) for s in range(...]
    ppermute x1, waiting for transfers between devices: 0.01 us -> 29.7 us  [body(): grad_out_weight = lax.ppermute(out_shard, BOTH, home)]
    convert_element_type x12 -> x20, other arithmetic: 20.9 us -> 45.5 us  [seq_scatter(): onward = (kept[half:].astype(F32) + sent[half:].astype(F32)).astype(BF16)]
    concatenate x14 -> x23, other arithmetic: 16.9 us -> 39.4 us  [seq_gather(): current = jnp.concatenate([current, seq_step(current, n_seq, step)], axis=0)]
  transfers between devices with their start and end apart: 76 -> 109, of which waited for: 31 -> 33; matrix products, arithmetic and copies ran while one was open for 51% -> 46% of each run, Pallas kernels for 1% -> 15%
where the time goes in v7:
time: 1420 us; the launch traced here: 1410 us
  waiting for transfers between devices  309 us (22%)
  local copies, waits for them, and re-layouts  262 us (18%)
  matrix products  247 us (17%)
  Pallas kernels  217 us (15%)
  other arithmetic  189 us (13%)
  starting transfers between devices  171 us (12%)
  between operations  17.8 us (1%)
    dot_general x72, matrix products, contract(): lax.dot_general(left_side, right_side, (((left_dim,), (right_dim,)), ((),...  223 us
    pallas_call x1, Pallas kernels, lay_out(): pl.pallas_call(lay_out_kernel, out_shape=jax.ShapeDtypeStruct((count * ro...  208 us
    ppermute x35, waiting for transfers between devices, dp_swap(): return lax.ppermute(values, 'dp', [(d, d ^ step) for d in range(n_dp)])  154 us
    ppermute x44, waiting for transfers between devices, seq_step(): lax.ppermute(values, 'seq', [(s, s ^ orders[s & 1][step]) for s in range(...  114 us
    unnamed x576, local copies, waits for them, and re-layouts  74.7 us
    ppermute x35, starting transfers between devices, dp_swap(): return lax.ppermute(values, 'dp', [(d, d ^ step) for d in range(n_dp)])  55.7 us
    convert_element_type x20, other arithmetic, seq_scatter(): onward = (kept[half:].astype(F32) + sent[half:].astype(F32)).astype(BF16)  45.5 us
    ppermute x44, starting transfers between devices, seq_step(): lax.ppermute(values, 'seq', [(s, s ^ orders[s & 1][step]) for s in range(...  43.7 us
  transfers between devices with their start and end apart: 109, of which 33 were waited for; matrix products, arithmetic and copies ran while one was open for 46% of the time, Pallas kernels for 15%

profile of v7, /device:TPU:25, one launch (start us, length us, event | category | flops | bytes accessed | tf_op | source)
XLA Modules:
  0.0 1413.2 jit_solution(18178231506670295772)
XLA Ops:
  26.9 8.6 constant_dynamic-slice_fusion.13
  46.6 31.7 %collective-permute-done.10 = bf16[128,2048]{1,0:T(8,128)(2,1)} collective-permute-done((bf16[128,2048]{1,0:T(8,128)(2,1)S(1)}, bf16[128,2048]{1,0:T(8,128)(2,1)}, u32[]{:S(2)}, u32[]{:S(2)}) %collective-permute-start.10) | collective-permute-done | bytes 524320 | tf_op jit(solution)/shard_map/ppermute | solution.py:145
  78.4 15.0 %copy.272 = bf16[512,2,2816]{0,2,1:T(8,128)(2,1)} copy(bf16[512,2,2816]{2,1,0:T(2,128)(2,1)} %param.29) | data formatting | bytes 11534336 | tf_op args[11]
  102.9 32.2 %collective-permute-done.4 = bf16[512,512]{1,0:T(8,128)(2,1)} collective-permute-done((bf16[512,512]{1,0:T(8,128)(2,1)}, bf16[512,512]{1,0:T(8,128)(2,1)}, u32[]{:S(2)}, u32[]{:S(2)}) %collective-permute-start.4) | collective-permute-done | bytes 524320 | tf_op jit(solution)/shard_map/ppermute | solution.py:145
  146.4 7.6 collective-permute-done.20
  180.6 11.1 collective-permute-start.12
  230.9 8.1 fusion.300
  243.3 13.1 collective-permute-done.13
  303.7 7.3 collective-permute-done.15
  318.5 7.0 pad_maximum_fusion.1
  325.5 8.3 gather_fusion.2
  333.8 6.3 fusion.297
  350.4 8.2 pad_maximum_fusion.2
  403.3 207.6 %lay_out.1 = bf16[2048,1584]{1,0:T(8,128)(2,1)} custom-call(s32[1]{0:T(128)} %bitcast.58.index_ref, bf16[512,1584]{1,0:T(8,128)(2,1)} %bitcast.378, bf16[512,1584]{1,0:T(8,128)(2,1)} %copy.283.refs_1_, bf16[512,1584]{1,0:T(8,128)(2,1)} %copy.284.refs_2_, bf16[512,1584]{1,0:T(8,128)(2,1)} %copy.285.refs_3_), custom_call_target="tpu_custom_call" | custom-call | tf_op jit(solution)/shard_map/lay_out/pallas_call | solution.py:229
  633.1 10.0 collective-permute-done.33
  646.4 8.0 collective-permute-done.37
  655.7 11.0 collective-permute-done.42
  681.9 7.3 collective-permute-done.34
  694.3 6.1 collective-permute-done.38
  1002.7 13.6 convolution_convert_fusion
  1037.6 6.7 fusion.25
  1082.0 14.4 %collective-permute-done.82.refs_2_ = bf16[512,1408]{1,0:T(8,128)(2,1)S(1)} collective-permute-done((bf16[512,1408]{1,0:T(8,128)(2,1)}, bf16[512,1408]{1,0:T(8,128)(2,1)S(1)}, u32[]{:S(2)}, u32[]{:S(2)}) %collective-permute-start.82) | collective-permute-done | bytes 1441824 | tf_op jit(solution)/shard_map/ppermute | solution.py:145
  1149.3 19.3 %collective-permute-done.85 = bf16[512,512]{1,0:T(8,128)(2,1)S(1)} collective-permute-done((bf16[512,512]{1,0:T(8,128)(2,1)S(1)}, bf16[512,512]{1,0:T(8,128)(2,1)S(1)}, u32[]{:S(2)}, u32[]{:S(2)}) %collective-permute-start.85) | collective-permute-done | bytes 524320 | tf_op jit(solution)/shard_map/ppermute | solution.py:145
  1182.5 10.6 collective-permute-start.90
  1216.4 8.8 collective-permute-done.74
  1261.2 8.0 collective-permute-done.101.refs_3_
  1272.2 7.0 copy.328
  1290.4 9.6 assemble.1
  1312.6 9.3 all-to-all-start.3
  1321.9 11.8 all-to-all-done.3
  1342.4 28.9 %collective-permute-done.68 = bf16[128,2048]{1,0:T(8,128)(2,1)S(1)} collective-permute-done((bf16[128,2048]{1,0:T(8,128)(2,1)}, bf16[128,2048]{1,0:T(8,128)(2,1)S(1)}, u32[]{:S(2)}, u32[]{:S(2)}) %collective-permute-start.68) | collective-permute-done | bytes 524320 | tf_op jit(solution)/shard_map/ppermute | solution.py:145
  1375.7 29.7 %collective-permute-done.99 = f32[64,2048]{1,0:T(8,128)S(1)} collective-permute-done((f32[64,2048]{1,0:T(8,128)S(1)}, f32[64,2048]{1,0:T(8,128)S(1)}, u32[]{:S(2)}, u32[]{:S(2)}) %collective-permute-start.99) | collective-permute-done | bytes 524320 | tf_op jit(solution)/shard_map/ppermute | solution.py:549
  (1108 shorter events, 803.2 us)
Async XLA Ops:
  23.3 180.4 %all-gather.3.cloned.1.call-start = ((), (), s32[]{:S(2)}) async-start(), calls=%async_computation.6 | async-start | bytes 3379200 | tf_op jit(solution)/shard_map/all_gather | solution.py:354
  41.0 60.2 %collective-permute-start.11 = (bf16[128,2048]{1,0:T(8,128)(2,1)S(1)}, bf16[128,2048]{1,0:T(8,128)(2,1)}, u32[]{:S(2)}, u32[]{:S(2)}) collective-permute-start(bf16[128,2048]{1,0:T(8,128)(2,1)S(1)} %copy-done.27), channel_id=1, source_target_pairs={{0,24},{8,16},{16,8},{24,0},{1,25},{9,17},{17,9},{25,1},{2,26},{10... | collective-permute-start | bytes 1572872 | tf_op jit(solution)/shard_map/ppermute | solution.py:145
  42.4 60.5 %collective-permute-start.9 = (bf16[128,2048]{1,0:T(8,128)(2,1)S(1)}, bf16[128,2048]{1,0:T(8,128)(2,1)}, u32[]{:S(2)}, u32[]{:S(2)}) collective-permute-start(bf16[128,2048]{1,0:T(8,128)(2,1)S(1)} %copy-done.27), channel_id=1, source_target_pairs={{0,8},{8,0},{16,24},{24,16},{1,9},{9,1},{17,25},{25,17},{2,10},{10... | collective-permute-start | bytes 1572872 | tf_op jit(solution)/shard_map/ppermute | solution.py:145
  44.6 58.3 %collective-permute-start.3 = (bf16[512,512]{1,0:T(8,128)(2,1)}, bf16[512,512]{1,0:T(8,128)(2,1)}, u32[]{:S(2)}, u32[]{:S(2)}) collective-permute-start(bf16[512,512]{1,0:T(8,128)(2,1)} %slice.715), channel_id=1, source_target_pairs={{0,8},{8,0},{16,24},{24,16},{1,9},{9,1},{17,25},{25,17},{2,10},{10... | collective-permute-start | bytes 1572872 | tf_op jit(solution)/shard_map/ppermute | solution.py:145
  46.6 88.5 %collective-permute-start.4 = (bf16[512,512]{1,0:T(8,128)(2,1)}, bf16[512,512]{1,0:T(8,128)(2,1)}, u32[]{:S(2)}, u32[]{:S(2)}) collective-permute-start(bf16[512,512]{1,0:T(8,128)(2,1)} %slice.715), channel_id=1, source_target_pairs={{0,16},{8,24},{16,0},{24,8},{1,17},{9,25},{17,1},{25,9},{2,18},{10... | collective-permute-start | bytes 1572872 | tf_op jit(solution)/shard_map/ppermute | solution.py:145
  180.6 80.6 %collective-permute-start.12 = (bf16[512,1584]{0,1:T(8,128)(2,1)}, bf16[512,1584]{0,1:T(8,128)(2,1)}, u32[]{:S(2)}, u32[]{:S(2)}) collective-permute-start(bf16[512,1584]{0,1:T(8,128)(2,1)} %dynamic-slice_bitcast_fusion.2), channel_id=1, source_target_pairs={{0,16},{8,24},{16,0},{24,8},{1,17},{9,25},{17,1},{25,9},{2,18},{10... | collective-permute-start | bytes 4866056 | tf_op jit(solution)/shard_map/ppermute | solution.py:145
  191.7 64.7 %collective-permute-start.13 = (bf16[352,2048]{1,0:T(8,128)(2,1)}, bf16[352,2048]{1,0:T(8,128)(2,1)}, u32[]{:S(2)}, u32[]{:S(2)}) collective-permute-start(bf16[352,2048]{1,0:T(8,128)(2,1)} %get-tuple-element.104), channel_id=1, source_target_pairs={{0,8},{8,0},{16,24},{24,16},{1,9},{9,1},{17,25},{25,17},{2,10},{10... | collective-permute-start | bytes 4325384 | tf_op jit(solution)/shard_map/ppermute | solution.py:145
  202.5 116.0 %collective-permute-start.22 = (bf16[1024,2048]{1,0:T(8,128)(2,1)}, bf16[1024,2048]{1,0:T(8,128)(2,1)}, u32[]{:S(2)}, u32[]{:S(2)}) collective-permute-start(bf16[1024,2048]{1,0:T(8,128)(2,1)} %pad_maximum_fusion.5), channel_id=1, source_target_pairs={{0,1},{1,0},{2,3},{3,2},{4,5},{5,4},{6,7},{7,6},{8,9},{9,8},{10,11... | collective-permute-start | bytes 12582920 | tf_op jit(solution)/shard_map/ppermute | solution.py:111
  227.9 58.9 %collective-permute-start.14 = (bf16[128,2048]{1,0:T(8,128)(2,1)S(1)}, bf16[128,2048]{1,0:T(8,128)(2,1)S(1)}, u32[]{:S(2)}, u32[]{:S(2)}) collective-permute-start(bf16[128,2048]{1,0:T(8,128)(2,1)S(1)} %copy-done.28), channel_id=1, source_target_pairs={{0,2},{1,5},{2,0},{3,7},{4,6},{5,1},{6,4},{7,3},{8,10},{9,13},{10,... | collective-permute-start | bytes 1572872 | tf_op jit(solution)/shard_map/ppermute | solution.py:107
  272.6 96.3 %collective-permute-start.26 = (bf16[512,1584]{0,1:T(8,128)(2,1)}, bf16[512,1584]{0,1:T(8,128)(2,1)}, u32[]{:S(2)}, u32[]{:S(2)}) collective-permute-start(bf16[512,1584]{0,1:T(8,128)(2,1)} %get-tuple-element.273), channel_id=1, source_target_pairs={{0,8},{8,0},{16,24},{24,16},{1,9},{9,1},{17,25},{25,17},{2,10},{10... | collective-permute-start | bytes 4866056 | tf_op jit(solution)/shard_map/ppermute | solution.py:145
  272.6 96.3 %collective-permute-start.27 = (bf16[512,1584]{0,1:T(8,128)(2,1)}, bf16[512,1584]{0,1:T(8,128)(2,1)}, u32[]{:S(2)}, u32[]{:S(2)}) collective-permute-start(bf16[512,1584]{0,1:T(8,128)(2,1)} %get-tuple-element.272), channel_id=1, source_target_pairs={{0,24},{8,16},{16,8},{24,0},{1,25},{9,17},{17,9},{25,1},{2,26},{10... | collective-permute-start | bytes 4866056 | tf_op jit(solution)/shard_map/ppermute | solution.py:145
  368.9 247.8 %collective-permute-start.28 = (bf16[128,2048]{1,0:T(8,128)(2,1)S(1)}, bf16[128,2048]{1,0:T(8,128)(2,1)S(1)}, u32[]{:S(2)}, u32[]{:S(2)}) collective-permute-start(bf16[128,2048]{1,0:T(8,128)(2,1)S(1)} %multiply_convert_fusion.26), channel_id=1, source_target_pairs={{0,8},{8,0},{16,24},{24,16},{1,9},{9,1},{17,25},{25,17},{2,10},{10... | collective-permute-start | bytes 1572872 | tf_op jit(solution)/shard_map/ppermute | solution.py:145
  369.8 248.0 %collective-permute-start.32 = (bf16[128,2048]{1,0:T(8,128)(2,1)S(1)}, bf16[128,2048]{1,0:T(8,128)(2,1)S(1)}, u32[]{:S(2)}, u32[]{:S(2)}) collective-permute-start(bf16[128,2048]{1,0:T(8,128)(2,1)S(1)} %multiply_convert_fusion.26), channel_id=1, source_target_pairs={{0,16},{8,24},{16,0},{24,8},{1,17},{9,25},{17,1},{25,9},{2,18},{10... | collective-permute-start | bytes 1572872 | tf_op jit(solution)/shard_map/ppermute | solution.py:145
  370.0 248.8 %collective-permute-start.41 = (bf16[128,2048]{1,0:T(8,128)(2,1)}, bf16[128,2048]{1,0:T(8,128)(2,1)S(1)}, u32[]{:S(2)}, u32[]{:S(2)}) collective-permute-start(bf16[128,2048]{1,0:T(8,128)(2,1)} %collective-permute-done.10), channel_id=1, source_target_pairs={{0,2},{1,5},{2,0},{3,7},{4,6},{5,1},{6,4},{7,3},{8,10},{9,13},{10,... | collective-permute-start | bytes 1572872 | tf_op jit(solution)/shard_map/ppermute | solution.py:107
  372.0 253.4 %collective-permute-start.36 = (bf16[128,2048]{1,0:T(8,128)(2,1)S(1)}, bf16[128,2048]{1,0:T(8,128)(2,1)S(1)}, u32[]{:S(2)}, u32[]{:S(2)}) collective-permute-start(bf16[128,2048]{1,0:T(8,128)(2,1)S(1)} %multiply_convert_fusion.26), channel_id=1, source_target_pairs={{0,24},{8,16},{16,8},{24,0},{1,25},{9,17},{17,9},{25,1},{2,26},{10... | collective-permute-start | bytes 1572872 | tf_op jit(solution)/shard_map/ppermute | solution.py:145
  390.1 223.1 %collective-permute-start.46 = (bf16[128,2048]{1,0:T(8,128)(2,1)}, bf16[128,2048]{1,0:T(8,128)(2,1)}, u32[]{:S(2)}, u32[]{:S(2)}) collective-permute-start(bf16[128,2048]{1,0:T(8,128)(2,1)} %collective-permute-done.11), channel_id=1, source_target_pairs={{0,2},{1,5},{2,0},{3,7},{4,6},{5,1},{6,4},{7,3},{8,10},{9,13},{10,... | collective-permute-start | bytes 1572872 | tf_op jit(solution)/shard_map/ppermute | solution.py:107
  705.7 61.4 %collective-permute-start.39 = (bf16[512,2048]{1,0:T(8,128)(2,1)}, bf16[512,2048]{1,0:T(8,128)(2,1)}, u32[]{:S(2)}, u32[]{:S(2)}) collective-permute-start(bf16[512,2048]{1,0:T(8,128)(2,1)} %pad_maximum_fusion.24), channel_id=1, source_target_pairs={{0,1},{1,0},{2,3},{3,2},{4,5},{5,4},{6,7},{7,6},{8,9},{9,8},{10,11... | collective-permute-start | bytes 6291464 | tf_op jit(solution)/shard_map/ppermute | solution.py:111
  881.7 67.2 %collective-permute-start.53 = (bf16[128,2048]{1,0:T(8,128)(2,1)}, bf16[128,2048]{1,0:T(8,128)(2,1)}, u32[]{:S(2)}, u32[]{:S(2)}) collective-permute-start(bf16[128,2048]{1,0:T(8,128)(2,1)} %convert_add_fusion.5), channel_id=1, source_target_pairs={{0,8},{8,0},{16,24},{24,16},{1,9},{9,1},{17,25},{25,17},{2,10},{10... | collective-permute-start | bytes 1572872 | tf_op jit(solution)/shard_map/ppermute | solution.py:145
  881.7 67.2 %collective-permute-start.55 = (bf16[128,2048]{1,0:T(8,128)(2,1)}, bf16[128,2048]{1,0:T(8,128)(2,1)}, u32[]{:S(2)}, u32[]{:S(2)}) collective-permute-start(bf16[128,2048]{1,0:T(8,128)(2,1)} %add_convert_fusion.5), channel_id=1, source_target_pairs={{0,16},{8,24},{16,0},{24,8},{1,17},{9,25},{17,1},{25,9},{2,18},{10... | collective-permute-start | bytes 1572872 | tf_op jit(solution)/shard_map/ppermute | solution.py:145
  891.1 57.8 %collective-permute-start.58 = (bf16[128,2048]{1,0:T(8,128)(2,1)}, bf16[128,2048]{1,0:T(8,128)(2,1)}, u32[]{:S(2)}, u32[]{:S(2)}) collective-permute-start(bf16[128,2048]{1,0:T(8,128)(2,1)} %fusion.123), channel_id=1, source_target_pairs={{0,24},{8,16},{16,8},{24,0},{1,25},{9,17},{17,9},{25,1},{2,26},{10... | collective-permute-start | bytes 1572872 | tf_op jit(solution)/shard_map/ppermute | solution.py:145
  974.3 153.9 %collective-permute-start.61 = (bf16[512,2048]{1,0:T(8,128)(2,1)}, bf16[512,2048]{1,0:T(8,128)(2,1)}, u32[]{:S(2)}, u32[]{:S(2)}) collective-permute-start(bf16[512,2048]{1,0:T(8,128)(2,1)} %convolution_convert_fusion.7), channel_id=1, source_target_pairs={{0,1},{1,0},{2,3},{3,2},{4,5},{5,4},{6,7},{7,6},{8,9},{9,8},{10,11... | collective-permute-start | bytes 6291464 | tf_op jit(solution)/shard_map/ppermute | solution.py:111
  974.4 157.7 %collective-permute-start.65 = (bf16[512,2048]{1,0:T(8,128)(2,1)}, bf16[512,2048]{1,0:T(8,128)(2,1)}, u32[]{:S(2)}, u32[]{:S(2)}) collective-permute-start(bf16[512,2048]{1,0:T(8,128)(2,1)} %convolution_convert_fusion.5), channel_id=1, source_target_pairs={{0,1},{1,0},{2,3},{3,2},{4,5},{5,4},{6,7},{7,6},{8,9},{9,8},{10,11... | collective-permute-start | bytes 6291464 | tf_op jit(solution)/shard_map/ppermute | solution.py:111
  1002.7 73.7 %collective-permute-start.83 = (bf16[352,2048]{1,0:T(8,128)(2,1)}, bf16[352,2048]{1,0:T(8,128)(2,1)}, u32[]{:S(2)}, u32[]{:S(2)}) collective-permute-start(bf16[352,2048]{1,0:T(8,128)(2,1)} %select_convert_fusion), channel_id=1, source_target_pairs={{0,8},{8,0},{16,24},{24,16},{1,9},{9,1},{17,25},{25,17},{2,10},{10... | collective-permute-start | bytes 4325384 | tf_op jit(solution)/shard_map/ppermute | solution.py:145
  1020.0 76.4 %collective-permute-start.82 = (bf16[512,1408]{1,0:T(8,128)(2,1)}, bf16[512,1408]{1,0:T(8,128)(2,1)S(1)}, u32[]{:S(2)}, u32[]{:S(2)}) collective-permute-start(bf16[512,1408]{1,0:T(8,128)(2,1)} %dynamic-slice_bitcast_fusion.6), channel_id=1, source_target_pairs={{0,16},{8,24},{16,0},{24,8},{1,17},{9,25},{17,1},{25,9},{2,18},{10... | collective-permute-start | bytes 4325384 | tf_op jit(solution)/shard_map/ppermute | solution.py:145
  1028.4 142.7 %all-to-all-start.4 = ((bf16[32,64,176]{2,1,0:T(8,128)(2,1)}), bf16[32,64,176]{2,1,0:T(8,128)(2,1)}, u32[]{:S(2)}, u32[]{:S(2)}) async-start(bf16[32,64,176]{2,1,0:T(8,128)(2,1)} %bitcast.387), calls=%async_computation.4 | async-start | bytes 2097152 | tf_op jit(solution)/shard_map/all_to_all | solution.py:540
  1076.3 61.8 %collective-permute-start.69 = (bf16[512,2048]{1,0:T(8,128)(2,1)}, bf16[512,2048]{1,0:T(8,128)(2,1)}, u32[]{:S(2)}, u32[]{:S(2)}) collective-permute-start(bf16[512,2048]{1,0:T(8,128)(2,1)} %convolution_convert_fusion.3), channel_id=1, source_target_pairs={{0,1},{1,0},{2,3},{3,2},{4,5},{5,4},{6,7},{7,6},{8,9},{9,8},{10,11... | collective-permute-start | bytes 6291464 | tf_op jit(solution)/shard_map/ppermute | solution.py:111
  1124.9 69.1 %collective-permute-start.76 = (bf16[512,2048]{1,0:T(8,128)(2,1)}, bf16[512,2048]{1,0:T(8,128)(2,1)}, u32[]{:S(2)}, u32[]{:S(2)}) collective-permute-start(bf16[512,2048]{1,0:T(8,128)(2,1)} %get-tuple-element.378), channel_id=1, source_target_pairs={{0,1},{1,0},{2,3},{3,2},{4,5},{5,4},{6,7},{7,6},{8,9},{9,8},{10,11... | collective-permute-start | bytes 6291464 | tf_op jit(solution)/shard_map/ppermute | solution.py:111
  1199.1 100.9 %collective-permute-start.95 = (bf16[512,2048]{1,0:T(8,128)(2,1)}, bf16[512,2048]{1,0:T(8,128)(2,1)}, u32[]{:S(2)}, u32[]{:S(2)}) collective-permute-start(bf16[512,2048]{1,0:T(8,128)(2,1)} %pad_maximum_fusion.27), channel_id=1, source_target_pairs={{0,1},{1,0},{2,3},{3,2},{4,5},{5,4},{6,7},{7,6},{8,9},{9,8},{10,11... | collective-permute-start | bytes 6291464 | tf_op jit(solution)/shard_map/ppermute | solution.py:111
  1207.3 61.9 %collective-permute-start.101 = (bf16[512,1408]{1,0:T(8,128)(2,1)}, bf16[512,1408]{1,0:T(8,128)(2,1)}, u32[]{:S(2)}, u32[]{:S(2)}) collective-permute-start(bf16[512,1408]{1,0:T(8,128)(2,1)} %get-tuple-element.282), channel_id=1, source_target_pairs={{0,24},{8,16},{16,8},{24,0},{1,25},{9,17},{17,9},{25,1},{2,26},{10... | collective-permute-start | bytes 4325384 | tf_op jit(solution)/shard_map/ppermute | solution.py:145
  1251.1 91.2 %collective-permute-start.75 = (bf16[128,2048]{1,0:T(8,128)(2,1)}, bf16[128,2048]{1,0:T(8,128)(2,1)}, u32[]{:S(2)}, u32[]{:S(2)}) collective-permute-start(bf16[128,2048]{1,0:T(8,128)(2,1)} %fusion.105), channel_id=1, source_target_pairs={{0,2},{1,5},{2,0},{3,7},{4,6},{5,1},{6,4},{7,3},{8,10},{9,13},{10,... | collective-permute-start | bytes 1572872 | tf_op jit(solution)/shard_map/ppermute | solution.py:107
  1260.6 81.8 %collective-permute-start.64 = (bf16[128,2048]{1,0:T(8,128)(2,1)}, bf16[128,2048]{1,0:T(8,128)(2,1)}, u32[]{:S(2)}, u32[]{:S(2)}) collective-permute-start(bf16[128,2048]{1,0:T(8,128)(2,1)} %fusion.117), channel_id=1, source_target_pairs={{0,8},{8,0},{16,24},{24,16},{1,9},{9,1},{17,25},{25,17},{2,10},{10... | collective-permute-start | bytes 1572872 | tf_op jit(solution)/shard_map/ppermute | solution.py:145
  1338.7 66.7 %collective-permute-start.99 = (f32[64,2048]{1,0:T(8,128)S(1)}, f32[64,2048]{1,0:T(8,128)S(1)}, u32[]{:S(2)}, u32[]{:S(2)}) collective-permute-start(f32[64,2048]{1,0:T(8,128)S(1)} %fusion.185), channel_id=1, source_target_pairs={{0,0},{1,4},{2,8},{3,12},{4,16},{5,20},{6,24},{7,28},{8,1},{9,5},{... | collective-permute-start | bytes 1572872 | tf_op jit(solution)/shard_map/ppermute | solution.py:549
  (351 other events, 5179.6 us)
Sparse Core Ops, SparseCore 0:
  27.0 103.5 all-gather.2
